TPU v7x, 32 devices: a whole 2x2x4 slice. The times are simulated.
32 devices in a mesh: seq: 4 (over z), exp: 2 (over core), hid: 4 (over y, x).
Axes of the slice: x: 2, y: 2, z: 4, core: 2. Of those that a mesh axis runs over, the one named last changes fastest.
Arguments:
- tokens: bfloat16 [512, 6144], P('seq'), may hold values from -6 to 6
- out_grad: bfloat16 [512, 6144], P('seq'), may hold values from -3 to 3
- expert_ids: int32 [512, 2], P('seq'), may hold values from 0 to 7, as said below
- gate_probs: float32 [512, 2], P('seq'), may hold values from 0.1 to 1
- w_gate: bfloat16 [2, 6144, 16384], P('exp', None, ('seq', 'hid')), may hold values from -0.078125 to 0.078125
- w_up: bfloat16 [2, 6144, 16384], P('exp', None, ('seq', 'hid')), may hold values from -0.078125 to 0.078125
- w_down: bfloat16 [2, 16384, 6144], P('exp', ('seq', 'hid')), may hold values from -0.046875 to 0.046875
Outputs:
- d_w_gate: bfloat16 [2, 6144, 16384], P('exp', None, ('seq', 'hid'))
- d_w_up: bfloat16 [2, 6144, 16384], P('exp', None, ('seq', 'hid'))
- d_w_down: bfloat16 [2, 16384, 6144], P('exp', ('seq', 'hid'))
- d_tokens: float32 [512, 6144], P('seq', 'hid')
- d_gates: float32 [512, 2], P('seq')
Inputs may be any that keep to these rules, and one draw needn't show every extreme that they name: `expert_ids`: in each block of 128 rows (the tokens of one index of seq) the two ids of a row differ and no expert is named more than 40 times; each expert below 2 is named 40 // 2 to 40 times in a block, exactly 40 times in the first block.
All inputs are finite; a program needn't handle non-finite values.
Results may differ from a plain program's by a relative error of at most 0.015.
Values may be sent and summed in bfloat16 or wider, within the bound.
No kernel may reach another device: no remote copies, remote signals or barrier semaphores. Data moves between devices by JAX's collectives and lax.ppermute only.
A program may use at most 192 MiB of HBM per device.

v0:
```python
import jax
import jax.numpy as jnp
from jax import lax
from jax.sharding import PartitionSpec as P


def on_device(tokens, out_grad, expert_ids, gate_probs, w_gate, w_up, w_down):
    expert = lax.axis_index("exp")
    tok_rows = tokens.shape[0]
    model_width = tokens.shape[1]
    capacity = 5 * tok_rows // 16
    seq_count = lax.axis_size("seq")
    hid_count = lax.axis_size("hid")
    piece_width = model_width // hid_count
    hidden_local = w_gate.shape[2]
    chosen = (expert_ids == expert).astype(jnp.int32)
    slot_index = (jnp.cumsum(chosen.reshape(-1)) - 1).reshape(tok_rows, 2)
    columns = jnp.arange(capacity, dtype=jnp.int32)
    pick_table = (
        (chosen[:, :, None] == 1) & (slot_index[:, :, None] == columns[None, None, :])
    ).astype(jnp.float32)
    select_rows = jnp.sum(pick_table, axis=1)
    select_half = select_rows.astype(jnp.bfloat16)
    contract_rows = (((0,), (0,)), ((), ()))
    token_slots = lax.dot_general(
        select_half, tokens, contract_rows, preferred_element_type=jnp.float32
    ).astype(jnp.bfloat16)
    grad_slots = lax.dot_general(
        select_half, out_grad, contract_rows, preferred_element_type=jnp.float32
    ).astype(jnp.bfloat16)
    weight_slots = jnp.sum(pick_table * gate_probs[:, :, None], axis=(0, 1))
    rows_e, grads_e, weight_e = (
        lax.all_gather(token_slots, "seq", axis=0, tiled=True),
        lax.all_gather(grad_slots, "seq", axis=0, tiled=True),
        lax.all_gather(weight_slots.astype(jnp.bfloat16), "seq", axis=0, tiled=True).astype(
            weight_slots.dtype
        ),
    )
    gate_mat = w_gate[0]
    up_mat = w_up[0]
    down_mat = w_down[0]
    gate_pre = jnp.dot(rows_e, gate_mat, preferred_element_type=jnp.float32)
    up_pre = jnp.dot(rows_e, up_mat, preferred_element_type=jnp.float32)
    sig_gate = jax.nn.sigmoid(gate_pre)
    activated = gate_pre * sig_gate
    hidden = (activated * up_pre).astype(jnp.bfloat16)
    back_hidden = lax.dot_general(
        grads_e, down_mat, (((1,), (1,)), ((), ())), preferred_element_type=jnp.float32
    )
    slot_part = jnp.sum(hidden.astype(jnp.float32) * back_hidden, axis=1)
    weighted = (weight_e[:, None] * hidden.astype(jnp.float32)).astype(jnp.bfloat16)
    grad_down = lax.dot_general(
        weighted, grads_e, contract_rows, preferred_element_type=jnp.float32
    ).astype(jnp.bfloat16)
    scaled_back = weight_e[:, None] * back_hidden
    d_gate = (scaled_back * up_pre * (sig_gate * (1.0 + gate_pre * (1.0 - sig_gate)))).astype(
        jnp.bfloat16
    )
    d_up = (scaled_back * activated).astype(jnp.bfloat16)
    grad_gate = lax.dot_general(
        rows_e, d_gate, contract_rows, preferred_element_type=jnp.float32
    ).astype(jnp.bfloat16)
    grad_up = lax.dot_general(
        rows_e, d_up, contract_rows, preferred_element_type=jnp.float32
    ).astype(jnp.bfloat16)
    gate_blocks = d_gate.reshape(seq_count, capacity, hidden_local)
    up_blocks = d_up.reshape(seq_count, capacity, hidden_local)
    partials = jnp.einsum(
        "sqf,hcf->shqc",
        gate_blocks,
        gate_mat.reshape(hid_count, piece_width, hidden_local),
        preferred_element_type=jnp.float32,
    )
    partials = partials + jnp.einsum(
        "sqf,hcf->shqc",
        up_blocks,
        up_mat.reshape(hid_count, piece_width, hidden_local),
        preferred_element_type=jnp.float32,
    )
    slot_terms = jnp.broadcast_to(
        slot_part.reshape(seq_count, 1, capacity), (seq_count, hid_count, capacity)
    )
    flat_parts = partials.reshape(seq_count * hid_count, capacity, piece_width)
    flat_slots = slot_terms.reshape(seq_count * hid_count, capacity)
    partials, slot_terms = (
        lax.psum_scatter(flat_parts, ("seq", "hid"), scatter_dimension=0, tiled=True),
        lax.psum_scatter(flat_slots, ("seq", "hid"), scatter_dimension=0, tiled=True),
    )
    own_rows = partials.reshape(capacity, piece_width)
    slot_grad = slot_terms.reshape(capacity)
    token_part = jnp.dot(
        select_rows, own_rows, precision=lax.Precision.HIGHEST, preferred_element_type=jnp.float32
    )
    gate_part = jnp.sum(pick_table * slot_grad[None, None, :], axis=2)
    token_sum, gate_sum = (
        lax.psum(token_part.astype(jnp.bfloat16), "exp").astype(jnp.float32),
        lax.psum(gate_part.astype(jnp.bfloat16), "exp").astype(jnp.float32),
    )
    return (grad_gate[None], grad_up[None], grad_down[None], token_sum, gate_sum)


def solution(mesh):
    return jax.shard_map(
        on_device,
        mesh=mesh,
        in_specs=(
            P("seq", None),
            P("seq", None),
            P("seq", None),
            P("seq", None),
            P("exp", None, ("seq", "hid")),
            P("exp", None, ("seq", "hid")),
            P("exp", ("seq", "hid"), None),
        ),
        out_specs=(
            P("exp", None, ("seq", "hid")),
            P("exp", None, ("seq", "hid")),
            P("exp", ("seq", "hid"), None),
            P("seq", "hid"),
            P("seq", None),
        ),
        check_vma=False,
    )
```

profile of v0, /device:TPU:0, one launch (start us, length us, event | category | flops | bytes accessed | tf_op | source)
XLA Modules:
  0.0 344.5 jit_solution(5438517381305366996)
XLA Ops:
  7.3 0.8 broadcast_compare_fusion
  8.0 0.1 copy.22
  8.2 0.1 reshape.70
  8.3 0.3 reduce-window.9
  8.6 0.1 reshape.71
  8.9 0.1 slice_reduce_fusion
  9.3 1.1 convolution_convert_fusion.1
  10.5 2.5 convolution_convert_fusion
  13.1 0.6 dynamic-slice.1
  13.7 0.6 dynamic-slice
  14.9 41.9 %all-gather.3.cloned.1.call-done = bf16[160,6144]{1,0:T(8,128)(2,1)} async-done(((bf16[40,6144]{1,0:T(8,128)(2,1)}), bf16[160,6144]{1,0:T(8,128)(2,1)}) %all-gather.3.cloned.1.call-update) | async-done | bytes 1966096 | tf_op jit(solution)/shard_map/all_gather | solution.py:33
  56.8 7.5 %fusion = f32[160,1024]{1,0:T(8,128)S(1)} fusion(bf16[160,6144]{1,0:T(8,128)(2,1)} %all-gather.3.cloned.1.call-done, bf16[1,6144,1024]{2,1,0:T(8,128)(2,1)} %param.11), kind=kOutput, calls=%fused_computation | convolution fusion | flops 2013265920 | bytes 15204352 | tf_op jit(solution)/shard_map/dot_general | solution.py:42
  64.4 7.1 %fusion.2 = f32[160,1024]{1,0:T(8,128)S(1)} fusion(bf16[160,6144]{1,0:T(8,128)(2,1)S(1)} %copy-done.2, bf16[1,6144,1024]{2,1,0:T(8,128)(2,1)} %param.12), kind=kOutput, calls=%fused_computation.2 | convolution fusion | flops 2013265920 | bytes 15204352 | tf_op jit(solution)/shard_map/dot_general | solution.py:43
  71.5 29.9 %all-gather.5.cloned.1.call-done = bf16[160,6144]{1,0:T(8,128)(2,1)} async-done(((bf16[40,6144]{1,0:T(8,128)(2,1)}), bf16[160,6144]{1,0:T(8,128)(2,1)}) %all-gather.5.cloned.1.call-update) | async-done | bytes 1966096 | tf_op jit(solution)/shard_map/all_gather | solution.py:34
  101.4 10.4 %fusion.7 = (f32[160]{0:T(256)S(1)}, bf16[160,1024]{1,0:T(8,128)(2,1)}, f32[160,1024]{1,0:T(8,128)}) fusion(f32[160,1024]{1,0:T(8,128)S(1)} %fusion.2, f32[160,1024]{1,0:T(8,128)S(1)} %fusion, bf16[160,6144]{1,0:T(8,128)(2,1)} %all-gather.5.cloned.1.call-done, bf16[1,1024,6144]{2,1,0:T(8,128)(2,1)} %param.13), kind=kOutput, calls=%fused_computation.16 | convolution fusion | flops 2014740352 | bytes 16843392 | tf_op jit(solution)/shard_map/dot_general | solution.py:47
  111.9 40.0 %all-reduce.1 = f32[16,40]{1,0:T(8,128)S(1)} all-reduce(f32[16,40]{1,0:T(8,128)S(1)} %bitcast.64), channel_id=3, replica_groups=mesh['seq'=4,'exp'=2,'hid'=4] {'seq','hid'}, use_global_device_ids=true, to_apply=%region_7.8.clone | all-reduce | flops 640 | bytes 5120
  151.9 0.7 dynamic-slice_bitcast_fusion
  152.6 0.1 select_reduce_fusion
  152.7 0.2 dynamic-update-slice
  153.0 8.5 %all-reduce = bf16[160]{0:T(256)(128)(2,1)S(1)} all-reduce(bf16[160]{0:T(256)(128)(2,1)S(1)} %dynamic-update-slice), channel_id=1, replica_groups=mesh['seq'=4,'exp'=2,'hid'=4] {'seq'}, use_global_device_ids=true, to_apply=%add | all-reduce | flops 160 | bytes 640
  161.5 1.4 multiply_convert_fusion.1
  163.0 9.0 %fusion.15 = f32[4,40,4,1536]{3,1,2,0:T(8,128)S(1)} fusion(bf16[4,40,1024,1]{2,1,3,0:T(8,128)(2,1)S(1)} %bitcast.62, bf16[4,1536,1024,1]{2,1,0,3:T(8,128)(2,1)} %bitcast.59), kind=kOutput, calls=%fused_computation.36 | convolution fusion | flops 2013265920 | bytes 16842752 | tf_op jit(solution)/shard_map/sqf,hcf->shqc/dot_general | solution.py:68
  172.0 10.8 %convolution_add_fusion = f32[4,40,4,1536]{3,1,2,0:T(8,128)} fusion(f32[4,40,4,1536]{3,1,2,0:T(8,128)S(1)} %fusion.15, bf16[4,40,1024,1]{2,1,3,0:T(8,128)(2,1)S(1)} %bitcast.63, bf16[4,1536,1024,1]{2,1,0,3:T(8,128)(2,1)} %bitcast.60), kind=kOutput, calls=%fused_computation.11 | convolution fusion | flops 2014248960 | bytes 20774912 | tf_op jit(solution)/shard_map/sqf,hcf->shqc/dot_general | solution.py:74
  182.9 2.7 psum.15
  185.6 0.6 convert_element_type.76
  186.2 6.6 %convert_bitcast_fusion.1 = bf16[1,6144,1024]{2,1,0:T(8,128)(2,1)} fusion(bf16[160,6144]{1,0:T(8,128)(2,1)S(1)} %copy-done.2, bf16[160,1024]{1,0:T(8,128)(2,1)S(1)} %copy-done.8), kind=kOutput, calls=%fused_computation.7 | convolution fusion | flops 2019557376 | bytes 14876672 | tf_op jit(solution)/shard_map/dot_general | solution.py:63
  192.8 6.6 %convert_bitcast_fusion.2 = bf16[1,6144,1024]{2,1,0:T(8,128)(2,1)} fusion(bf16[160,6144]{1,0:T(8,128)(2,1)S(1)} %copy-done.2, bf16[160,1024]{1,0:T(8,128)(2,1)S(1)} %copy-done.6), kind=kOutput, calls=%fused_computation.8 | convolution fusion | flops 2019557376 | bytes 14876672 | tf_op jit(solution)/shard_map/dot_general | solution.py:60
  199.4 116.0 %reduce-scatter.2.cloned.1.call-done = f32[1,40,1536]{2,1,0:T(8,128)} async-done(((f32[16,40,1536]{2,1,0:T(8,128)}), f32[1,40,1536]{2,1,0:T(8,128)}) %reduce-scatter.2.cloned.1.call-update) | async-done | bytes 245776 | tf_op jit(solution)/shard_map/reduce_scatter | solution.py:86
  315.5 2.5 convolution_convert_fusion.2
  318.0 10.1 %convert_bitcast_fusion = bf16[1,1024,6144]{2,1,0:T(8,128)(2,1)} fusion(bf16[160,6144]{1,0:T(8,128)(2,1)} %all-gather.5.cloned.1.call-done, bf16[160,1024]{1,0:T(8,128)(2,1)} %get-tuple-element.8, f32[160]{0:T(256)S(1)} %convert_element_type.63), kind=kOutput, calls=%fused_computation.6 | convolution fusion | flops 2020048896 | bytes 14877312 | tf_op jit(solution)/shard_map/dot_general | solution.py:52
  328.1 7.9 %all-reduce.4.cloned.1.call-done = bf16[128,1536]{1,0:T(8,128)(2,1)} async-done(((bf16[128,1536]{1,0:T(8,128)(2,1)}), bf16[128,1536]{1,0:T(8,128)(2,1)}) %all-reduce.4.cloned.1.call-update) | async-done | bytes 393232 | tf_op jit(solution)/shard_map/psum | solution.py:96
  336.1 2.0 convert_element_type.74
  (43 shorter events, 0.7 us)
Async XLA Ops:
  7.2 2.1 copy-start
  7.2 5.9 %copy-start.11 = (u32[32]{0:T(128)S(1)}, u32[32]{0:T(128)}, u32[]{:S(2)}) copy-start(u32[32]{0:T(128)} %constant.32) | copy-start | bytes 388
  7.2 6.5 %copy-start.10 = (u32[32]{0:T(128)S(1)}, u32[32]{0:T(128)}, u32[]{:S(2)}) copy-start(u32[32]{0:T(128)} %constant.26) | copy-start | bytes 388
  7.2 49.6 %all-gather.3.cloned.1.call-start = ((), (), s32[]{:S(2)}) async-start(), calls=%async_computation.1 | async-start | bytes 2457600 | tf_op jit(solution)/shard_map/all_gather | solution.py:33
  9.3 5.7 %copy-start.3 = (f32[128,40]{0,1:T(8,128)}, f32[128,40]{0,1:T(8,128)S(1)}, u32[]{:S(2)}) copy-start(f32[128,40]{0,1:T(8,128)S(1)} %convert_reduce_fusion) | copy-start | bytes 61444
  10.4 91.0 %all-gather.5.cloned.1.call-start = ((), (), s32[]{:S(2)}) async-start(), calls=%async_computation.2 | async-start | bytes 2457600 | tf_op jit(solution)/shard_map/all_gather | solution.py:34
  13.0 302.4 %reduce-scatter.2.cloned.1.call-start = ((), (), s32[]{:S(2)}) async-start(), calls=%async_computation.3 | async-start | bytes 4177920 | tf_op jit(solution)/shard_map/reduce_scatter | solution.py:86
  56.8 7.5 %copy-start.2 = (bf16[160,6144]{1,0:T(8,128)(2,1)S(1)}, bf16[160,6144]{1,0:T(8,128)(2,1)}, u32[]{:S(2)}) copy-start(bf16[160,6144]{1,0:T(8,128)(2,1)} %all-gather.3.cloned.1.call-done) | copy-start | bytes 5898244
  71.5 81.1 %copy-start.9 = (f32[128,2]{0,1:T(2,128)S(1)}, f32[128,2]{0,1:T(2,128)}, u32[]{:S(2)}) copy-start(f32[128,2]{0,1:T(2,128)} %param.10) | copy-start | bytes 3076
  163.0 9.0 %copy-start.5 = (bf16[160,1024]{1,0:T(8,128)(2,1)}, bf16[160,1024]{1,0:T(8,128)(2,1)S(1)}, u32[]{:S(2)}) copy-start(bf16[160,1024]{1,0:T(8,128)(2,1)S(1)} %get-tuple-element.12) | copy-start | bytes 983044
  163.0 9.0 %copy-start.7 = (bf16[160,1024]{1,0:T(8,128)(2,1)}, bf16[160,1024]{1,0:T(8,128)(2,1)S(1)}, u32[]{:S(2)}) copy-start(bf16[160,1024]{1,0:T(8,128)(2,1)S(1)} %get-tuple-element.11) | copy-start | bytes 983044
  182.8 3.3 copy-start.8
  182.8 153.2 %all-reduce.4.cloned.1.call-start = ((), (), s32[]{:S(2)}) async-start(), calls=%async_computation.4 | async-start | bytes 786432 | tf_op jit(solution)/shard_map/psum | solution.py:96
  186.2 6.6 %copy-start.6 = (bf16[160,1024]{1,0:T(8,128)(2,1)S(1)}, bf16[160,1024]{1,0:T(8,128)(2,1)}, u32[]{:S(2)}) copy-start(bf16[160,1024]{1,0:T(8,128)(2,1)} %copy-done.5) | copy-start | bytes 983044
  192.8 122.7 %copy-start.4 = (f32[128,40]{0,1:T(8,128)S(1)}, f32[128,40]{0,1:T(8,128)}, u32[]{:S(2)}) copy-start(f32[128,40]{0,1:T(8,128)} %copy-done.3) | copy-start | bytes 61444
  318.0 20.0 %copy-start.1 = (bf16[128,6144]{1,0:T(8,128)(2,1)S(1)}, bf16[128,6144]{1,0:T(8,128)(2,1)}, u32[]{:S(2)}) copy-start(bf16[128,6144]{1,0:T(8,128)(2,1)} %param.7) | copy-start | bytes 4718596
Sparse Core Ops, SparseCore 0:
  10.5 46.2 all-gather.2
  59.0 42.3 all-gather.4
  183.0 132.4 reduce-scatter.1
  318.2 17.7 all-reduce.3
where the time goes:
time: 345 us
  waiting for transfers between devices  196 us (57%)
  matrix products  74.3 us (22%)
  blocking collectives  51.3 us (15%)
  between operations  14.6 us (4%)
  other arithmetic  5.25 us (2%)
    reduce_scatter x1, waiting for transfers between devices, on_device(): lax.psum_scatter(flat_parts, ('seq', 'hid'), scatter_dimension=0, tiled=T...  116 us
    unnamed x2, blocking collectives  48.6 us
    all_gather x1, waiting for transfers between devices, on_device(): lax.all_gather(token_slots, 'seq', axis=0, tiled=True)  41.9 us
    all_gather x1, waiting for transfers between devices, on_device(): lax.all_gather(grad_slots, 'seq', axis=0, tiled=True)  29.9 us
    dot_general x1, matrix products, on_device(): jnp.einsum('sqf,hcf->shqc', up_blocks, up_mat.reshape(hid_count, piece_wi...  10.8 us
    dot_general x1, matrix products, on_device(): lax.dot_general(grads_e, down_mat, (((1,), (1,)), ((), ())), preferred_el...  10.4 us
    dot_general x1, matrix products, on_device(): lax.dot_general(weighted, grads_e, contract_rows, preferred_element_type=...  10.1 us
    dot_general x1, matrix products, on_device(): jnp.einsum('sqf,hcf->shqc', gate_blocks, gate_mat.reshape(hid_count, piec...  9.01 us
  transfers between devices with their start and end apart: 4, of which 4 were waited for; matrix products, arithmetic and copies ran while one was open for 12% of the time, Pallas kernels for 0%

commit v1 on v0

v1 whole, which is shorter than its diff:
```python
import jax
import jax.numpy as jnp
from jax import lax
from jax.sharding import PartitionSpec as P


def swap(x, axis, bits):
    size = lax.axis_size(axis)
    return lax.ppermute(x, axis, [(i, i ^ bits) for i in range(size)])


def pick_of(expert_ids, expert, capacity):
    tok_rows = expert_ids.shape[0]
    chosen = (expert_ids == expert).astype(jnp.int32)
    slot_index = (jnp.cumsum(chosen.reshape(-1)) - 1).reshape(tok_rows, 2)
    columns = jnp.arange(capacity, dtype=jnp.int32)
    return (
        (chosen[:, :, None] == 1) & (slot_index[:, :, None] == columns[None, None, :])
    ).astype(jnp.float32)


def on_device(tokens, out_grad, expert_ids, gate_probs, w_gate, w_up, w_down):
    expert = lax.axis_index("exp")
    hid = lax.axis_index("hid")
    tok_rows, model_width = tokens.shape
    capacity = 5 * tok_rows // 16
    seq_count = lax.axis_size("seq")
    hid_count = lax.axis_size("hid")
    piece = model_width // hid_count
    bf16, f32 = jnp.bfloat16, jnp.float32
    contract_rows = (((0,), (0,)), ((), ()))

    pick_own = pick_of(expert_ids, expert, capacity)
    pick_other = pick_of(expert_ids, 1 - expert, capacity)
    select_own = jnp.sum(pick_own, axis=1).astype(bf16)
    select_other = jnp.sum(pick_other, axis=1).astype(bf16)
    weight_own = jnp.sum(pick_own * gate_probs[:, :, None], axis=(0, 1))

    def slots_of(x):
        return lax.dot_general(
            select_own, x, contract_rows, preferred_element_type=f32
        ).astype(bf16)

    def quarter(x):
        return lax.dynamic_slice_in_dim(x, hid * piece, piece, axis=1)

    message = jnp.concatenate([slots_of(quarter(tokens)), slots_of(quarter(out_grad))], axis=0)
    arrived = [swap(message, "seq", k) for k in range(1, seq_count)]
    weight_box = jnp.broadcast_to(weight_own[None, :], (8, capacity))
    weights = [weight_own] + [swap(weight_box, "seq", k)[0] for k in range(1, seq_count)]
    weight_e = jnp.concatenate(weights)

    own_rows = slots_of(tokens)
    own_grads = slots_of(out_grad)
    row_pieces = [[] for _ in range(hid_count)]
    grad_pieces = [[] for _ in range(hid_count)]
    for block in arrived:
        row_pieces[0].append(block[:capacity])
        grad_pieces[0].append(block[capacity:])
        if hid_count == 4:
            one = swap(block, "hid", 1)
            two = swap(block, "hid", 2)
            three_rows = swap(one[:capacity], "hid", 2)
            three_grads = swap(two[capacity:], "hid", 1)
            got = [one, two, None]
            row_pieces[1].append(one[:capacity])
            grad_pieces[1].append(one[capacity:])
            row_pieces[2].append(two[:capacity])
            grad_pieces[2].append(two[capacity:])
            row_pieces[3].append(three_rows)
            grad_pieces[3].append(three_grads)
        else:
            for j in range(1, hid_count):
                other = swap(block, "hid", j)
                row_pieces[j].append(other[:capacity])
                grad_pieces[j].append(other[capacity:])

    def whole(own, pieces):
        rest = jnp.zeros(((seq_count - 1) * capacity, model_width), bf16)
        for j in range(hid_count):
            rest = lax.dynamic_update_slice_in_dim(
                rest, jnp.concatenate(pieces[j], axis=0), (hid ^ j) * piece, axis=1
            )
        return jnp.concatenate([own, rest], axis=0)

    rows_e = whole(own_rows, row_pieces)
    grads_e = whole(own_grads, grad_pieces)

    gate_mat, up_mat, down_mat = w_gate[0], w_up[0], w_down[0]
    gate_pre = jnp.dot(rows_e, gate_mat, preferred_element_type=f32)
    up_pre = jnp.dot(rows_e, up_mat, preferred_element_type=f32)
    sig_gate = jax.nn.sigmoid(gate_pre)
    activated = gate_pre * sig_gate
    hidden = (activated * up_pre).astype(bf16)
    back_hidden = lax.dot_general(
        grads_e, down_mat, (((1,), (1,)), ((), ())), preferred_element_type=f32
    )
    slot_part = jnp.sum(hidden.astype(f32) * back_hidden, axis=1)
    weighted = (weight_e[:, None] * hidden.astype(f32)).astype(bf16)
    scaled_back = weight_e[:, None] * back_hidden
    d_gate = (scaled_back * up_pre * (sig_gate * (1.0 + gate_pre * (1.0 - sig_gate)))).astype(bf16)
    d_up = (scaled_back * activated).astype(bf16)

    contract_last = (((1,), (1,)), ((), ()))

    def partial_of(j):
        start = (hid ^ j) * piece
        gate_part = lax.dynamic_slice_in_dim(gate_mat, start, piece, axis=0)
        up_part = lax.dynamic_slice_in_dim(up_mat, start, piece, axis=0)
        return lax.dot_general(
            d_gate, gate_part, contract_last, preferred_element_type=f32
        ) + lax.dot_general(d_up, up_part, contract_last, preferred_element_type=f32)

    received = [
        swap(partial_of(j).astype(bf16), "hid", j) for j in range(hid_count - 1, 0, -1)
    ]
    total = partial_of(0)
    for part in received:
        total = total + part.astype(f32)
    slot_box = jnp.broadcast_to(slot_part.reshape(1, -1), (8, seq_count * capacity))
    slot_all = slot_box
    for j in range(1, hid_count):
        slot_all = slot_all + swap(slot_box, "hid", j)
    own_sum = total[:capacity]
    slot_grad = slot_all[:, :capacity]
    for k in range(1, seq_count):
        lines = slice(k * capacity, (k + 1) * capacity)
        own_sum = own_sum + swap(total[lines].astype(bf16), "seq", k).astype(f32)
        slot_grad = slot_grad + swap(slot_all[:, lines], "seq", k)

    half = own_sum.astype(bf16)
    other_half = swap(half, "exp", 1)
    other_slot = swap(slot_grad, "exp", 1)
    d_tokens = jnp.dot(select_own, half, preferred_element_type=f32) + jnp.dot(
        select_other, other_half, preferred_element_type=f32
    )
    d_gates = jnp.sum(pick_own * slot_grad[0][None, None, :], axis=2) + jnp.sum(
        pick_other * other_slot[0][None, None, :], axis=2
    )

    grad_down = lax.dot_general(
        weighted, grads_e, contract_rows, preferred_element_type=f32
    ).astype(bf16)
    grad_gate = lax.dot_general(
        rows_e, d_gate, contract_rows, preferred_element_type=f32
    ).astype(bf16)
    grad_up = lax.dot_general(
        rows_e, d_up, contract_rows, preferred_element_type=f32
    ).astype(bf16)
    return (grad_gate[None], grad_up[None], grad_down[None], d_tokens, d_gates)


def solution(mesh):
    return jax.shard_map(
        on_device,
        mesh=mesh,
        in_specs=(
            P("seq", None),
            P("seq", None),
            P("seq", None),
            P("seq", None),
            P("exp", None, ("seq", "hid")),
            P("exp", None, ("seq", "hid")),
            P("exp", ("seq", "hid"), None),
        ),
        out_specs=(
            P("exp", None, ("seq", "hid")),
            P("exp", None, ("seq", "hid")),
            P("exp", ("seq", "hid"), None),
            P("seq", "hid"),
            P("seq", None),
        ),
        check_vma=False,
    )
```

time: 345 us -> 174 us (0.50)
  waiting for transfers between devices: 196 us -> 45.4 us
  blocking collectives: 51.3 us -> 0 us
  starting transfers between devices: 0.16 us -> 38.7 us
  between operations: 14.6 us -> 1.14 us
  local copies, waits for them, and re-layouts: 3.03 us -> 8.36 us
    reduce_scatter x1 -> x0, waiting for transfers between devices: 116 us -> none  [on_device(): lax.psum_scatter(flat_parts, ('seq', 'hid'), scatter_dimension=0, tiled=T...]
    all_gather x2 -> x0, waiting for transfers between devices: 71.8 us -> none  [the longest x1 41.9 us: on_device(): lax.all_gather(token_slots, 'seq', axis=0, tiled=True)]
    unnamed x2 -> x0, blocking collectives: 48.6 us -> none
    ppermute x0 -> x32, waiting for transfers between devices: none -> 45.4 us  [swap(): return lax.ppermute(x, axis, [(i, i ^ bits) for i in range(size)])]
    ppermute x0 -> x32, starting transfers between devices: none -> 38.7 us  [swap(): return lax.ppermute(x, axis, [(i, i ^ bits) for i in range(size)])]
    psum x1 -> x0, waiting for transfers between devices: 7.95 us -> none  [on_device(): lax.psum(token_part.astype(jnp.bfloat16), 'exp').astype(jnp.float32)]
    dot_general x9 -> x18, matrix products: 53.9 us -> 52.5 us  [the longest x4 16.4 us: partial_of(): lax.dot_general(d_up, up_part, contract_last, preferred_element_type=f32)]
  transfers between devices with their start and end apart: 4 -> 32, of which waited for: 4 -> 15; matrix products, arithmetic and copies ran while one was open for 12% -> 39% of each run, Pallas kernels for 0% -> 0%
where the time goes in v1:
time: 174 us; the launch traced here: 173 us
  matrix products  72.5 us (42%)
  waiting for transfers between devices  45.4 us (26%)
  starting transfers between devices  38.7 us (22%)
  local copies, waits for them, and re-layouts  8.36 us (5%)
  other arithmetic  7.22 us (4%)
    ppermute x32, waiting for transfers between devices, swap(): return lax.ppermute(x, axis, [(i, i ^ bits) for i in range(size)])  45.4 us
    ppermute x32, starting transfers between devices, swap(): return lax.ppermute(x, axis, [(i, i ^ bits) for i in range(size)])  38.7 us
    dot_general x4, matrix products, partial_of(): lax.dot_general(d_up, up_part, contract_last, preferred_element_type=f32)  16.4 us
    dot_general x4, matrix products, partial_of(): lax.dot_general(d_gate, gate_part, contract_last, preferred_element_type=...  11.2 us
    dot_general x1, matrix products, on_device(): lax.dot_general(grads_e, down_mat, (((1,), (1,)), ((), ())), preferred_el...  10.1 us
    dot_general x1, matrix products, on_device(): lax.dot_general(weighted, grads_e, contract_rows, preferred_element_type=...  9.93 us
    dot_general x1, matrix products, on_device(): lax.dot_general(rows_e, d_gate, contract_rows, preferred_element_type=f32)  8.13 us
    dot_general x1, matrix products, on_device(): lax.dot_general(rows_e, d_up, contract_rows, preferred_element_type=f32)  7.98 us
  transfers between devices with their start and end apart: 32, of which 15 were waited for; matrix products, arithmetic and copies ran while one was open for 39% of the time, Pallas kernels for 0%

profile of v1, /device:TPU:0, one launch (start us, length us, event | category | flops | bytes accessed | tf_op | source)
XLA Modules:
  0.0 173.4 jit_solution(13388430199129351818)
XLA Ops:
  5.4 5.1 %collective-permute-start.2 = (bf16[80,1536]{1,0:T(8,128)(2,1)}, bf16[80,1536]{1,0:T(8,128)(2,1)}, u32[]{:S(2)}, u32[]{:S(2)}) collective-permute-start(bf16[80,1536]{1,0:T(8,128)(2,1)} %pad_maximum_fusion.4), channel_id=1, source_target_pairs={{0,24},{8,16},{16,8},{24,0},{1,25},{9,17},{17,9},{25,1},{2,26},{10... | collective-permute-start | bytes 737288 | tf_op jit(solution)/shard_map/ppermute | solution.py:9
  12.5 5.2 %collective-permute-done.2 = bf16[80,1536]{1,0:T(8,128)(2,1)} collective-permute-done((bf16[80,1536]{1,0:T(8,128)(2,1)}, bf16[80,1536]{1,0:T(8,128)(2,1)}, u32[]{:S(2)}, u32[]{:S(2)}) %collective-permute-start.2) | collective-permute-done | bytes 245792 | tf_op jit(solution)/shard_map/ppermute | solution.py:9
  17.7 1.7 collective-permute-start.8
  20.4 11.3 %collective-permute-done.1 = bf16[80,1536]{1,0:T(8,128)(2,1)} collective-permute-done((bf16[80,1536]{1,0:T(8,128)(2,1)}, bf16[80,1536]{1,0:T(8,128)(2,1)}, u32[]{:S(2)}, u32[]{:S(2)}) %collective-permute-start.1) | collective-permute-done | bytes 245792 | tf_op jit(solution)/shard_map/ppermute | solution.py:9
  32.8 1.6 collective-permute-start.5
  37.2 1.6 collective-permute-start.3
  38.8 3.3 %collective-permute-done.5 = bf16[80,1536]{1,0:T(8,128)(2,1)S(1)} collective-permute-done((bf16[80,1536]{1,0:T(8,128)(2,1)}, bf16[80,1536]{1,0:T(8,128)(2,1)S(1)}, u32[]{:S(2)}, u32[]{:S(2)}) %collective-permute-start.5) | collective-permute-done | bytes 245792 | tf_op jit(solution)/shard_map/ppermute | solution.py:9
  43.5 3.8 %collective-permute-done.4 = bf16[80,1536]{1,0:T(8,128)(2,1)S(1)} collective-permute-done((bf16[80,1536]{1,0:T(8,128)(2,1)}, bf16[80,1536]{1,0:T(8,128)(2,1)S(1)}, u32[]{:S(2)}, u32[]{:S(2)}) %collective-permute-start.4) | collective-permute-done | bytes 245792 | tf_op jit(solution)/shard_map/ppermute | solution.py:9
  48.8 3.2 %collective-permute-done.3 = bf16[80,1536]{1,0:T(8,128)(2,1)S(1)} collective-permute-done((bf16[80,1536]{1,0:T(8,128)(2,1)S(1)}, bf16[80,1536]{1,0:T(8,128)(2,1)S(1)}, u32[]{:S(2)}, u32[]{:S(2)}) %collective-permute-start.3) | collective-permute-done | bytes 245792 | tf_op jit(solution)/shard_map/ppermute | solution.py:9
  54.2 1.5 collective-permute-start.16
  56.9 1.6 collective-permute-done.9
  58.6 2.2 %fusion = f32[160,1024]{1,0:T(8,128)S(1)} fusion(bf16[1,6144,1024]{2,1,0:T(8,128)(2,1)S(1)} %copy-done.2, bf16[120,6144]{1,0:T(8,128)(2,1)S(1)} %maximum_dynamic-update-slice_fusion.3, bf16[40,6144]{1,0:T(8,128)(2,1)S(1)} %copy-done.10), kind=kOutput, calls=%fused_computation | convolution fusion | flops 2017198080 | bytes 15204352 | tf_op jit(solution)/shard_map/dot_general | solution.py:90
  63.7 2.2 %fusion.2 = f32[160,1024]{1,0:T(8,128)S(1)} fusion(bf16[1,6144,1024]{2,1,0:T(8,128)(2,1)S(1)} %bitcast.90, bf16[120,6144]{1,0:T(8,128)(2,1)S(1)} %maximum_dynamic-update-slice_fusion.3, bf16[40,6144]{1,0:T(8,128)(2,1)S(1)} %copy-done.10), kind=kOutput, calls=%fused_computation.2 | convolution fusion | flops 2017198080 | bytes 15204352 | tf_op jit(solution)/shard_map/dot_general | solution.py:91
  66.0 10.1 %fusion.52 = (f32[160]{0:T(256)S(1)}, bf16[160,1024]{1,0:T(8,128)(2,1)}, f32[160,1024]{1,0:T(8,128)S(1)}) fusion(f32[160,1024]{1,0:T(8,128)S(1)} %fusion.2, f32[160,1024]{1,0:T(8,128)S(1)} %fusion, bf16[1,1024,6144]{2,1,0:T(8,128)(2,1)} %param.13, bf16[120,6144]{1,0:T(8,128)(2,1)S(1)} %maximum_dynamic-update-slice_fusion.7, ...), kind=kOutput, calls=%fused_computation.51 | convolution fusion | flops 2018672512 | bytes 16843392 | tf_op jit(solution)/shard_map/dot_general | solution.py:95
  77.4 1.7 collective-permute-start.27
  80.3 1.6 collective-permute-done.27
  82.8 2.4 %collective-permute-start.30 = (f32[8,40]{1,0:T(8,128)S(1)}, f32[8,40]{1,0:T(8,128)S(1)}, u32[]{:S(2)}, u32[]{:S(2)}) collective-permute-start(f32[8,40]{1,0:T(8,128)S(1)} %get-tuple-element.39), channel_id=1, source_target_pairs={{0,24},{8,16},{16,8},{24,0},{1,25},{9,17},{17,9},{25,1},{2,26},{10... | collective-permute-start | bytes 3848 | tf_op jit(solution)/shard_map/ppermute | solution.py:9
  94.7 1.9 %collective-permute-start.12 = (f32[8,40]{1,0:T(8,128)S(1)}, f32[8,40]{1,0:T(8,128)S(1)}, u32[]{:S(2)}, u32[]{:S(2)}) collective-permute-start(f32[8,40]{1,0:T(8,128)S(1)} %broadcast_in_dim.10), channel_id=1, source_target_pairs={{0,8},{8,0},{16,24},{24,16},{1,9},{9,1},{17,25},{25,17},{2,10},{10... | collective-permute-start | bytes 3848 | tf_op jit(solution)/shard_map/ppermute | solution.py:9
  99.0 4.0 %fusion.6 = f32[160,1536]{1,0:T(8,128)} fusion(bf16[160,1024]{1,0:T(8,128)(2,1)S(1)} %get-tuple-element.15, bf16[1,6144,1024]{2,1,0:T(8,128)(2,1)} %param.12, s32[]{:T(128)S(6)} %select_n.9), kind=kOutput, calls=%fused_computation.11 | convolution fusion | flops 503316480 | bytes 4456452 | tf_op jit(solution)/shard_map/dot_general | solution.py:112
  103.0 4.0 %fusion.10 = f32[160,1536]{1,0:T(8,128)} fusion(bf16[160,1024]{1,0:T(8,128)(2,1)S(1)} %get-tuple-element.15, bf16[1,6144,1024]{2,1,0:T(8,128)(2,1)} %param.12, s32[]{:T(128)S(6)} %select_n.10), kind=kOutput, calls=%fused_computation.15 | convolution fusion | flops 503316480 | bytes 4456452 | tf_op jit(solution)/shard_map/dot_general | solution.py:112
  107.0 4.2 %fusion.14 = f32[160,1536]{1,0:T(8,128)} fusion(bf16[160,1024]{1,0:T(8,128)(2,1)S(1)} %get-tuple-element.15, bf16[1,6144,1024]{2,1,0:T(8,128)(2,1)} %param.12, s32[]{:T(128)S(6)} %select_n.11), kind=kOutput, calls=%fused_computation.19 | convolution fusion | flops 503316480 | bytes 4456452 | tf_op jit(solution)/shard_map/dot_general | solution.py:112
  111.2 4.2 %fusion.18 = f32[160,1536]{1,0:T(8,128)} fusion(bf16[160,1024]{1,0:T(8,128)(2,1)S(1)} %get-tuple-element.15, bf16[1,6144,1024]{2,1,0:T(8,128)(2,1)} %param.12, s32[]{:T(128)S(6)} %select_n.8), kind=kOutput, calls=%fused_computation.23 | convolution fusion | flops 503316480 | bytes 4456452 | tf_op jit(solution)/shard_map/dot_general | solution.py:112
  115.4 8.1 %convert_bitcast_fusion.2 = bf16[1,6144,1024]{2,1,0:T(8,128)(2,1)} fusion(bf16[160,1024]{1,0:T(8,128)(2,1)S(1)} %get-tuple-element.16, bf16[120,6144]{1,0:T(8,128)(2,1)} %copy-done.9, bf16[40,6144]{1,0:T(8,128)(2,1)S(1)} %copy-done.11), kind=kOutput, calls=%fused_computation.8 | convolution fusion | flops 2023489536 | bytes 14876672 | tf_op jit(solution)/shard_map/dot_general | solution.py:144
  123.6 3.3 %fusion.42 = bf16[160,1536]{1,0:T(8,128)(2,1)} fusion(f32[160,1536]{1,0:T(8,128)} %fusion.6, bf16[160,1024]{1,0:T(8,128)(2,1)S(1)} %get-tuple-element.16, bf16[1,6144,1024]{2,1,0:T(8,128)(2,1)S(1)} %bitcast.92, s32[]{:T(128)S(6)} %select_n.9), kind=kOutput, calls=%fused_computation.40 | convolution fusion | flops 503808000 | bytes 4947972 | tf_op jit(solution)/shard_map/dot_general | solution.py:110
  127.5 2.0 %fusion.45 = bf16[160,1536]{1,0:T(8,128)(2,1)} fusion(f32[160,1536]{1,0:T(8,128)S(1)} %copy-done.5, bf16[160,1024]{1,0:T(8,128)(2,1)S(1)} %get-tuple-element.16, bf16[1,6144,1024]{2,1,0:T(8,128)(2,1)S(1)} %bitcast.92, s32[]{:T(128)S(6)} %select_n.10), kind=kOutput, calls=%fused_computation.41 | convolution fusion | flops 503808000 | bytes 4947972 | tf_op jit(solution)/shard_map/dot_general | solution.py:110
  130.6 2.0 %fusion.48 = bf16[160,1536]{1,0:T(8,128)(2,1)} fusion(f32[160,1536]{1,0:T(8,128)S(1)} %copy-done.4, bf16[160,1024]{1,0:T(8,128)(2,1)S(1)} %get-tuple-element.16, bf16[1,6144,1024]{2,1,0:T(8,128)(2,1)S(1)} %bitcast.92, s32[]{:T(128)S(6)} %select_n.11), kind=kOutput, calls=%fused_computation.42 | convolution fusion | flops 503808000 | bytes 4947972 | tf_op jit(solution)/shard_map/dot_general | solution.py:110
  132.6 1.7 collective-permute-start.18
  134.3 8.0 %convert_bitcast_fusion.1 = bf16[1,6144,1024]{2,1,0:T(8,128)(2,1)} fusion(bf16[160,1024]{1,0:T(8,128)(2,1)S(1)} %get-tuple-element.15, bf16[120,6144]{1,0:T(8,128)(2,1)} %copy-done.9, bf16[40,6144]{1,0:T(8,128)(2,1)S(1)} %copy-done.11), kind=kOutput, calls=%fused_computation.7 | convolution fusion | flops 2023489536 | bytes 14876672 | tf_op jit(solution)/shard_map/dot_general | solution.py:147
  142.3 9.7 %collective-permute-done.19 = bf16[160,1536]{1,0:T(8,128)(2,1)} collective-permute-done((bf16[160,1536]{1,0:T(8,128)(2,1)}, bf16[160,1536]{1,0:T(8,128)(2,1)}, u32[]{:S(2)}, u32[]{:S(2)}) %collective-permute-start.19) | collective-permute-done | bytes 491552 | tf_op jit(solution)/shard_map/ppermute | solution.py:9
  152.0 3.9 %fusion.92 = (bf16[160,1536]{1,0:T(8,128)(2,1)S(1)}, f32[160,1536]{1,0:T(8,128)}) fusion(bf16[160,1536]{1,0:T(8,128)(2,1)} %collective-permute-done.20, bf16[160,1536]{1,0:T(8,128)(2,1)} %collective-permute-done.19, bf16[160,1536]{1,0:T(8,128)(2,1)} %collective-permute-done.18, f32[160,1536]{1,0:T(8,128)} %fusion.18, ...), kind=kOutput, calls=%fused_computation.125 | convolution fusion | flops 505282560 | bytes 7405572 | tf_op jit(solution)/shard_map/dot_general | solution.py:110
  157.7 1.8 %collective-permute-start.22 = (bf16[40,1536]{1,0:T(8,128)(2,1)S(1)}, bf16[40,1536]{1,0:T(8,128)(2,1)S(1)}, u32[]{:S(2)}, u32[]{:S(2)}) collective-permute-start(bf16[40,1536]{1,0:T(8,128)(2,1)S(1)} %get-tuple-element.19), channel_id=1, source_target_pairs={{0,16},{8,24},{16,0},{24,8},{1,17},{9,25},{17,1},{25,9},{2,18},{10... | collective-permute-start | bytes 368648 | tf_op jit(solution)/shard_map/ppermute | solution.py:9
  159.6 9.9 %convert_bitcast_fusion = bf16[1,1024,6144]{2,1,0:T(8,128)(2,1)} fusion(bf16[120,6144]{1,0:T(8,128)(2,1)} %copy-done.3, bf16[40,6144]{1,0:T(8,128)(2,1)S(1)} %copy-done.8, bf16[160,1024]{1,0:T(8,128)(2,1)} %get-tuple-element.12, f32[160]{0:T(256)S(1)} %pad_maximum_fusion.5), kind=kOutput, calls=%fused_computation.6 | convolution fusion | flops 2023981056 | bytes 14877312 | tf_op jit(solution)/shard_map/dot_general | solution.py:141
  (164 shorter events, 43.6 us)
Async XLA Ops:
  5.4 12.3 %collective-permute-start.2 = (bf16[80,1536]{1,0:T(8,128)(2,1)}, bf16[80,1536]{1,0:T(8,128)(2,1)}, u32[]{:S(2)}, u32[]{:S(2)}) collective-permute-start(bf16[80,1536]{1,0:T(8,128)(2,1)} %pad_maximum_fusion.4), channel_id=1, source_target_pairs={{0,24},{8,16},{16,8},{24,0},{1,25},{9,17},{17,9},{25,1},{2,26},{10... | collective-permute-start | bytes 737288 | tf_op jit(solution)/shard_map/ppermute | solution.py:9
  10.4 21.2 %collective-permute-start.1 = (bf16[80,1536]{1,0:T(8,128)(2,1)}, bf16[80,1536]{1,0:T(8,128)(2,1)}, u32[]{:S(2)}, u32[]{:S(2)}) collective-permute-start(bf16[80,1536]{1,0:T(8,128)(2,1)} %pad_maximum_fusion.4), channel_id=1, source_target_pairs={{0,16},{8,24},{16,0},{24,8},{1,17},{9,25},{17,1},{25,9},{2,18},{10... | collective-permute-start | bytes 737288 | tf_op jit(solution)/shard_map/ppermute | solution.py:9
  10.4 22.2 %collective-permute-start = (bf16[80,1536]{1,0:T(8,128)(2,1)}, bf16[80,1536]{1,0:T(8,128)(2,1)S(1)}, u32[]{:S(2)}, u32[]{:S(2)}) collective-permute-start(bf16[80,1536]{1,0:T(8,128)(2,1)} %pad_maximum_fusion.4), channel_id=1, source_target_pairs={{0,8},{8,0},{16,24},{24,16},{1,9},{9,1},{17,25},{25,17},{2,10},{10... | collective-permute-start | bytes 737288 | tf_op jit(solution)/shard_map/ppermute | solution.py:9
  17.7 19.5 %collective-permute-start.8 = (bf16[80,1536]{1,0:T(8,128)(2,1)}, bf16[80,1536]{1,0:T(8,128)(2,1)S(1)}, u32[]{:S(2)}, u32[]{:S(2)}) collective-permute-start(bf16[80,1536]{1,0:T(8,128)(2,1)} %collective-permute-done.2), channel_id=1, source_target_pairs={{0,2},{1,3},{2,0},{3,1},{4,6},{5,7},{6,4},{7,5},{8,10},{9,11},{10,... | collective-permute-start | bytes 737288 | tf_op jit(solution)/shard_map/ppermute | solution.py:9
  32.8 9.2 %collective-permute-start.5 = (bf16[80,1536]{1,0:T(8,128)(2,1)}, bf16[80,1536]{1,0:T(8,128)(2,1)S(1)}, u32[]{:S(2)}, u32[]{:S(2)}) collective-permute-start(bf16[80,1536]{1,0:T(8,128)(2,1)} %collective-permute-done.2), channel_id=1, source_target_pairs={{0,1},{1,0},{2,3},{3,2},{4,5},{5,4},{6,7},{7,6},{8,9},{9,8},{10,11... | collective-permute-start | bytes 737288 | tf_op jit(solution)/shard_map/ppermute | solution.py:9
  34.4 19.1 %collective-permute-start.7 = (bf16[80,1536]{1,0:T(8,128)(2,1)}, bf16[80,1536]{1,0:T(8,128)(2,1)S(1)}, u32[]{:S(2)}, u32[]{:S(2)}) collective-permute-start(bf16[80,1536]{1,0:T(8,128)(2,1)} %collective-permute-done.1), channel_id=1, source_target_pairs={{0,2},{1,3},{2,0},{3,1},{4,6},{5,7},{6,4},{7,5},{8,10},{9,11},{10,... | collective-permute-start | bytes 737288 | tf_op jit(solution)/shard_map/ppermute | solution.py:9
  35.9 11.4 %collective-permute-start.4 = (bf16[80,1536]{1,0:T(8,128)(2,1)}, bf16[80,1536]{1,0:T(8,128)(2,1)S(1)}, u32[]{:S(2)}, u32[]{:S(2)}) collective-permute-start(bf16[80,1536]{1,0:T(8,128)(2,1)} %collective-permute-done.1), channel_id=1, source_target_pairs={{0,1},{1,0},{2,3},{3,2},{4,5},{5,4},{6,7},{7,6},{8,9},{9,8},{10,11... | collective-permute-start | bytes 737288 | tf_op jit(solution)/shard_map/ppermute | solution.py:9
  36.5 17.8 %collective-permute-start.6 = (bf16[80,1536]{1,0:T(8,128)(2,1)S(1)}, bf16[80,1536]{1,0:T(8,128)(2,1)S(1)}, u32[]{:S(2)}, u32[]{:S(2)}) collective-permute-start(bf16[80,1536]{1,0:T(8,128)(2,1)S(1)} %collective-permute-done), channel_id=1, source_target_pairs={{0,2},{1,3},{2,0},{3,1},{4,6},{5,7},{6,4},{7,5},{8,10},{9,11},{10,... | collective-permute-start | bytes 737288 | tf_op jit(solution)/shard_map/ppermute | solution.py:9
  37.2 14.8 %collective-permute-start.3 = (bf16[80,1536]{1,0:T(8,128)(2,1)S(1)}, bf16[80,1536]{1,0:T(8,128)(2,1)S(1)}, u32[]{:S(2)}, u32[]{:S(2)}) collective-permute-start(bf16[80,1536]{1,0:T(8,128)(2,1)S(1)} %collective-permute-done), channel_id=1, source_target_pairs={{0,1},{1,0},{2,3},{3,2},{4,5},{5,4},{6,7},{7,6},{8,9},{9,8},{10,11... | collective-permute-start | bytes 737288 | tf_op jit(solution)/shard_map/ppermute | solution.py:9
  42.0 23.9 %collective-permute-start.17 = (bf16[40,1536]{1,0:T(8,128)(2,1)S(1)}, bf16[40,1536]{1,0:T(8,128)(2,1)S(1)}, u32[]{:S(2)}, u32[]{:S(2)}) collective-permute-start(bf16[40,1536]{1,0:T(8,128)(2,1)S(1)} %get-tuple-element.24), channel_id=1, source_target_pairs={{0,1},{1,0},{2,3},{3,2},{4,5},{5,4},{6,7},{7,6},{8,9},{9,8},{10,11... | collective-permute-start | bytes 368648 | tf_op jit(solution)/shard_map/ppermute | solution.py:9
  47.3 8.6 %collective-permute-start.11 = (bf16[40,1536]{1,0:T(8,128)(2,1)S(1)}, bf16[40,1536]{1,0:T(8,128)(2,1)S(1)}, u32[]{:S(2)}, u32[]{:S(2)}) collective-permute-start(bf16[40,1536]{1,0:T(8,128)(2,1)S(1)} %get-tuple-element.31), channel_id=1, source_target_pairs={{0,2},{1,3},{2,0},{3,1},{4,6},{5,7},{6,4},{7,5},{8,10},{9,11},{10,... | collective-permute-start | bytes 368648 | tf_op jit(solution)/shard_map/ppermute | solution.py:9
  52.0 4.9 %collective-permute-start.10 = (bf16[40,1536]{1,0:T(8,128)(2,1)S(1)}, bf16[40,1536]{1,0:T(8,128)(2,1)S(1)}, u32[]{:S(2)}, u32[]{:S(2)}) collective-permute-start(bf16[40,1536]{1,0:T(8,128)(2,1)S(1)} %get-tuple-element.29), channel_id=1, source_target_pairs={{0,2},{1,3},{2,0},{3,1},{4,6},{5,7},{6,4},{7,5},{8,10},{9,11},{10,... | collective-permute-start | bytes 368648 | tf_op jit(solution)/shard_map/ppermute | solution.py:9
  53.5 4.9 %collective-permute-start.9 = (bf16[40,1536]{1,0:T(8,128)(2,1)S(1)}, bf16[40,1536]{1,0:T(8,128)(2,1)S(1)}, u32[]{:S(2)}, u32[]{:S(2)}) collective-permute-start(bf16[40,1536]{1,0:T(8,128)(2,1)S(1)} %get-tuple-element.27), channel_id=1, source_target_pairs={{0,2},{1,3},{2,0},{3,1},{4,6},{5,7},{6,4},{7,5},{8,10},{9,11},{10,... | collective-permute-start | bytes 368648 | tf_op jit(solution)/shard_map/ppermute | solution.py:9
  54.2 11.7 %collective-permute-start.16 = (bf16[40,1536]{1,0:T(8,128)(2,1)S(1)}, bf16[40,1536]{1,0:T(8,128)(2,1)S(1)}, u32[]{:S(2)}, u32[]{:S(2)}) collective-permute-start(bf16[40,1536]{1,0:T(8,128)(2,1)S(1)} %get-tuple-element.22), channel_id=1, source_target_pairs={{0,1},{1,0},{2,3},{3,2},{4,5},{5,4},{6,7},{7,6},{8,9},{9,8},{10,11... | collective-permute-start | bytes 368648 | tf_op jit(solution)/shard_map/ppermute | solution.py:9
  55.9 10.0 %collective-permute-start.15 = (bf16[40,1536]{1,0:T(8,128)(2,1)S(1)}, bf16[40,1536]{1,0:T(8,128)(2,1)S(1)}, u32[]{:S(2)}, u32[]{:S(2)}) collective-permute-start(bf16[40,1536]{1,0:T(8,128)(2,1)S(1)} %get-tuple-element.20), channel_id=1, source_target_pairs={{0,1},{1,0},{2,3},{3,2},{4,5},{5,4},{6,7},{7,6},{8,9},{9,8},{10,11... | collective-permute-start | bytes 368648 | tf_op jit(solution)/shard_map/ppermute | solution.py:9
  76.1 4.2 %collective-permute-start.26 = (f32[8,160]{1,0:T(8,128)S(1)}, f32[8,160]{1,0:T(8,128)S(1)}, u32[]{:S(2)}, u32[]{:S(2)}) collective-permute-start(f32[8,160]{1,0:T(8,128)S(1)} %broadcast_in_dim.14), channel_id=1, source_target_pairs={{0,2},{1,3},{2,0},{3,1},{4,6},{5,7},{6,4},{7,5},{8,10},{9,11},{10,... | collective-permute-start | bytes 15368 | tf_op jit(solution)/shard_map/ppermute | solution.py:9
  77.4 4.5 %collective-permute-start.27 = (f32[8,160]{1,0:T(8,128)S(1)}, f32[8,160]{1,0:T(8,128)S(1)}, u32[]{:S(2)}, u32[]{:S(2)}) collective-permute-start(f32[8,160]{1,0:T(8,128)S(1)} %broadcast_in_dim.14), channel_id=1, source_target_pairs={{0,3},{1,2},{2,1},{3,0},{4,7},{5,6},{6,5},{7,4},{8,11},{9,10},{10,... | collective-permute-start | bytes 15368 | tf_op jit(solution)/shard_map/ppermute | solution.py:9
  79.1 3.7 %collective-permute-start.25 = (f32[8,160]{1,0:T(8,128)S(1)}, f32[8,160]{1,0:T(8,128)S(1)}, u32[]{:S(2)}, u32[]{:S(2)}) collective-permute-start(f32[8,160]{1,0:T(8,128)S(1)} %broadcast_in_dim.14), channel_id=1, source_target_pairs={{0,1},{1,0},{2,3},{3,2},{4,5},{5,4},{6,7},{7,6},{8,9},{9,8},{10,11... | collective-permute-start | bytes 15368 | tf_op jit(solution)/shard_map/ppermute | solution.py:9
  82.8 4.0 %collective-permute-start.28 = (f32[8,40]{1,0:T(8,128)S(1)}, f32[8,40]{1,0:T(8,128)S(1)}, u32[]{:S(2)}, u32[]{:S(2)}) collective-permute-start(f32[8,40]{1,0:T(8,128)S(1)} %get-tuple-element.38), channel_id=1, source_target_pairs={{0,8},{8,0},{16,24},{24,16},{1,9},{9,1},{17,25},{25,17},{2,10},{10... | collective-permute-start | bytes 3848 | tf_op jit(solution)/shard_map/ppermute | solution.py:9
  82.8 5.5 %collective-permute-start.30 = (f32[8,40]{1,0:T(8,128)S(1)}, f32[8,40]{1,0:T(8,128)S(1)}, u32[]{:S(2)}, u32[]{:S(2)}) collective-permute-start(f32[8,40]{1,0:T(8,128)S(1)} %get-tuple-element.39), channel_id=1, source_target_pairs={{0,24},{8,16},{16,8},{24,0},{1,25},{9,17},{17,9},{25,1},{2,26},{10... | collective-permute-start | bytes 3848 | tf_op jit(solution)/shard_map/ppermute | solution.py:9
  85.2 4.5 %collective-permute-start.29 = (f32[8,40]{1,0:T(8,128)S(1)}, f32[8,40]{1,0:T(8,128)S(1)}, u32[]{:S(2)}, u32[]{:S(2)}) collective-permute-start(f32[8,40]{1,0:T(8,128)S(1)} %get-tuple-element.40), channel_id=1, source_target_pairs={{0,16},{8,24},{16,0},{24,8},{1,17},{9,25},{17,1},{25,9},{2,18},{10... | collective-permute-start | bytes 3848 | tf_op jit(solution)/shard_map/ppermute | solution.py:9
  91.7 5.4 %collective-permute-start.14 = (f32[8,40]{1,0:T(8,128)S(1)}, f32[8,40]{1,0:T(8,128)S(1)}, u32[]{:S(2)}, u32[]{:S(2)}) collective-permute-start(f32[8,40]{1,0:T(8,128)S(1)} %broadcast_in_dim.10), channel_id=1, source_target_pairs={{0,24},{8,16},{16,8},{24,0},{1,25},{9,17},{17,9},{25,1},{2,26},{10... | collective-permute-start | bytes 3848 | tf_op jit(solution)/shard_map/ppermute | solution.py:9
  93.7 4.5 %collective-permute-start.13 = (f32[8,40]{1,0:T(8,128)S(1)}, f32[8,40]{1,0:T(8,128)S(1)}, u32[]{:S(2)}, u32[]{:S(2)}) collective-permute-start(f32[8,40]{1,0:T(8,128)S(1)} %broadcast_in_dim.10), channel_id=1, source_target_pairs={{0,16},{8,24},{16,0},{24,8},{1,17},{9,25},{17,1},{25,9},{2,18},{10... | collective-permute-start | bytes 3848 | tf_op jit(solution)/shard_map/ppermute | solution.py:9
  94.7 3.6 %collective-permute-start.12 = (f32[8,40]{1,0:T(8,128)S(1)}, f32[8,40]{1,0:T(8,128)S(1)}, u32[]{:S(2)}, u32[]{:S(2)}) collective-permute-start(f32[8,40]{1,0:T(8,128)S(1)} %broadcast_in_dim.10), channel_id=1, source_target_pairs={{0,8},{8,0},{16,24},{24,16},{1,9},{9,1},{17,25},{25,17},{2,10},{10... | collective-permute-start | bytes 3848 | tf_op jit(solution)/shard_map/ppermute | solution.py:9
  96.6 74.0 %collective-permute-start.31 = (f32[8,40]{1,0:T(8,128)}, f32[8,40]{1,0:T(8,128)}, u32[]{:S(2)}, u32[]{:S(2)}) collective-permute-start(f32[8,40]{1,0:T(8,128)} %fusion.78), channel_id=1, source_target_pairs={{0,4},{4,0},{1,5},{5,1},{2,6},{6,2},{3,7},{7,3},{8,12},{12,8},{9,1... | collective-permute-start | bytes 3848 | tf_op jit(solution)/shard_map/ppermute | solution.py:9
  126.8 15.5 %collective-permute-start.20 = (bf16[160,1536]{1,0:T(8,128)(2,1)}, bf16[160,1536]{1,0:T(8,128)(2,1)}, u32[]{:S(2)}, u32[]{:S(2)}) collective-permute-start(bf16[160,1536]{1,0:T(8,128)(2,1)} %fusion.42), channel_id=1, source_target_pairs={{0,1},{1,0},{2,3},{3,2},{4,5},{5,4},{6,7},{7,6},{8,9},{9,8},{10,11... | collective-permute-start | bytes 1474568 | tf_op jit(solution)/shard_map/ppermute | solution.py:9
  129.5 22.5 %collective-permute-start.19 = (bf16[160,1536]{1,0:T(8,128)(2,1)}, bf16[160,1536]{1,0:T(8,128)(2,1)}, u32[]{:S(2)}, u32[]{:S(2)}) collective-permute-start(bf16[160,1536]{1,0:T(8,128)(2,1)} %fusion.45), channel_id=1, source_target_pairs={{0,2},{1,3},{2,0},{3,1},{4,6},{5,7},{6,4},{7,5},{8,10},{9,11},{10,... | collective-permute-start | bytes 1474568 | tf_op jit(solution)/shard_map/ppermute | solution.py:9
  132.6 19.4 %collective-permute-start.18 = (bf16[160,1536]{1,0:T(8,128)(2,1)}, bf16[160,1536]{1,0:T(8,128)(2,1)}, u32[]{:S(2)}, u32[]{:S(2)}) collective-permute-start(bf16[160,1536]{1,0:T(8,128)(2,1)} %fusion.48), channel_id=1, source_target_pairs={{0,3},{1,2},{2,1},{3,0},{4,7},{5,6},{6,5},{7,4},{8,11},{9,10},{10,... | collective-permute-start | bytes 1474568 | tf_op jit(solution)/shard_map/ppermute | solution.py:9
  156.0 13.5 %collective-permute-start.21 = (bf16[40,1536]{1,0:T(8,128)(2,1)S(1)}, bf16[40,1536]{1,0:T(8,128)(2,1)S(1)}, u32[]{:S(2)}, u32[]{:S(2)}) collective-permute-start(bf16[40,1536]{1,0:T(8,128)(2,1)S(1)} %get-tuple-element.17), channel_id=1, source_target_pairs={{0,8},{8,0},{16,24},{24,16},{1,9},{9,1},{17,25},{25,17},{2,10},{10... | collective-permute-start | bytes 368648 | tf_op jit(solution)/shard_map/ppermute | solution.py:9
  156.2 13.3 %collective-permute-start.23 = (bf16[40,1536]{1,0:T(8,128)(2,1)S(1)}, bf16[40,1536]{1,0:T(8,128)(2,1)S(1)}, u32[]{:S(2)}, u32[]{:S(2)}) collective-permute-start(bf16[40,1536]{1,0:T(8,128)(2,1)S(1)} %get-tuple-element.18), channel_id=1, source_target_pairs={{0,24},{8,16},{16,8},{24,0},{1,25},{9,17},{17,9},{25,1},{2,26},{10... | collective-permute-start | bytes 368648 | tf_op jit(solution)/shard_map/ppermute | solution.py:9
  157.7 11.8 %collective-permute-start.22 = (bf16[40,1536]{1,0:T(8,128)(2,1)S(1)}, bf16[40,1536]{1,0:T(8,128)(2,1)S(1)}, u32[]{:S(2)}, u32[]{:S(2)}) collective-permute-start(bf16[40,1536]{1,0:T(8,128)(2,1)S(1)} %get-tuple-element.19), channel_id=1, source_target_pairs={{0,16},{8,24},{16,0},{24,8},{1,17},{9,25},{17,1},{25,9},{2,18},{10... | collective-permute-start | bytes 368648 | tf_op jit(solution)/shard_map/ppermute | solution.py:9
  170.5 1.4 collective-permute-start.24
  (25 other events, 333.9 us)

commit v2 on v1

v2 whole, which is shorter than its diff:
```python
import functools

import jax
import jax.numpy as jnp
from jax import lax
from jax.experimental import pallas as pl
from jax.experimental.pallas import tpu as pltpu
from jax.sharding import PartitionSpec as P

LANES = 128
VMEM_LIMIT = 16 * 1024 * 1024
FETCH_PARTS = 8
LAST = (((1,), (1,)), ((), ()))
FIRST = (((0,), (0,)), ((), ()))


def swap(x, axis, bits):
    size = lax.axis_size(axis)
    return lax.ppermute(x, axis, [(i, i ^ bits) for i in range(size)])


def block_of(extent, most):
    size = most
    while extent % size:
        size -= LANES
    return size


def pick_of(expert_ids, expert, capacity):
    tok_rows = expert_ids.shape[0]
    chosen = (expert_ids == expert).astype(jnp.int32)
    slot_index = (jnp.cumsum(chosen.reshape(-1)) - 1).reshape(tok_rows, 2)
    columns = jnp.arange(capacity, dtype=jnp.int32)
    return (
        (chosen[:, :, None] == 1) & (slot_index[:, :, None] == columns[None, None, :])
    ).astype(jnp.float32)


def fetch_kernel(*refs):
    count = (len(refs) - 1) // 2
    sources, targets, sems = refs[:count], refs[count : 2 * count], refs[-1]
    copies = []
    for m in range(count):
        lines = sources[m].shape[0] // FETCH_PARTS
        for i in range(FETCH_PARTS):
            part = pl.ds(i * lines, lines)
            copies.append(
                pltpu.make_async_copy(sources[m].at[part], targets[m].at[part], sems.at[m, i])
            )
    for copy in copies:
        copy.start()
    for copy in copies:
        copy.wait()


def fetch(*arrays):
    return pl.pallas_call(
        fetch_kernel,
        in_specs=[pl.BlockSpec(memory_space=pl.ANY)] * len(arrays),
        out_specs=[pl.BlockSpec(memory_space=pltpu.VMEM)] * len(arrays),
        out_shape=[pltpu.VMEM(x.shape, x.dtype) for x in arrays],
        scratch_shapes=[pltpu.SemaphoreType.DMA((len(arrays), FETCH_PARTS))],
        compiler_params=pltpu.CompilerParams(vmem_limit_bytes=VMEM_LIMIT),
        name="fetch",
    )(*arrays)


def forward_kernel(
    rows_ref, grads_ref, gate_ref, up_ref, down_ref, hidden_ref, d_gate_ref, d_up_ref, slot_ref,
    gate_acc, up_acc, back_acc,
):
    width = rows_ref.shape[1]
    block = block_of(width, 512)

    def add(i, first):
        lines = pl.ds(pl.multiple_of(i * block, block), block)
        gate = jnp.dot(rows_ref[:, lines], gate_ref[lines, :], preferred_element_type=jnp.float32)
        up = jnp.dot(rows_ref[:, lines], up_ref[lines, :], preferred_element_type=jnp.float32)
        back = lax.dot_general(
            down_ref[:, lines], grads_ref[:, lines], LAST, preferred_element_type=jnp.float32
        )
        if first:
            gate_acc[...] = gate
            up_acc[...] = up
            back_acc[...] = back
        else:
            gate_acc[...] += gate
            up_acc[...] += up
            back_acc[...] += back

    add(0, True)

    @pl.loop(1, width // block)
    def _(i):
        add(i, False)

    back = back_acc[...].T
    gate = gate_acc[...]
    up = up_acc[...]
    sig = jax.nn.sigmoid(gate)
    activated = gate * sig
    hidden = (activated * up).astype(jnp.bfloat16)
    hidden_ref[...] = hidden
    slots = jnp.sum(hidden.astype(jnp.float32) * back, axis=1, keepdims=True)
    slot_ref[...] = jnp.broadcast_to(slots, slot_ref.shape)
    d_gate_ref[...] = (back * up * (sig * (1.0 + gate * (1.0 - sig)))).astype(jnp.bfloat16)
    d_up_ref[...] = (back * activated).astype(jnp.bfloat16)


def forward_step(rows, grads, gate_mat, up_mat, down_mat):
    count, width = rows.shape
    hidden_local = gate_mat.shape[1]
    half = jax.ShapeDtypeStruct((count, hidden_local), jnp.bfloat16)
    acc = pltpu.VMEM((count, hidden_local), jnp.float32)
    return pl.pallas_call(
        forward_kernel,
        in_specs=[pl.BlockSpec(memory_space=pltpu.VMEM)] * 5,
        out_specs=[pl.BlockSpec(memory_space=pltpu.VMEM)] * 4,
        out_shape=[half, half, half, jax.ShapeDtypeStruct((count, LANES), jnp.float32)],
        scratch_shapes=[acc, acc, pltpu.VMEM((hidden_local, count), jnp.float32)],
        compiler_params=pltpu.CompilerParams(vmem_limit_bytes=VMEM_LIMIT),
        name="forward_step",
    )(rows, grads, gate_mat, up_mat, down_mat)


def piece_kernel(piece_ref, d_gate_ref, d_up_ref, slot_ref, gate_ref, up_ref, out_ref):
    piece = out_ref.shape[1] - LANES
    block = block_of(piece, 384)
    for i in range(piece // block):
        lines = pl.ds(pl.multiple_of(piece_ref[0] * piece + i * block, LANES), block)
        part = lax.dot_general(
            gate_ref[lines, :], d_gate_ref[...], LAST, preferred_element_type=jnp.float32
        ) + lax.dot_general(up_ref[lines, :], d_up_ref[...], LAST, preferred_element_type=jnp.float32)
        out_ref[:, i * block : (i + 1) * block] = part.T.astype(out_ref.dtype)
    out_ref[:, piece:] = slot_ref[...].astype(out_ref.dtype)


def row_piece(index, d_gate, d_up, slots, gate_mat, up_mat, piece, dtype):
    rows, hidden_local = d_gate.shape
    return pl.pallas_call(
        piece_kernel,
        in_specs=[pl.BlockSpec(memory_space=pltpu.SMEM)] + [pl.BlockSpec(memory_space=pltpu.VMEM)] * 5,
        out_specs=pl.BlockSpec(memory_space=pltpu.VMEM),
        out_shape=jax.ShapeDtypeStruct((rows, piece + LANES), dtype),
        compiler_params=pltpu.CompilerParams(vmem_limit_bytes=VMEM_LIMIT),
        name="row_piece",
    )(index.reshape(1), d_gate, d_up, slots, gate_mat, up_mat)


def on_device(tokens, out_grad, expert_ids, gate_probs, w_gate, w_up, w_down):
    expert = lax.axis_index("exp")
    hid = lax.axis_index("hid")
    tok_rows, model_width = tokens.shape
    capacity = 5 * tok_rows // 16
    seq_count = lax.axis_size("seq")
    hid_count = lax.axis_size("hid")
    piece = model_width // hid_count
    bf16, f32 = jnp.bfloat16, jnp.float32

    pick_own = pick_of(expert_ids, expert, capacity)
    select_own = jnp.sum(pick_own, axis=1).astype(bf16)
    weight_own = jnp.sum(pick_own * gate_probs[:, :, None], axis=(0, 1))

    def slots_of(x):
        return lax.dot_general(select_own, x, FIRST, preferred_element_type=f32)

    def row_slots(x):
        return slots_of(x).astype(bf16)

    def grad_slots(x):
        return (slots_of(x) * weight_own[:, None]).astype(bf16)

    def quarter(x):
        return lax.dynamic_slice_in_dim(x, hid * piece, piece, axis=1)

    message = jnp.concatenate([row_slots(quarter(tokens)), grad_slots(quarter(out_grad))], axis=0)

    def after(x, done):
        return lax.optimization_barrier((x, done))[0]

    pieces = [[None] * seq_count for _ in range(hid_count)]
    for k in range(seq_count - 1, 0, -1):
        pieces[0][k] = swap(message, "seq", k)
    gate_mat, up_mat, down_mat, _ = after((w_gate[0], w_up[0], w_down[0], 0), message)
    gate_mat, up_mat, down_mat = fetch(gate_mat, up_mat, down_mat)
    pieces[0] = after(pieces[0], gate_mat[:8, :LANES])
    for k in range(seq_count - 1, 0, -1):
        block = pieces[0][k]
        if hid_count == 4:
            one, two = swap(block, "hid", 1), swap(block, "hid", 2)
            pieces[1][k], pieces[2][k] = one, two
            pieces[3][k] = jnp.concatenate(
                [swap(one[:capacity], "hid", 2), swap(two[capacity:], "hid", 1)], axis=0
            )
        else:
            for j in range(1, hid_count):
                pieces[j][k] = swap(block, "hid", j)
    row_pieces = [[x[:capacity] for x in y[1:]] for y in pieces]
    grad_pieces = [[x[capacity:] for x in y[1:]] for y in pieces]

    def whole(own, pieces):
        rest = jnp.zeros(((seq_count - 1) * capacity, model_width), bf16)
        for j in range(hid_count):
            rest = lax.dynamic_update_slice_in_dim(
                rest, jnp.concatenate(pieces[j], axis=0), (hid ^ j) * piece, axis=1
            )
        return jnp.concatenate([own, rest], axis=0)

    rows_e = whole(row_slots(tokens), row_pieces)
    grads_e = whole(grad_slots(out_grad), grad_pieces)

    hidden, d_gate, d_up, slots = forward_step(rows_e, grads_e, gate_mat, up_mat, down_mat)

    received = []
    source = (d_gate, d_up, slots)
    for j in range(hid_count - 1, -1, -1):
        part = row_piece(hid ^ j, *source, gate_mat, up_mat, piece, bf16 if j else f32)
        source = after(source, part)
        if j:
            received.append(swap(part, "hid", j))
    total = part
    hidden, d_gate, d_up = after((hidden, d_gate, d_up), part)
    for part in received:
        total = total + part.astype(f32)
    own_sum = total[:capacity]
    for k in range(1, seq_count):
        lines = slice(k * capacity, (k + 1) * capacity)
        own_sum = own_sum + swap(total[lines].astype(bf16), "seq", k).astype(f32)

    half = own_sum.astype(bf16)
    other_half = swap(half, "exp", 1)
    pick_other = pick_of(expert_ids, 1 - expert, capacity)
    select_other = jnp.sum(pick_other, axis=1).astype(bf16)
    d_tokens = jnp.dot(select_own, half[:, :piece], preferred_element_type=f32) + jnp.dot(
        select_other, other_half[:, :piece], preferred_element_type=f32
    )
    slot_own = own_sum[:, piece]
    slot_other = other_half[:, piece].astype(f32)
    d_gates = (
        jnp.sum(pick_own * slot_own[None, None, :], axis=2)
        + jnp.sum(pick_other * slot_other[None, None, :], axis=2)
    ) / gate_probs

    grad_down = lax.dot_general(hidden, grads_e, FIRST, preferred_element_type=f32).astype(bf16)
    grad_gate = lax.dot_general(rows_e, d_gate, FIRST, preferred_element_type=f32).astype(bf16)
    grad_up = lax.dot_general(rows_e, d_up, FIRST, preferred_element_type=f32).astype(bf16)
    return (grad_gate[None], grad_up[None], grad_down[None], d_tokens, d_gates)


def solution(mesh):
    return jax.shard_map(
        on_device,
        mesh=mesh,
        in_specs=(
            P("seq", None),
            P("seq", None),
            P("seq", None),
            P("seq", None),
            P("exp", None, ("seq", "hid")),
            P("exp", None, ("seq", "hid")),
            P("exp", ("seq", "hid"), None),
        ),
        out_specs=(
            P("exp", None, ("seq", "hid")),
            P("exp", None, ("seq", "hid")),
            P("exp", ("seq", "hid"), None),
            P("seq", "hid"),
            P("seq", None),
        ),
        check_vma=False,
    )
```

time: 174 us -> 124 us (0.71)
  matrix products: 72.5 us -> 23.4 us
  Pallas kernels: 0 us -> 34.8 us
  waiting for transfers between devices: 45.4 us -> 18 us
  starting transfers between devices: 38.7 us -> 29.1 us
  local copies, waits for them, and re-layouts: 8.36 us -> 12.2 us
  other arithmetic: 7.22 us -> 4.7 us
    dot_general x20 -> x9, matrix products: 72.5 us -> 23.4 us  [the longest x1 6.65 us: on_device(): lax.dot_general(rows_e, d_gate, FIRST, preferred_element_type=f32)]
    pallas_call x0 -> x6, Pallas kernels: none -> 34.8 us  [the longest x1 15 us: forward_step(): pl.pallas_call(forward_kernel, in_specs=[pl.BlockSpec(memory_space=pltpu....]
    ppermute x32 -> x22, waiting for transfers between devices: 45.4 us -> 18 us  [swap(): return lax.ppermute(x, axis, [(i, i ^ bits) for i in range(size)])]
    ppermute x32 -> x22, starting transfers between devices: 38.7 us -> 29.1 us  [swap(): return lax.ppermute(x, axis, [(i, i ^ bits) for i in range(size)])]
    unnamed x50 -> x26, local copies, waits for them, and re-layouts: 2.94 us -> 9.68 us
    slice x11, local copies, waits for them, and re-layouts: 2.24 us -> 0.34 us  [the longest x9 0.15 us: on_device(): grad_pieces = [[x[capacity:] for x in y[1:]] for y in pieces]]
  transfers between devices with their start and end apart: 32 -> 22, of which waited for: 15 -> 11; matrix products, arithmetic and copies ran while one was open for 39% -> 18% of each run, Pallas kernels for 0% -> 11%
where the time goes in v2:
time: 124 us; the launch traced here: 123 us
  Pallas kernels  34.8 us (28%)
  starting transfers between devices  29.1 us (23%)
  matrix products  23.4 us (19%)
  waiting for transfers between devices  18 us (15%)
  local copies, waits for them, and re-layouts  12.2 us (10%)
  other arithmetic  4.7 us (4%)
    ppermute x22, starting transfers between devices, swap(): return lax.ppermute(x, axis, [(i, i ^ bits) for i in range(size)])  29.1 us
    ppermute x22, waiting for transfers between devices, swap(): return lax.ppermute(x, axis, [(i, i ^ bits) for i in range(size)])  18 us
    pallas_call x1, Pallas kernels, forward_step(): pl.pallas_call(forward_kernel, in_specs=[pl.BlockSpec(memory_space=pltpu....  15 us
    pallas_call x1, Pallas kernels, fetch(): pl.pallas_call(fetch_kernel, in_specs=[pl.BlockSpec(memory_space=pl.ANY)]...  12 us
    unnamed x26, local copies, waits for them, and re-layouts  9.68 us
    pallas_call x4, Pallas kernels, row_piece(): pl.pallas_call(piece_kernel, in_specs=[pl.BlockSpec(memory_space=pltpu.SM...  7.72 us
    dot_general x1, matrix products, on_device(): lax.dot_general(rows_e, d_gate, FIRST, preferred_element_type=f32)  6.65 us
    dot_general x1, matrix products, on_device(): lax.dot_general(rows_e, d_up, FIRST, preferred_element_type=f32)  6.63 us
  transfers between devices with their start and end apart: 22, of which 11 were waited for; matrix products, arithmetic and copies ran while one was open for 18% of the time, Pallas kernels for 11%

profile of v2, /device:TPU:0, one launch (start us, length us, event | category | flops | bytes accessed | tf_op | source)
XLA Modules:
  0.0 123.3 jit_solution(6632358811602000397)
XLA Ops:
  0.7 1.3 %broadcast_compare_fusion = (pred[128,2]{0,1:T(4,128)(4,1)}, s32[128,2]{0,1:T(2,128)S(1)}, pred[128,2]{0,1:T(4,128)(4,1)S(1)}, s32[128,2]{0,1:T(2,128)S(1)}) fusion(s32[128,2]{0,1:T(2,128)} %param.9, s32[]{:T(128)S(6)} %sub.10, s32[]{:T(128)S(6)} %axis_index.23), kind=kLoop, calls=%fused_computation.51 | loop fusion | flops 1536 | bytes 3592 | tf_op jit(solution)/shard_map/eq | solution.py:35
  6.6 5.1 %collective-permute-start.2 = (bf16[80,1536]{1,0:T(8,128)(2,1)S(1)}, bf16[80,1536]{1,0:T(8,128)(2,1)S(1)}, u32[]{:S(2)}, u32[]{:S(2)}) collective-permute-start(bf16[80,1536]{1,0:T(8,128)(2,1)S(1)} %pad_maximum_fusion.2), channel_id=1, source_target_pairs={{0,24},{8,16},{16,8},{24,0},{1,25},{9,17},{17,9},{25,1},{2,26},{10... | collective-permute-start | bytes 737288 | tf_op jit(solution)/shard_map/ppermute | solution.py:19
  13.6 12.0 %fetch.1 = (bf16[6144,1024]{1,0:T(8,128)(2,1)S(1)}, bf16[6144,1024]{1,0:T(8,128)(2,1)S(1)}, bf16[1024,6144]{1,0:T(8,128)(2,1)S(1)}) custom-call(bf16[6144,1024]{1,0:T(8,128)(2,1)} %bitcast.24, bf16[6144,1024]{1,0:T(8,128)(2,1)} %bitcast.25, bf16[1024,6144]{1,0:T(8,128)(2,1)} %bitcast.26), custom_call_target="tpu_custom_call" | custom-call | tf_op jit(solution)/shard_map/fetch/pallas_call | solution.py:57
  25.6 4.8 %copy-done.2 = bf16[6144,1024]{1,0:T(8,128)(2,1)} copy-done((bf16[6144,1024]{1,0:T(8,128)(2,1)}, bf16[6144,1024]{1,0:T(8,128)(2,1)S(1)}, u32[]{:S(2)}) %copy-start.2) | copy-done | bytes 12582936
  30.4 4.8 %copy-done.4 = bf16[1024,6144]{1,0:T(8,128)(2,1)} copy-done((bf16[1024,6144]{1,0:T(8,128)(2,1)}, bf16[1024,6144]{1,0:T(8,128)(2,1)S(1)}, u32[]{:S(2)}) %copy-start.4) | copy-done | bytes 12582936
  35.2 1.7 %collective-permute-start.6 = (bf16[80,1536]{1,0:T(8,128)(2,1)S(1)}, bf16[80,1536]{1,0:T(8,128)(2,1)S(1)}, u32[]{:S(2)}, u32[]{:S(2)}) collective-permute-start(bf16[80,1536]{1,0:T(8,128)(2,1)S(1)} %collective-permute-done), channel_id=1, source_target_pairs={{0,2},{1,3},{2,0},{3,1},{4,6},{5,7},{6,4},{7,5},{8,10},{9,11},{10,... | collective-permute-start | bytes 737288 | tf_op jit(solution)/shard_map/ppermute | solution.py:19
  36.9 1.5 %collective-permute-start.3 = (bf16[80,1536]{1,0:T(8,128)(2,1)S(1)}, bf16[80,1536]{1,0:T(8,128)(2,1)S(1)}, u32[]{:S(2)}, u32[]{:S(2)}) collective-permute-start(bf16[80,1536]{1,0:T(8,128)(2,1)S(1)} %collective-permute-done), channel_id=1, source_target_pairs={{0,1},{1,0},{2,3},{3,2},{4,5},{5,4},{6,7},{7,6},{8,9},{9,8},{10,11... | collective-permute-start | bytes 737288 | tf_op jit(solution)/shard_map/ppermute | solution.py:19
  39.4 1.8 %collective-permute-start.8 = (bf16[80,1536]{1,0:T(8,128)(2,1)S(1)}, bf16[80,1536]{1,0:T(8,128)(2,1)S(1)}, u32[]{:S(2)}, u32[]{:S(2)}) collective-permute-start(bf16[80,1536]{1,0:T(8,128)(2,1)S(1)} %collective-permute-done.2), channel_id=1, source_target_pairs={{0,2},{1,3},{2,0},{3,1},{4,6},{5,7},{6,4},{7,5},{8,10},{9,11},{10,... | collective-permute-start | bytes 737288 | tf_op jit(solution)/shard_map/ppermute | solution.py:19
  41.6 2.6 %collective-permute-done.6 = bf16[80,1536]{1,0:T(8,128)(2,1)S(1)} collective-permute-done((bf16[80,1536]{1,0:T(8,128)(2,1)S(1)}, bf16[80,1536]{1,0:T(8,128)(2,1)S(1)}, u32[]{:S(2)}, u32[]{:S(2)}) %collective-permute-start.6) | collective-permute-done | bytes 245792 | tf_op jit(solution)/shard_map/ppermute | solution.py:19
  44.2 1.6 %collective-permute-start.5 = (bf16[80,1536]{1,0:T(8,128)(2,1)S(1)}, bf16[80,1536]{1,0:T(8,128)(2,1)S(1)}, u32[]{:S(2)}, u32[]{:S(2)}) collective-permute-start(bf16[80,1536]{1,0:T(8,128)(2,1)S(1)} %collective-permute-done.2), channel_id=1, source_target_pairs={{0,1},{1,0},{2,3},{3,2},{4,5},{5,4},{6,7},{7,6},{8,9},{9,8},{10,11... | collective-permute-start | bytes 737288 | tf_op jit(solution)/shard_map/ppermute | solution.py:19
  45.8 1.5 %collective-permute-start.12 = (bf16[40,1536]{1,0:T(8,128)(2,1)S(1)}, bf16[40,1536]{1,0:T(8,128)(2,1)S(1)}, u32[]{:S(2)}, u32[]{:S(2)}) collective-permute-start(bf16[40,1536]{1,0:T(8,128)(2,1)S(1)} %get-tuple-element.70), channel_id=1, source_target_pairs={{0,1},{1,0},{2,3},{3,2},{4,5},{5,4},{6,7},{7,6},{8,9},{9,8},{10,11... | collective-permute-start | bytes 368648 | tf_op jit(solution)/shard_map/ppermute | solution.py:19
  47.3 2.1 %collective-permute-done.7 = bf16[80,1536]{1,0:T(8,128)(2,1)S(1)} collective-permute-done((bf16[80,1536]{1,0:T(8,128)(2,1)S(1)}, bf16[80,1536]{1,0:T(8,128)(2,1)S(1)}, u32[]{:S(2)}, u32[]{:S(2)}) %collective-permute-start.7) | collective-permute-done | bytes 245792 | tf_op jit(solution)/shard_map/ppermute | solution.py:19
  49.4 1.7 %collective-permute-start.9 = (bf16[40,1536]{1,0:T(8,128)(2,1)S(1)}, bf16[40,1536]{1,0:T(8,128)(2,1)S(1)}, u32[]{:S(2)}, u32[]{:S(2)}) collective-permute-start(bf16[40,1536]{1,0:T(8,128)(2,1)S(1)} %get-tuple-element.77), channel_id=1, source_target_pairs={{0,2},{1,3},{2,0},{3,1},{4,6},{5,7},{6,4},{7,5},{8,10},{9,11},{10,... | collective-permute-start | bytes 368648 | tf_op jit(solution)/shard_map/ppermute | solution.py:19
  51.1 1.6 %collective-permute-start.13 = (bf16[40,1536]{1,0:T(8,128)(2,1)S(1)}, bf16[40,1536]{1,0:T(8,128)(2,1)S(1)}, u32[]{:S(2)}, u32[]{:S(2)}) collective-permute-start(bf16[40,1536]{1,0:T(8,128)(2,1)S(1)} %get-tuple-element.72), channel_id=1, source_target_pairs={{0,1},{1,0},{2,3},{3,2},{4,5},{5,4},{6,7},{7,6},{8,9},{9,8},{10,11... | collective-permute-start | bytes 368648 | tf_op jit(solution)/shard_map/ppermute | solution.py:19
  52.7 1.9 %collective-permute-done.8 = bf16[80,1536]{1,0:T(8,128)(2,1)S(1)} collective-permute-done((bf16[80,1536]{1,0:T(8,128)(2,1)S(1)}, bf16[80,1536]{1,0:T(8,128)(2,1)S(1)}, u32[]{:S(2)}, u32[]{:S(2)}) %collective-permute-start.8) | collective-permute-done | bytes 245792 | tf_op jit(solution)/shard_map/ppermute | solution.py:19
  54.6 1.7 %collective-permute-start.10 = (bf16[40,1536]{1,0:T(8,128)(2,1)S(1)}, bf16[40,1536]{1,0:T(8,128)(2,1)S(1)}, u32[]{:S(2)}, u32[]{:S(2)}) collective-permute-start(bf16[40,1536]{1,0:T(8,128)(2,1)S(1)} %get-tuple-element.79), channel_id=1, source_target_pairs={{0,2},{1,3},{2,0},{3,1},{4,6},{5,7},{6,4},{7,5},{8,10},{9,11},{10,... | collective-permute-start | bytes 368648 | tf_op jit(solution)/shard_map/ppermute | solution.py:19
  56.4 1.5 %collective-permute-start.14 = (bf16[40,1536]{1,0:T(8,128)(2,1)S(1)}, bf16[40,1536]{1,0:T(8,128)(2,1)S(1)}, u32[]{:S(2)}, u32[]{:S(2)}) collective-permute-start(bf16[40,1536]{1,0:T(8,128)(2,1)S(1)} %get-tuple-element.74), channel_id=1, source_target_pairs={{0,1},{1,0},{2,3},{3,2},{4,5},{5,4},{6,7},{7,6},{8,9},{9,8},{10,11... | collective-permute-start | bytes 368648 | tf_op jit(solution)/shard_map/ppermute | solution.py:19
  59.3 1.4 %collective-permute-done.13 = bf16[40,1536]{1,0:T(8,128)(2,1)S(1)} collective-permute-done((bf16[40,1536]{1,0:T(8,128)(2,1)S(1)}, bf16[40,1536]{1,0:T(8,128)(2,1)S(1)}, u32[]{:S(2)}, u32[]{:S(2)}) %collective-permute-start.13) | collective-permute-done | bytes 122912 | tf_op jit(solution)/shard_map/ppermute | solution.py:19
  62.3 1.6 %collective-permute-done.11 = bf16[40,1536]{1,0:T(8,128)(2,1)S(1)} collective-permute-done((bf16[40,1536]{1,0:T(8,128)(2,1)S(1)}, bf16[40,1536]{1,0:T(8,128)(2,1)S(1)}, u32[]{:S(2)}, u32[]{:S(2)}) %collective-permute-start.11) | collective-permute-done | bytes 122912 | tf_op jit(solution)/shard_map/ppermute | solution.py:19
  64.1 15.0 %forward_step.1 = (bf16[160,1024]{1,0:T(8,128)(2,1)S(1)}, bf16[160,1024]{1,0:T(8,128)(2,1)S(1)}, bf16[160,1024]{1,0:T(8,128)(2,1)S(1)}, f32[160,128]{1,0:T(8,128)S(1)}) custom-call(bf16[160,6144]{1,0:T(8,128)(2,1)S(1)} %pad_maximum_fusion.rows_ref, bf16[160,6144]{1,0:T(8,128)(2,1)S(1)} %pad_maximum_fusion.1.grads_ref, bf16[6144,1024]{1,0:T(8,128)(2,1)S(1)} %copy-done.3, ...), custom_call_target="tpu_custom_call" | custom-call | tf_op jit(solution)/shard_map/forward_step/pallas_call | solution.py:115
  79.2 1.9 %row_piece.4 = bf16[160,1664]{1,0:T(8,128)(2,1)S(1)} custom-call(s32[1]{0:T(128)} %bitcast.4.piece_ref, bf16[160,1024]{1,0:T(8,128)(2,1)S(1)} %get-tuple-element.52.d_gate_ref, bf16[160,1024]{1,0:T(8,128)(2,1)S(1)} %get-tuple-element.53.d_up_ref, f32[160,128]{1,0:T(8,128)S(1)} %get-tuple-element.51.slot_ref, bf16[6144,1024]{1,0:T(8,128)(2,1)S(1)} %copy-done.3, ...), custom_call_target="tpu_custom_call" | custom-call | tf_op jit(solution)/shard_map/row_piece/pallas_call | solution.py:140
  81.1 1.9 %row_piece.5 = bf16[160,1664]{1,0:T(8,128)(2,1)S(1)} custom-call(s32[1]{0:T(128)} %bitcast.5.piece_ref, bf16[160,1024]{1,0:T(8,128)(2,1)S(1)} %get-tuple-element.52.d_gate_ref, bf16[160,1024]{1,0:T(8,128)(2,1)S(1)} %get-tuple-element.53.d_up_ref, f32[160,128]{1,0:T(8,128)S(1)} %get-tuple-element.51.slot_ref, bf16[6144,1024]{1,0:T(8,128)(2,1)S(1)} %copy-done.3, ...), custom_call_target="tpu_custom_call" | custom-call | tf_op jit(solution)/shard_map/row_piece/pallas_call | solution.py:140
  83.0 1.9 %row_piece.6 = bf16[160,1664]{1,0:T(8,128)(2,1)S(1)} custom-call(s32[1]{0:T(128)} %bitcast.6.piece_ref, bf16[160,1024]{1,0:T(8,128)(2,1)S(1)} %get-tuple-element.52.d_gate_ref, bf16[160,1024]{1,0:T(8,128)(2,1)S(1)} %get-tuple-element.53.d_up_ref, f32[160,128]{1,0:T(8,128)S(1)} %get-tuple-element.51.slot_ref, bf16[6144,1024]{1,0:T(8,128)(2,1)S(1)} %copy-done.3, ...), custom_call_target="tpu_custom_call" | custom-call | tf_op jit(solution)/shard_map/row_piece/pallas_call | solution.py:140
  84.9 1.5 %collective-permute-start.17 = (bf16[160,1664]{1,0:T(8,128)(2,1)S(1)}, bf16[160,1664]{1,0:T(8,128)(2,1)S(1)}, u32[]{:S(2)}, u32[]{:S(2)}) collective-permute-start(bf16[160,1664]{1,0:T(8,128)(2,1)S(1)} %row_piece.6), channel_id=1, source_target_pairs={{0,1},{1,0},{2,3},{3,2},{4,5},{5,4},{6,7},{7,6},{8,9},{9,8},{10,11... | collective-permute-start | bytes 1597448 | tf_op jit(solution)/shard_map/ppermute | solution.py:19
  87.0 1.5 %collective-permute-start.15 = (bf16[160,1664]{1,0:T(8,128)(2,1)S(1)}, bf16[160,1664]{1,0:T(8,128)(2,1)S(1)}, u32[]{:S(2)}, u32[]{:S(2)}) collective-permute-start(bf16[160,1664]{1,0:T(8,128)(2,1)S(1)} %row_piece.4), channel_id=1, source_target_pairs={{0,3},{1,2},{2,1},{3,0},{4,7},{5,6},{6,5},{7,4},{8,11},{9,10},{10,... | collective-permute-start | bytes 1597448 | tf_op jit(solution)/shard_map/ppermute | solution.py:19
  88.5 2.0 %row_piece.7 = f32[160,1664]{1,0:T(8,128)S(1)} custom-call(s32[1]{0:T(128)} %bitcast.3.piece_ref, bf16[160,1024]{1,0:T(8,128)(2,1)S(1)} %get-tuple-element.52.d_gate_ref, bf16[160,1024]{1,0:T(8,128)(2,1)S(1)} %get-tuple-element.53.d_up_ref, f32[160,128]{1,0:T(8,128)S(1)} %get-tuple-element.51.slot_ref, bf16[6144,1024]{1,0:T(8,128)(2,1)S(1)} %copy-done.3, ...), custom_call_target="tpu_custom_call" | custom-call | tf_op jit(solution)/shard_map/row_piece/pallas_call | solution.py:140
  90.5 6.6 %convert_bitcast_fusion.2 = bf16[1,6144,1024]{2,1,0:T(8,128)(2,1)} fusion(bf16[160,1024]{1,0:T(8,128)(2,1)S(1)} %get-tuple-element.52.d_gate_ref, bf16[120,6144]{1,0:T(8,128)(2,1)S(1)} %maximum_dynamic-update-slice_fusion.3, bf16[40,6144]{1,0:T(8,128)(2,1)S(1)} %convolution_convert_fusion), kind=kOutput, calls=%fused_computation.2 | convolution fusion | flops 2023489536 | bytes 14876672 | tf_op jit(solution)/shard_map/dot_general | solution.py:245
  97.1 6.6 %convert_bitcast_fusion.1 = bf16[1,6144,1024]{2,1,0:T(8,128)(2,1)} fusion(bf16[160,1024]{1,0:T(8,128)(2,1)S(1)} %get-tuple-element.53.d_up_ref, bf16[120,6144]{1,0:T(8,128)(2,1)S(1)} %maximum_dynamic-update-slice_fusion.3, bf16[40,6144]{1,0:T(8,128)(2,1)S(1)} %convolution_convert_fusion), kind=kOutput, calls=%fused_computation.1 | convolution fusion | flops 2023489536 | bytes 14876672 | tf_op jit(solution)/shard_map/dot_general | solution.py:246
  103.7 4.2 %collective-permute-done.16 = bf16[160,1664]{1,0:T(8,128)(2,1)S(1)} collective-permute-done((bf16[160,1664]{1,0:T(8,128)(2,1)S(1)}, bf16[160,1664]{1,0:T(8,128)(2,1)S(1)}, u32[]{:S(2)}, u32[]{:S(2)}) %collective-permute-start.16) | collective-permute-done | bytes 532512 | tf_op jit(solution)/shard_map/ppermute | solution.py:19
  108.3 1.6 %collective-permute-start.18 = (bf16[40,1664]{1,0:T(8,128)(2,1)S(1)}, bf16[40,1664]{1,0:T(8,128)(2,1)S(1)}, u32[]{:S(2)}, u32[]{:S(2)}) collective-permute-start(bf16[40,1664]{1,0:T(8,128)(2,1)S(1)} %get-tuple-element.67), channel_id=1, source_target_pairs={{0,8},{8,0},{16,24},{24,16},{1,9},{9,1},{17,25},{25,17},{2,10},{10... | collective-permute-start | bytes 399368 | tf_op jit(solution)/shard_map/ppermute | solution.py:19
  109.9 2.4 %collective-permute-start.20 = (bf16[40,1664]{1,0:T(8,128)(2,1)S(1)}, bf16[40,1664]{1,0:T(8,128)(2,1)S(1)}, u32[]{:S(2)}, u32[]{:S(2)}) collective-permute-start(bf16[40,1664]{1,0:T(8,128)(2,1)S(1)} %get-tuple-element.68), channel_id=1, source_target_pairs={{0,24},{8,16},{16,8},{24,0},{1,25},{9,17},{17,9},{25,1},{2,26},{10... | collective-permute-start | bytes 399368 | tf_op jit(solution)/shard_map/ppermute | solution.py:19
  112.3 6.6 %convert_bitcast_fusion = bf16[1,1024,6144]{2,1,0:T(8,128)(2,1)} fusion(bf16[160,1024]{1,0:T(8,128)(2,1)S(1)} %get-tuple-element.54, bf16[120,6144]{1,0:T(8,128)(2,1)S(1)} %maximum_dynamic-update-slice_fusion.7, bf16[40,6144]{1,0:T(8,128)(2,1)S(1)} %fusion), kind=kOutput, calls=%fused_computation | convolution fusion | flops 2023489536 | bytes 14876672 | tf_op jit(solution)/shard_map/dot_general | solution.py:244
  (106 shorter events, 16.4 us)
Async XLA Ops:
  0.6 5.8 %copy-start = (bf16[128,6144]{1,0:T(8,128)(2,1)S(1)}, bf16[128,6144]{1,0:T(8,128)(2,1)}, u32[]{:S(2)}) copy-start(bf16[128,6144]{1,0:T(8,128)(2,1)} %param.8) | copy-start | bytes 4718596
  2.0 9.8 %copy-start.8 = (pred[128,2]{0,1:T(4,128)(4,1)}, pred[128,2]{0,1:T(4,128)(4,1)S(1)}, u32[]{:S(2)}) copy-start(pred[128,2]{0,1:T(4,128)(4,1)S(1)} %get-tuple-element.88) | copy-start | bytes 772
  6.4 6.4 %copy-start.5 = (bf16[128,6144]{1,0:T(8,128)(2,1)S(1)}, bf16[128,6144]{1,0:T(8,128)(2,1)}, u32[]{:S(2)}) copy-start(bf16[128,6144]{1,0:T(8,128)(2,1)} %param.7) | copy-start | bytes 4718596
  6.6 28.5 %collective-permute-start.2 = (bf16[80,1536]{1,0:T(8,128)(2,1)S(1)}, bf16[80,1536]{1,0:T(8,128)(2,1)S(1)}, u32[]{:S(2)}, u32[]{:S(2)}) collective-permute-start(bf16[80,1536]{1,0:T(8,128)(2,1)S(1)} %pad_maximum_fusion.2), channel_id=1, source_target_pairs={{0,24},{8,16},{16,8},{24,0},{1,25},{9,17},{17,9},{25,1},{2,26},{10... | collective-permute-start | bytes 737288 | tf_op jit(solution)/shard_map/ppermute | solution.py:19
  11.8 23.4 %collective-permute-start.1 = (bf16[80,1536]{1,0:T(8,128)(2,1)S(1)}, bf16[80,1536]{1,0:T(8,128)(2,1)S(1)}, u32[]{:S(2)}, u32[]{:S(2)}) collective-permute-start(bf16[80,1536]{1,0:T(8,128)(2,1)S(1)} %pad_maximum_fusion.2), channel_id=1, source_target_pairs={{0,16},{8,24},{16,0},{24,8},{1,17},{9,25},{17,1},{25,9},{2,18},{10... | collective-permute-start | bytes 737288 | tf_op jit(solution)/shard_map/ppermute | solution.py:19
  11.8 23.4 %collective-permute-start = (bf16[80,1536]{1,0:T(8,128)(2,1)S(1)}, bf16[80,1536]{1,0:T(8,128)(2,1)S(1)}, u32[]{:S(2)}, u32[]{:S(2)}) collective-permute-start(bf16[80,1536]{1,0:T(8,128)(2,1)S(1)} %pad_maximum_fusion.2), channel_id=1, source_target_pairs={{0,8},{8,0},{16,24},{24,16},{1,9},{9,1},{17,25},{25,17},{2,10},{10... | collective-permute-start | bytes 737288 | tf_op jit(solution)/shard_map/ppermute | solution.py:19
  25.6 4.8 %copy-start.2 = (bf16[6144,1024]{1,0:T(8,128)(2,1)}, bf16[6144,1024]{1,0:T(8,128)(2,1)S(1)}, u32[]{:S(2)}) copy-start(bf16[6144,1024]{1,0:T(8,128)(2,1)S(1)} %get-tuple-element.36.gate_ref) | copy-start | bytes 37748740
  30.4 4.8 %copy-start.4 = (bf16[1024,6144]{1,0:T(8,128)(2,1)}, bf16[1024,6144]{1,0:T(8,128)(2,1)S(1)}, u32[]{:S(2)}) copy-start(bf16[1024,6144]{1,0:T(8,128)(2,1)S(1)} %get-tuple-element.38.down_ref) | copy-start | bytes 37748740
  35.2 9.0 %collective-permute-start.6 = (bf16[80,1536]{1,0:T(8,128)(2,1)S(1)}, bf16[80,1536]{1,0:T(8,128)(2,1)S(1)}, u32[]{:S(2)}, u32[]{:S(2)}) collective-permute-start(bf16[80,1536]{1,0:T(8,128)(2,1)S(1)} %collective-permute-done), channel_id=1, source_target_pairs={{0,2},{1,3},{2,0},{3,1},{4,6},{5,7},{6,4},{7,5},{8,10},{9,11},{10,... | collective-permute-start | bytes 737288 | tf_op jit(solution)/shard_map/ppermute | solution.py:19
  36.9 8.9 %collective-permute-start.3 = (bf16[80,1536]{1,0:T(8,128)(2,1)S(1)}, bf16[80,1536]{1,0:T(8,128)(2,1)S(1)}, u32[]{:S(2)}, u32[]{:S(2)}) collective-permute-start(bf16[80,1536]{1,0:T(8,128)(2,1)S(1)} %collective-permute-done), channel_id=1, source_target_pairs={{0,1},{1,0},{2,3},{3,2},{4,5},{5,4},{6,7},{7,6},{8,9},{9,8},{10,11... | collective-permute-start | bytes 737288 | tf_op jit(solution)/shard_map/ppermute | solution.py:19
  38.4 11.0 %collective-permute-start.7 = (bf16[80,1536]{1,0:T(8,128)(2,1)S(1)}, bf16[80,1536]{1,0:T(8,128)(2,1)S(1)}, u32[]{:S(2)}, u32[]{:S(2)}) collective-permute-start(bf16[80,1536]{1,0:T(8,128)(2,1)S(1)} %collective-permute-done.1), channel_id=1, source_target_pairs={{0,2},{1,3},{2,0},{3,1},{4,6},{5,7},{6,4},{7,5},{8,10},{9,11},{10,... | collective-permute-start | bytes 737288 | tf_op jit(solution)/shard_map/ppermute | solution.py:19
  39.0 12.1 %collective-permute-start.4 = (bf16[80,1536]{1,0:T(8,128)(2,1)S(1)}, bf16[80,1536]{1,0:T(8,128)(2,1)S(1)}, u32[]{:S(2)}, u32[]{:S(2)}) collective-permute-start(bf16[80,1536]{1,0:T(8,128)(2,1)S(1)} %collective-permute-done.1), channel_id=1, source_target_pairs={{0,1},{1,0},{2,3},{3,2},{4,5},{5,4},{6,7},{7,6},{8,9},{9,8},{10,11... | collective-permute-start | bytes 737288 | tf_op jit(solution)/shard_map/ppermute | solution.py:19
  39.4 15.1 %collective-permute-start.8 = (bf16[80,1536]{1,0:T(8,128)(2,1)S(1)}, bf16[80,1536]{1,0:T(8,128)(2,1)S(1)}, u32[]{:S(2)}, u32[]{:S(2)}) collective-permute-start(bf16[80,1536]{1,0:T(8,128)(2,1)S(1)} %collective-permute-done.2), channel_id=1, source_target_pairs={{0,2},{1,3},{2,0},{3,1},{4,6},{5,7},{6,4},{7,5},{8,10},{9,11},{10,... | collective-permute-start | bytes 737288 | tf_op jit(solution)/shard_map/ppermute | solution.py:19
  44.2 12.2 %collective-permute-start.5 = (bf16[80,1536]{1,0:T(8,128)(2,1)S(1)}, bf16[80,1536]{1,0:T(8,128)(2,1)S(1)}, u32[]{:S(2)}, u32[]{:S(2)}) collective-permute-start(bf16[80,1536]{1,0:T(8,128)(2,1)S(1)} %collective-permute-done.2), channel_id=1, source_target_pairs={{0,1},{1,0},{2,3},{3,2},{4,5},{5,4},{6,7},{7,6},{8,9},{9,8},{10,11... | collective-permute-start | bytes 737288 | tf_op jit(solution)/shard_map/ppermute | solution.py:19
  45.8 13.2 %collective-permute-start.12 = (bf16[40,1536]{1,0:T(8,128)(2,1)S(1)}, bf16[40,1536]{1,0:T(8,128)(2,1)S(1)}, u32[]{:S(2)}, u32[]{:S(2)}) collective-permute-start(bf16[40,1536]{1,0:T(8,128)(2,1)S(1)} %get-tuple-element.70), channel_id=1, source_target_pairs={{0,1},{1,0},{2,3},{3,2},{4,5},{5,4},{6,7},{7,6},{8,9},{9,8},{10,11... | collective-permute-start | bytes 368648 | tf_op jit(solution)/shard_map/ppermute | solution.py:19
  49.4 12.8 %collective-permute-start.9 = (bf16[40,1536]{1,0:T(8,128)(2,1)S(1)}, bf16[40,1536]{1,0:T(8,128)(2,1)S(1)}, u32[]{:S(2)}, u32[]{:S(2)}) collective-permute-start(bf16[40,1536]{1,0:T(8,128)(2,1)S(1)} %get-tuple-element.77), channel_id=1, source_target_pairs={{0,2},{1,3},{2,0},{3,1},{4,6},{5,7},{6,4},{7,5},{8,10},{9,11},{10,... | collective-permute-start | bytes 368648 | tf_op jit(solution)/shard_map/ppermute | solution.py:19
  51.1 9.6 %collective-permute-start.13 = (bf16[40,1536]{1,0:T(8,128)(2,1)S(1)}, bf16[40,1536]{1,0:T(8,128)(2,1)S(1)}, u32[]{:S(2)}, u32[]{:S(2)}) collective-permute-start(bf16[40,1536]{1,0:T(8,128)(2,1)S(1)} %get-tuple-element.72), channel_id=1, source_target_pairs={{0,1},{1,0},{2,3},{3,2},{4,5},{5,4},{6,7},{7,6},{8,9},{9,8},{10,11... | collective-permute-start | bytes 368648 | tf_op jit(solution)/shard_map/ppermute | solution.py:19
  54.6 7.7 %collective-permute-start.10 = (bf16[40,1536]{1,0:T(8,128)(2,1)S(1)}, bf16[40,1536]{1,0:T(8,128)(2,1)S(1)}, u32[]{:S(2)}, u32[]{:S(2)}) collective-permute-start(bf16[40,1536]{1,0:T(8,128)(2,1)S(1)} %get-tuple-element.79), channel_id=1, source_target_pairs={{0,2},{1,3},{2,0},{3,1},{4,6},{5,7},{6,4},{7,5},{8,10},{9,11},{10,... | collective-permute-start | bytes 368648 | tf_op jit(solution)/shard_map/ppermute | solution.py:19
  56.4 5.7 %collective-permute-start.14 = (bf16[40,1536]{1,0:T(8,128)(2,1)S(1)}, bf16[40,1536]{1,0:T(8,128)(2,1)S(1)}, u32[]{:S(2)}, u32[]{:S(2)}) collective-permute-start(bf16[40,1536]{1,0:T(8,128)(2,1)S(1)} %get-tuple-element.74), channel_id=1, source_target_pairs={{0,1},{1,0},{2,3},{3,2},{4,5},{5,4},{6,7},{7,6},{8,9},{9,8},{10,11... | collective-permute-start | bytes 368648 | tf_op jit(solution)/shard_map/ppermute | solution.py:19
  57.8 6.3 %copy-start.3 = (bf16[6144,1024]{1,0:T(8,128)(2,1)S(1)}, bf16[6144,1024]{1,0:T(8,128)(2,1)}, u32[]{:S(2)}) copy-start(bf16[6144,1024]{1,0:T(8,128)(2,1)} %copy-done.2) | copy-start | bytes 37748740
  59.0 4.9 %collective-permute-start.11 = (bf16[40,1536]{1,0:T(8,128)(2,1)S(1)}, bf16[40,1536]{1,0:T(8,128)(2,1)S(1)}, u32[]{:S(2)}, u32[]{:S(2)}) collective-permute-start(bf16[40,1536]{1,0:T(8,128)(2,1)S(1)} %get-tuple-element.81), channel_id=1, source_target_pairs={{0,2},{1,3},{2,0},{3,1},{4,6},{5,7},{6,4},{7,5},{8,10},{9,11},{10,... | collective-permute-start | bytes 368648 | tf_op jit(solution)/shard_map/ppermute | solution.py:19
  84.9 18.8 %collective-permute-start.17 = (bf16[160,1664]{1,0:T(8,128)(2,1)S(1)}, bf16[160,1664]{1,0:T(8,128)(2,1)S(1)}, u32[]{:S(2)}, u32[]{:S(2)}) collective-permute-start(bf16[160,1664]{1,0:T(8,128)(2,1)S(1)} %row_piece.6), channel_id=1, source_target_pairs={{0,1},{1,0},{2,3},{3,2},{4,5},{5,4},{6,7},{7,6},{8,9},{9,8},{10,11... | collective-permute-start | bytes 1597448 | tf_op jit(solution)/shard_map/ppermute | solution.py:19
  86.5 21.5 %collective-permute-start.16 = (bf16[160,1664]{1,0:T(8,128)(2,1)S(1)}, bf16[160,1664]{1,0:T(8,128)(2,1)S(1)}, u32[]{:S(2)}, u32[]{:S(2)}) collective-permute-start(bf16[160,1664]{1,0:T(8,128)(2,1)S(1)} %row_piece.5), channel_id=1, source_target_pairs={{0,2},{1,3},{2,0},{3,1},{4,6},{5,7},{6,4},{7,5},{8,10},{9,11},{10,... | collective-permute-start | bytes 1597448 | tf_op jit(solution)/shard_map/ppermute | solution.py:19
  87.0 21.0 %collective-permute-start.15 = (bf16[160,1664]{1,0:T(8,128)(2,1)S(1)}, bf16[160,1664]{1,0:T(8,128)(2,1)S(1)}, u32[]{:S(2)}, u32[]{:S(2)}) collective-permute-start(bf16[160,1664]{1,0:T(8,128)(2,1)S(1)} %row_piece.4), channel_id=1, source_target_pairs={{0,3},{1,2},{2,1},{3,0},{4,7},{5,6},{6,5},{7,4},{8,11},{9,10},{10,... | collective-permute-start | bytes 1597448 | tf_op jit(solution)/shard_map/ppermute | solution.py:19
  108.3 10.6 %collective-permute-start.18 = (bf16[40,1664]{1,0:T(8,128)(2,1)S(1)}, bf16[40,1664]{1,0:T(8,128)(2,1)S(1)}, u32[]{:S(2)}, u32[]{:S(2)}) collective-permute-start(bf16[40,1664]{1,0:T(8,128)(2,1)S(1)} %get-tuple-element.67), channel_id=1, source_target_pairs={{0,8},{8,0},{16,24},{24,16},{1,9},{9,1},{17,25},{25,17},{2,10},{10... | collective-permute-start | bytes 399368 | tf_op jit(solution)/shard_map/ppermute | solution.py:19
  109.9 9.1 %collective-permute-start.20 = (bf16[40,1664]{1,0:T(8,128)(2,1)S(1)}, bf16[40,1664]{1,0:T(8,128)(2,1)S(1)}, u32[]{:S(2)}, u32[]{:S(2)}) collective-permute-start(bf16[40,1664]{1,0:T(8,128)(2,1)S(1)} %get-tuple-element.68), channel_id=1, source_target_pairs={{0,24},{8,16},{16,8},{24,0},{1,25},{9,17},{17,9},{25,1},{2,26},{10... | collective-permute-start | bytes 399368 | tf_op jit(solution)/shard_map/ppermute | solution.py:19
  112.3 7.6 %copy-start.7 = (s32[128,2]{0,1:T(2,128)S(1)}, s32[128,2]{0,1:T(2,128)}, u32[]{:S(2)}) copy-start(s32[128,2]{0,1:T(2,128)} %copy-done.6) | copy-start | bytes 3076
  112.3 7.6 %copy-start.9 = (pred[128,2]{0,1:T(4,128)(4,1)S(1)}, pred[128,2]{0,1:T(4,128)(4,1)}, u32[]{:S(2)}) copy-start(pred[128,2]{0,1:T(4,128)(4,1)} %copy-done.8) | copy-start | bytes 772
  112.3 8.9 %copy-start.11 = (pred[128,2]{0,1:T(4,128)(4,1)S(1)}, pred[128,2]{0,1:T(4,128)(4,1)}, u32[]{:S(2)}) copy-start(pred[128,2]{0,1:T(4,128)(4,1)} %get-tuple-element.59) | copy-start | bytes 772
  112.3 7.3 %collective-permute-start.19 = (bf16[40,1664]{1,0:T(8,128)(2,1)S(1)}, bf16[40,1664]{1,0:T(8,128)(2,1)S(1)}, u32[]{:S(2)}, u32[]{:S(2)}) collective-permute-start(bf16[40,1664]{1,0:T(8,128)(2,1)S(1)} %get-tuple-element.69), channel_id=1, source_target_pairs={{0,16},{8,24},{16,0},{24,8},{1,17},{9,25},{17,1},{25,9},{2,18},{10... | collective-permute-start | bytes 399368 | tf_op jit(solution)/shard_map/ppermute | solution.py:19
  119.6 3.8 %copy-start.1 = (bf16[128,6144]{1,0:T(8,128)(2,1)S(1)}, bf16[128,6144]{1,0:T(8,128)(2,1)}, u32[]{:S(2)}) copy-start(bf16[128,6144]{1,0:T(8,128)(2,1)} %param.8) | copy-start | bytes 4718596
  119.7 1.4 %collective-permute-start.21 = (bf16[40,1664]{1,0:T(8,128)(2,1)S(1)}, bf16[40,1664]{1,0:T(8,128)(2,1)S(1)}, u32[]{:S(2)}, u32[]{:S(2)}) collective-permute-start(bf16[40,1664]{1,0:T(8,128)(2,1)S(1)} %get-tuple-element.61), channel_id=1, source_target_pairs={{0,4},{4,0},{1,5},{5,1},{2,6},{6,2},{3,7},{7,3},{8,12},{12,8},{9,1... | collective-permute-start | bytes 399368 | tf_op jit(solution)/shard_map/ppermute | solution.py:19
  (3 other events, 6.0 us)

commit v3 on v2

--- a/solution.py
+++ b/solution.py
@@ -1,3 +1,5 @@
+import functools
+
 import functools
 
 import jax
@@ -8,7 +10,7 @@
 from jax.sharding import PartitionSpec as P
 
 LANES = 128
-VMEM_LIMIT = 16 * 1024 * 1024
+VMEM_LIMIT = 8 * 1024 * 1024
 FETCH_PARTS = 8
 LAST = (((1,), (1,)), ((), ()))
 FIRST = (((0,), (0,)), ((), ()))
@@ -56,47 +58,85 @@
 def fetch(*arrays):
     return pl.pallas_call(
         fetch_kernel,
-        in_specs=[pl.BlockSpec(memory_space=pl.ANY)] * len(arrays),
+        in_specs=[pl.BlockSpec(memory_space=pltpu.HBM)] * len(arrays),
         out_specs=[pl.BlockSpec(memory_space=pltpu.VMEM)] * len(arrays),
         out_shape=[pltpu.VMEM(x.shape, x.dtype) for x in arrays],
         scratch_shapes=[pltpu.SemaphoreType.DMA((len(arrays), FETCH_PARTS))],
         compiler_params=pltpu.CompilerParams(vmem_limit_bytes=VMEM_LIMIT),
         name="fetch",
-    )(*arrays)
-
-
-def forward_kernel(
-    rows_ref, grads_ref, gate_ref, up_ref, down_ref, hidden_ref, d_gate_ref, d_up_ref, slot_ref,
-    gate_acc, up_acc, back_acc,
-):
-    width = rows_ref.shape[1]
-    block = block_of(width, 512)
-
-    def add(i, first):
-        lines = pl.ds(pl.multiple_of(i * block, block), block)
-        gate = jnp.dot(rows_ref[:, lines], gate_ref[lines, :], preferred_element_type=jnp.float32)
-        up = jnp.dot(rows_ref[:, lines], up_ref[lines, :], preferred_element_type=jnp.float32)
-        back = lax.dot_general(
-            down_ref[:, lines], grads_ref[:, lines], LAST, preferred_element_type=jnp.float32
+    )(*(pltpu.with_memory_space_constraint(x, pltpu.HBM) for x in arrays))
+
+
+def columns_kernel(index_ref, source_ref, *refs):
+    targets, sems = refs[:-1], refs[-1]
+    height, width = targets[0].shape
+    lines = height // FETCH_PARTS
+    copies = []
+    for j, target in enumerate(targets):
+        start = pl.multiple_of((index_ref[0] ^ j) * width, LANES)
+        for i in range(FETCH_PARTS):
+            part = pl.ds(i * lines, lines)
+            copies.append(
+                pltpu.make_async_copy(
+                    source_ref.at[part, pl.ds(start, width)], target.at[part], sems.at[j, i]
+                )
+            )
+    for copy in copies:
+        copy.start()
+    for copy in copies:
+        copy.wait()
+
+
+def fetch_columns(index, array, count):
+    height, width = array.shape[0], array.shape[1] // count
+    return pl.pallas_call(
+        columns_kernel,
+        in_specs=[
+            pl.BlockSpec(memory_space=pltpu.SMEM),
+            pl.BlockSpec(memory_space=pltpu.HBM),
+        ],
+        out_specs=[pl.BlockSpec(memory_space=pltpu.VMEM)] * count,
+        out_shape=[pltpu.VMEM((height, width), array.dtype)] * count,
+        scratch_shapes=[pltpu.SemaphoreType.DMA((count, FETCH_PARTS))],
+        compiler_params=pltpu.CompilerParams(vmem_limit_bytes=VMEM_LIMIT),
+        name="fetch_columns",
+    )(index.reshape(1), pltpu.with_memory_space_constraint(array, pltpu.HBM))
+
+
+def pair_kernel(first, index_ref, rows_ref, gate_ref, up_ref, *refs):
+    piece = rows_ref.shape[1]
+    block = block_of(piece, 512)
+    gate_out, up_out = refs[-2:]
+    gate, up = (None, None) if first else (refs[0][...], refs[1][...])
+    for i in range(piece // block):
+        lines = pl.ds(pl.multiple_of(index_ref[0] * piece + i * block, LANES), block)
+        rows = rows_ref[:, i * block : (i + 1) * block]
+        more_gate = jnp.dot(rows, gate_ref[lines, :], preferred_element_type=jnp.float32)
+        more_up = jnp.dot(rows, up_ref[lines, :], preferred_element_type=jnp.float32)
+        gate = more_gate if gate is None else gate + more_gate
+        up = more_up if up is None else up + more_up
+    gate_out[...] = gate
+    up_out[...] = up
+
+
+def back_kernel(first, last, grads_ref, down_ref, *refs):
+    piece = grads_ref.shape[1]
+    block = block_of(piece, 512)
+    back = None if first else refs[0][...]
+    for i in range(piece // block):
+        lines = slice(i * block, (i + 1) * block)
+        grads = grads_ref[:, lines]
+        more = lax.dot_general(
+            down_ref[:, lines], grads, LAST, preferred_element_type=jnp.float32
         )
-        if first:
-            gate_acc[...] = gate
-            up_acc[...] = up
-            back_acc[...] = back
-        else:
-            gate_acc[...] += gate
-            up_acc[...] += up
-            back_acc[...] += back
-
-    add(0, True)
-
-    @pl.loop(1, width // block)
-    def _(i):
-        add(i, False)
-
-    back = back_acc[...].T
-    gate = gate_acc[...]
-    up = up_acc[...]
+        back = more if back is None else back + more
+    if not last:
+        refs[-1][...] = back
+        return
+    gate_ref, up_ref, hidden_ref, d_gate_ref, d_up_ref, slot_ref = refs[-6:]
+    back = back.T
+    gate = gate_ref[...]
+    up = up_ref[...]
     sig = jax.nn.sigmoid(gate)
     activated = gate * sig
     hidden = (activated * up).astype(jnp.bfloat16)
@@ -107,20 +147,34 @@
     d_up_ref[...] = (back * activated).astype(jnp.bfloat16)
 
 
-def forward_step(rows, grads, gate_mat, up_mat, down_mat):
-    count, width = rows.shape
-    hidden_local = gate_mat.shape[1]
-    half = jax.ShapeDtypeStruct((count, hidden_local), jnp.bfloat16)
-    acc = pltpu.VMEM((count, hidden_local), jnp.float32)
+def whole_call(kernel, name, outs, index, *arrays):
+    scalars = [] if index is None else [index.reshape(1)]
     return pl.pallas_call(
-        forward_kernel,
-        in_specs=[pl.BlockSpec(memory_space=pltpu.VMEM)] * 5,
-        out_specs=[pl.BlockSpec(memory_space=pltpu.VMEM)] * 4,
-        out_shape=[half, half, half, jax.ShapeDtypeStruct((count, LANES), jnp.float32)],
-        scratch_shapes=[acc, acc, pltpu.VMEM((hidden_local, count), jnp.float32)],
+        kernel,
+        in_specs=[pl.BlockSpec(memory_space=pltpu.SMEM)] * len(scalars)
+        + [pl.BlockSpec(memory_space=pltpu.VMEM)] * len(arrays),
+        out_specs=[pl.BlockSpec(memory_space=pltpu.VMEM)] * len(outs),
+        out_shape=[jax.ShapeDtypeStruct(*x) for x in outs],
         compiler_params=pltpu.CompilerParams(vmem_limit_bytes=VMEM_LIMIT),
-        name="forward_step",
-    )(rows, grads, gate_mat, up_mat, down_mat)
+        name=name,
+    )(*scalars, *arrays)
+
+
+def pair_step(index, rows, gate_mat, up_mat, acc):
+    shape = ((rows.shape[0], gate_mat.shape[1]), jnp.float32)
+    kernel = functools.partial(pair_kernel, not acc)
+    return whole_call(kernel, "pair_step", [shape, shape], index, rows, gate_mat, up_mat, *acc)
+
+
+def back_step(grads, down_mat, acc, last):
+    rows, hidden_local = grads.shape[0], down_mat.shape[0]
+    half = ((rows, hidden_local), jnp.bfloat16)
+    if last:
+        outs = [half, half, half, ((rows, LANES), jnp.float32)]
+    else:
+        outs = [((hidden_local, rows), jnp.float32)]
+    kernel = functools.partial(back_kernel, not acc, bool(last))
+    return whole_call(kernel, "back_step", outs, None, grads, down_mat, *acc, *last)
 
 
 def piece_kernel(piece_ref, d_gate_ref, d_up_ref, slot_ref, gate_ref, up_ref, out_ref):
@@ -173,43 +227,76 @@
     def quarter(x):
         return lax.dynamic_slice_in_dim(x, hid * piece, piece, axis=1)
 
-    message = jnp.concatenate([row_slots(quarter(tokens)), grad_slots(quarter(out_grad))], axis=0)
-
     def after(x, done):
         return lax.optimization_barrier((x, done))[0]
 
-    pieces = [[None] * seq_count for _ in range(hid_count)]
-    for k in range(seq_count - 1, 0, -1):
-        pieces[0][k] = swap(message, "seq", k)
-    gate_mat, up_mat, down_mat, _ = after((w_gate[0], w_up[0], w_down[0], 0), message)
-    gate_mat, up_mat, down_mat = fetch(gate_mat, up_mat, down_mat)
-    pieces[0] = after(pieces[0], gate_mat[:8, :LANES])
-    for k in range(seq_count - 1, 0, -1):
-        block = pieces[0][k]
-        if hid_count == 4:
-            one, two = swap(block, "hid", 1), swap(block, "hid", 2)
-            pieces[1][k], pieces[2][k] = one, two
-            pieces[3][k] = jnp.concatenate(
-                [swap(one[:capacity], "hid", 2), swap(two[capacity:], "hid", 1)], axis=0
-            )
-        else:
-            for j in range(1, hid_count):
-                pieces[j][k] = swap(block, "hid", j)
-    row_pieces = [[x[:capacity] for x in y[1:]] for y in pieces]
-    grad_pieces = [[x[capacity:] for x in y[1:]] for y in pieces]
-
-    def whole(own, pieces):
-        rest = jnp.zeros(((seq_count - 1) * capacity, model_width), bf16)
+    def spread(x):
+        return [swap(x, "seq", k) for k in range(1, seq_count)]
+
+    def across(x):
+        return [swap(x, "hid", j) for j in ((1, 2) if hid_count == 4 else range(1, hid_count))]
+
+    remote = (seq_count - 1) * capacity
+    split = -(-remote // 32) * 16
+
+    def corner(one, two):
+        if hid_count != 4:
+            return []
+        return [
+            jnp.concatenate([swap(one[:split], "hid", 2), swap(two[split:], "hid", 1)], axis=0)
+        ]
+
+    def with_own(own, x, j):
+        mine = lax.dynamic_slice_in_dim(own, (hid ^ j) * piece, piece, axis=1)
+        return jnp.concatenate([mine, x], axis=0)
+
+    row_message = row_slots(quarter(tokens))
+    row_blocks = spread(row_message)
+    grad_message = after(grad_slots(quarter(out_grad)), row_message)
+    grad_blocks = spread(grad_message)
+    own_rows = row_slots(tokens)
+    own_grads = grad_slots(out_grad)
+    gate_mat, up_mat = after((w_gate[0], w_up[0]), (grad_message, own_rows, own_grads))
+    gate_mat, up_mat = fetch(gate_mat, up_mat)
+    row_blocks = after(row_blocks, gate_mat[:8, :LANES])
+    row_parts = [jnp.concatenate(row_blocks, axis=0)]
+    row_across = across(row_parts[0])
+    down = fetch_columns(hid, after(w_down[0], row_parts[0]), hid_count)
+    pair = pair_step(
+        hid, with_own(own_rows, row_parts[0], 0), gate_mat, up_mat, ()
+    )
+    grad_blocks = after(grad_blocks, (pair, down[0][:8, :LANES]))
+    grad_parts = [jnp.concatenate(grad_blocks, axis=0)]
+    grad_across = across(grad_parts[0])
+    row_across = after(row_across, grad_parts[0])
+    row_corner = corner(row_across[0], row_across[1])
+    for j, x in enumerate(row_across, 1):
+        pair = pair_step(hid ^ j, with_own(own_rows, x, j), gate_mat, up_mat, pair)
+    grad_across = after(grad_across, pair)
+    grad_corner = corner(grad_across[0], grad_across[1])
+    row_corner = after(row_corner, grad_across)
+    for j, x in enumerate(row_corner, 3):
+        pair = pair_step(hid ^ j, with_own(own_rows, x, j), gate_mat, up_mat, pair)
+    back = back_step(with_own(own_grads, grad_parts[0], 0), down[0], (), ())
+    rest = list(enumerate(grad_across, 1))
+    if not grad_corner:
+        final = rest.pop()
+    for j, x in rest:
+        back = back_step(with_own(own_grads, x, j), down[j], back, ())
+    if grad_corner:
+        final = (3, after(grad_corner[0], (back, pair)))
+    row_parts += row_across + row_corner
+    grad_parts += grad_across + grad_corner
+    j, x = final
+    hidden, d_gate, d_up, slots = back_step(
+        with_own(own_grads, x, j), down[j], back, pair
+    )
+
+    def whole(own, parts):
+        rest = jnp.zeros((remote, model_width), bf16)
         for j in range(hid_count):
-            rest = lax.dynamic_update_slice_in_dim(
-                rest, jnp.concatenate(pieces[j], axis=0), (hid ^ j) * piece, axis=1
-            )
+            rest = lax.dynamic_update_slice_in_dim(rest, parts[j], (hid ^ j) * piece, axis=1)
         return jnp.concatenate([own, rest], axis=0)
-
-    rows_e = whole(row_slots(tokens), row_pieces)
-    grads_e = whole(grad_slots(out_grad), grad_pieces)
-
-    hidden, d_gate, d_up, slots = forward_step(rows_e, grads_e, gate_mat, up_mat, down_mat)
 
     received = []
     source = (d_gate, d_up, slots)
@@ -220,6 +307,8 @@
             received.append(swap(part, "hid", j))
     total = part
     hidden, d_gate, d_up = after((hidden, d_gate, d_up), part)
+    rows_e = whole(own_rows, after(row_parts, part))
+    grads_e = whole(own_grads, after(grad_parts, part))
     for part in received:
         total = total + part.astype(f32)
     own_sum = total[:capacity]

time: 124 us -> 103 us (0.83)
  local copies, waits for them, and re-layouts: 12.2 us -> 2.57 us
  waiting for transfers between devices: 18 us -> 10.8 us
  Pallas kernels: 34.8 us -> 30.2 us
  matrix products: 23.4 us -> 24.7 us
    unnamed x26 -> x13, local copies, waits for them, and re-layouts: 9.68 us -> 0.08 us
    ppermute x22 -> x21, waiting for transfers between devices: 18 us -> 10.8 us  [swap(): return lax.ppermute(x, axis, [(i, i ^ bits) for i in range(size)])]
    pallas_call x2 -> x10, Pallas kernels: 27 us -> 22.3 us  [the longest x8 9.08 us: whole_call(): pl.pallas_call(kernel, in_specs=[pl.BlockSpec(memory_space=pltpu.SMEM)] *...]
    dot_general x4, matrix products: 2.08 us -> 3.38 us  [slots_of(): return lax.dot_general(select_own, x, FIRST, preferred_element_type=f32)]
    ppermute x22 -> x21, starting transfers between devices: 29.1 us -> 28.4 us  [swap(): return lax.ppermute(x, axis, [(i, i ^ bits) for i in range(size)])]
  transfers between devices with their start and end apart: 22 -> 21, of which waited for: 11 -> 7; matrix products, arithmetic and copies ran while one was open for 18% -> 23% of each run, Pallas kernels for 11% -> 22%
where the time goes in v3:
time: 103 us
  Pallas kernels  30.2 us (29%)
  starting transfers between devices  28.4 us (28%)
  matrix products  24.7 us (24%)
  waiting for transfers between devices  10.8 us (10%)
  other arithmetic  5.2 us (5%)
  local copies, waits for them, and re-layouts  2.57 us (2%)
  between operations  1.17 us (1%)
    ppermute x21, starting transfers between devices, swap(): return lax.ppermute(x, axis, [(i, i ^ bits) for i in range(size)])  28.4 us
    ppermute x21, waiting for transfers between devices, swap(): return lax.ppermute(x, axis, [(i, i ^ bits) for i in range(size)])  10.8 us
    pallas_call x8, Pallas kernels, whole_call(): pl.pallas_call(kernel, in_specs=[pl.BlockSpec(memory_space=pltpu.SMEM)] *...  9.08 us
    pallas_call x1, Pallas kernels, fetch(): pl.pallas_call(fetch_kernel, in_specs=[pl.BlockSpec(memory_space=pltpu.HB...  8.36 us
    pallas_call x4, Pallas kernels, row_piece(): pl.pallas_call(piece_kernel, in_specs=[pl.BlockSpec(memory_space=pltpu.SM...  7.86 us
    dot_general x1, matrix products, on_device(): lax.dot_general(rows_e, d_up, FIRST, preferred_element_type=f32)  6.65 us
    dot_general x1, matrix products, on_device(): lax.dot_general(rows_e, d_gate, FIRST, preferred_element_type=f32)  6.63 us
    dot_general x1, matrix products, on_device(): lax.dot_general(hidden, grads_e, FIRST, preferred_element_type=f32)  6.62 us
  transfers between devices with their start and end apart: 21, of which 7 were waited for; matrix products, arithmetic and copies ran while one was open for 23% of the time, Pallas kernels for 22%

profile of v3, /device:TPU:0, one launch (start us, length us, event | category | flops | bytes accessed | tf_op | source)
XLA Modules:
  0.0 103.0 jit_solution(7559481299304253965)
XLA Ops:
  3.6 1.8 %convolution_convert_fusion.1 = bf16[40,1536]{1,0:T(8,128)(2,1)} fusion(bf16[128,40]{0,1:T(8,128)(2,1)S(1)} %get-tuple-element.116, bf16[128,6144]{1,0:T(8,128)(2,1)} %param.7, s32[]{:T(128)S(6)} %select_n.8), kind=kOutput, calls=%fused_computation.9 | convolution fusion | flops 15790080 | bytes 526340 | tf_op jit(solution)/shard_map/dot_general | solution.py:219
  5.4 3.0 %collective-permute-start = (bf16[40,1536]{1,0:T(8,128)(2,1)}, bf16[40,1536]{1,0:T(8,128)(2,1)S(1)}, u32[]{:S(2)}, u32[]{:S(2)}) collective-permute-start(bf16[40,1536]{1,0:T(8,128)(2,1)} %convolution_convert_fusion.1), channel_id=1, source_target_pairs={{0,8},{8,0},{16,24},{24,16},{1,9},{9,1},{17,25},{25,17},{2,10},{10... | collective-permute-start | bytes 368648 | tf_op jit(solution)/shard_map/ppermute | solution.py:21
  8.4 2.6 %collective-permute-start.1 = (bf16[40,1536]{1,0:T(8,128)(2,1)}, bf16[40,1536]{1,0:T(8,128)(2,1)S(1)}, u32[]{:S(2)}, u32[]{:S(2)}) collective-permute-start(bf16[40,1536]{1,0:T(8,128)(2,1)} %convolution_convert_fusion.1), channel_id=1, source_target_pairs={{0,16},{8,24},{16,0},{24,8},{1,17},{9,25},{17,1},{25,9},{2,18},{10... | collective-permute-start | bytes 368648 | tf_op jit(solution)/shard_map/ppermute | solution.py:21
  12.8 3.5 %collective-permute-start.6 = (bf16[40,1536]{1,0:T(8,128)(2,1)}, bf16[40,1536]{1,0:T(8,128)(2,1)S(1)}, u32[]{:S(2)}, u32[]{:S(2)}) collective-permute-start(bf16[40,1536]{1,0:T(8,128)(2,1)} %fusion.1), channel_id=1, source_target_pairs={{0,16},{8,24},{16,0},{24,8},{1,17},{9,25},{17,1},{25,9},{2,18},{10... | collective-permute-start | bytes 368648 | tf_op jit(solution)/shard_map/ppermute | solution.py:21
  18.3 8.4 %fetch.1 = (bf16[6144,1024]{1,0:T(8,128)(2,1)S(1)}, bf16[6144,1024]{1,0:T(8,128)(2,1)S(1)}) custom-call(bf16[6144,1024]{1,0:T(8,128)(2,1)} %bitcast.24, bf16[6144,1024]{1,0:T(8,128)(2,1)} %bitcast.25), custom_call_target="tpu_custom_call" | custom-call | tf_op jit(solution)/shard_map/fetch/pallas_call | solution.py:59
  26.8 1.7 %collective-permute-start.3 = (bf16[120,1536]{1,0:T(8,128)(2,1)S(1)}, bf16[120,1536]{1,0:T(8,128)(2,1)S(1)}, u32[]{:S(2)}, u32[]{:S(2)}) collective-permute-start(bf16[120,1536]{1,0:T(8,128)(2,1)S(1)} %constant_dynamic-update-slice_fusion), channel_id=1, source_target_pairs={{0,1},{1,0},{2,3},{3,2},{4,5},{5,4},{6,7},{7,6},{8,9},{9,8},{10,11... | collective-permute-start | bytes 1105928 | tf_op jit(solution)/shard_map/ppermute | solution.py:21
  28.6 1.5 %collective-permute-start.4 = (bf16[120,1536]{1,0:T(8,128)(2,1)S(1)}, bf16[120,1536]{1,0:T(8,128)(2,1)S(1)}, u32[]{:S(2)}, u32[]{:S(2)}) collective-permute-start(bf16[120,1536]{1,0:T(8,128)(2,1)S(1)} %constant_dynamic-update-slice_fusion), channel_id=1, source_target_pairs={{0,2},{1,3},{2,0},{3,1},{4,6},{5,7},{6,4},{7,5},{8,10},{9,11},{10,... | collective-permute-start | bytes 1105928 | tf_op jit(solution)/shard_map/ppermute | solution.py:21
  30.1 1.2 %pair_step.4 = (f32[160,1024]{1,0:T(8,128)S(1)}, f32[160,1024]{1,0:T(8,128)S(1)}) custom-call(s32[1]{0:T(128)} %bitcast.index_ref.piece_ref, bf16[160,1536]{1,0:T(8,128)(2,1)S(1)} %pad_maximum_fusion.3.rows_ref, bf16[6144,1024]{1,0:T(8,128)(2,1)S(1)} %get-tuple-element.65.gate_ref, bf16[6144,1024]{1,0:T(8,128)(2,1)S(1)} %get-tuple-element.66.up_ref), custom_call_target="tpu_custom_call" | custom-call | tf_op jit(solution)/shard_map/pair_step/pallas_call | solution.py:152
  31.3 2.4 %collective-permute-done.7 = bf16[40,1536]{1,0:T(8,128)(2,1)S(1)} collective-permute-done((bf16[40,1536]{1,0:T(8,128)(2,1)}, bf16[40,1536]{1,0:T(8,128)(2,1)S(1)}, u32[]{:S(2)}, u32[]{:S(2)}) %collective-permute-start.7) | collective-permute-done | bytes 122912 | tf_op jit(solution)/shard_map/ppermute | solution.py:21
  33.8 1.6 %collective-permute-start.10 = (bf16[120,1536]{1,0:T(8,128)(2,1)S(1)}, bf16[120,1536]{1,0:T(8,128)(2,1)S(1)}, u32[]{:S(2)}, u32[]{:S(2)}) collective-permute-start(bf16[120,1536]{1,0:T(8,128)(2,1)S(1)} %constant_dynamic-update-slice_fusion.3), channel_id=1, source_target_pairs={{0,1},{1,0},{2,3},{3,2},{4,5},{5,4},{6,7},{7,6},{8,9},{9,8},{10,11... | collective-permute-start | bytes 1105928 | tf_op jit(solution)/shard_map/ppermute | solution.py:21
  35.3 1.5 %collective-permute-start.11 = (bf16[120,1536]{1,0:T(8,128)(2,1)S(1)}, bf16[120,1536]{1,0:T(8,128)(2,1)S(1)}, u32[]{:S(2)}, u32[]{:S(2)}) collective-permute-start(bf16[120,1536]{1,0:T(8,128)(2,1)S(1)} %constant_dynamic-update-slice_fusion.3), channel_id=1, source_target_pairs={{0,2},{1,3},{2,0},{3,1},{4,6},{5,7},{6,4},{7,5},{8,10},{9,11},{10,... | collective-permute-start | bytes 1105928 | tf_op jit(solution)/shard_map/ppermute | solution.py:21
  36.8 4.9 %fetch_columns.1 = (bf16[1024,1536]{1,0:T(8,128)(2,1)S(1)}, bf16[1024,1536]{1,0:T(8,128)(2,1)S(1)}, bf16[1024,1536]{1,0:T(8,128)(2,1)S(1)}, bf16[1024,1536]{1,0:T(8,128)(2,1)S(1)}) custom-call(s32[1]{0:T(128)} %bitcast.index_ref.piece_ref, bf16[1024,6144]{1,0:T(8,128)(2,1)} %bitcast.26), custom_call_target="tpu_custom_call" | custom-call | tf_op jit(solution)/shard_map/fetch_columns/pallas_call | solution.py:92
  44.0 1.2 %pair_step.5 = (f32[160,1024]{1,0:T(8,128)S(1)}, f32[160,1024]{1,0:T(8,128)S(1)}) custom-call(s32[1]{0:T(128)} %bitcast.4.index_ref.piece_ref, bf16[160,1536]{1,0:T(8,128)(2,1)S(1)} %pad_maximum_fusion.5.rows_ref, bf16[6144,1024]{1,0:T(8,128)(2,1)S(1)} %get-tuple-element.65.gate_ref, bf16[6144,1024]{1,0:T(8,128)(2,1)S(1)} %get-tuple-element.66.up_ref, ...), custom_call_target="tpu_custom_call" | custom-call | tf_op jit(solution)/shard_map/pair_step/pallas_call | solution.py:152
  45.3 1.2 %pair_step.6 = (f32[160,1024]{1,0:T(8,128)S(1)}, f32[160,1024]{1,0:T(8,128)S(1)}) custom-call(s32[1]{0:T(128)} %bitcast.3.index_ref.piece_ref, bf16[160,1536]{1,0:T(8,128)(2,1)S(1)} %pad_maximum_fusion.4.rows_ref, bf16[6144,1024]{1,0:T(8,128)(2,1)S(1)} %get-tuple-element.65.gate_ref, bf16[6144,1024]{1,0:T(8,128)(2,1)S(1)} %get-tuple-element.66.up_ref, ...), custom_call_target="tpu_custom_call" | custom-call | tf_op jit(solution)/shard_map/pair_step/pallas_call | solution.py:152
  47.0 1.6 %collective-permute-start.12 = (bf16[64,1536]{1,0:T(8,128)(2,1)S(1)}, bf16[64,1536]{1,0:T(8,128)(2,1)S(1)}, u32[]{:S(2)}, u32[]{:S(2)}) collective-permute-start(bf16[64,1536]{1,0:T(8,128)(2,1)S(1)} %slice.59), channel_id=1, source_target_pairs={{0,2},{1,3},{2,0},{3,1},{4,6},{5,7},{6,4},{7,5},{8,10},{9,11},{10,... | collective-permute-start | bytes 589832 | tf_op jit(solution)/shard_map/ppermute | solution.py:21
  51.9 1.2 %pair_step.7 = (f32[160,1024]{1,0:T(8,128)S(1)}, f32[160,1024]{1,0:T(8,128)S(1)}) custom-call(s32[1]{0:T(128)} %bitcast.6.index_ref.piece_ref, bf16[160,1536]{1,0:T(8,128)(2,1)S(1)} %pad_maximum_fusion.9.rows_ref, bf16[6144,1024]{1,0:T(8,128)(2,1)S(1)} %get-tuple-element.65.gate_ref, bf16[6144,1024]{1,0:T(8,128)(2,1)S(1)} %get-tuple-element.66.up_ref, ...), custom_call_target="tpu_custom_call" | custom-call | tf_op jit(solution)/shard_map/pair_step/pallas_call | solution.py:152
  54.1 1.3 %back_step.7 = (bf16[160,1024]{1,0:T(8,128)(2,1)S(1)}, bf16[160,1024]{1,0:T(8,128)(2,1)S(1)}, bf16[160,1024]{1,0:T(8,128)(2,1)S(1)}, f32[160,128]{1,0:T(8,128)S(1)}) custom-call(bf16[160,1536]{1,0:T(8,128)(2,1)S(1)} %pad_maximum_fusion.10.grads_ref, bf16[1024,1536]{1,0:T(8,128)(2,1)S(1)} %get-tuple-element.88.down_ref, f32[1024,160]{1,0:T(8,128)S(1)} %back_step.6.refs_0_, ...), custom_call_target="tpu_custom_call" | custom-call | tf_op jit(solution)/shard_map/back_step/pallas_call | solution.py:152
  55.5 1.9 %row_piece.4 = bf16[160,1664]{1,0:T(8,128)(2,1)S(1)} custom-call(s32[1]{0:T(128)} %bitcast.6.index_ref.piece_ref, bf16[160,1024]{1,0:T(8,128)(2,1)S(1)} %get-tuple-element.106.d_gate_ref, bf16[160,1024]{1,0:T(8,128)(2,1)S(1)} %get-tuple-element.107.d_up_ref, f32[160,128]{1,0:T(8,128)S(1)} %get-tuple-element.100.slot_ref, ...), custom_call_target="tpu_custom_call" | custom-call | tf_op jit(solution)/shard_map/row_piece/pallas_call | solution.py:194
  57.4 2.1 %row_piece.5 = bf16[160,1664]{1,0:T(8,128)(2,1)S(1)} custom-call(s32[1]{0:T(128)} %bitcast.3.index_ref.piece_ref, bf16[160,1024]{1,0:T(8,128)(2,1)S(1)} %get-tuple-element.106.d_gate_ref, bf16[160,1024]{1,0:T(8,128)(2,1)S(1)} %get-tuple-element.107.d_up_ref, f32[160,128]{1,0:T(8,128)S(1)} %get-tuple-element.100.slot_ref, ...), custom_call_target="tpu_custom_call" | custom-call | tf_op jit(solution)/shard_map/row_piece/pallas_call | solution.py:194
  59.5 1.9 %row_piece.6 = bf16[160,1664]{1,0:T(8,128)(2,1)S(1)} custom-call(s32[1]{0:T(128)} %bitcast.4.index_ref.piece_ref, bf16[160,1024]{1,0:T(8,128)(2,1)S(1)} %get-tuple-element.106.d_gate_ref, bf16[160,1024]{1,0:T(8,128)(2,1)S(1)} %get-tuple-element.107.d_up_ref, f32[160,128]{1,0:T(8,128)S(1)} %get-tuple-element.100.slot_ref, ...), custom_call_target="tpu_custom_call" | custom-call | tf_op jit(solution)/shard_map/row_piece/pallas_call | solution.py:194
  63.0 1.9 %collective-permute-start.14 = (bf16[160,1664]{1,0:T(8,128)(2,1)S(1)}, bf16[160,1664]{1,0:T(8,128)(2,1)}, u32[]{:S(2)}, u32[]{:S(2)}) collective-permute-start(bf16[160,1664]{1,0:T(8,128)(2,1)S(1)} %row_piece.4), channel_id=1, source_target_pairs={{0,3},{1,2},{2,1},{3,0},{4,7},{5,6},{6,5},{7,4},{8,11},{9,10},{10,... | collective-permute-start | bytes 1597448 | tf_op jit(solution)/shard_map/ppermute | solution.py:21
  64.9 2.0 %row_piece.7 = f32[160,1664]{1,0:T(8,128)S(1)} custom-call(s32[1]{0:T(128)} %bitcast.index_ref.piece_ref, bf16[160,1024]{1,0:T(8,128)(2,1)S(1)} %get-tuple-element.106.d_gate_ref, bf16[160,1024]{1,0:T(8,128)(2,1)S(1)} %get-tuple-element.107.d_up_ref, f32[160,128]{1,0:T(8,128)S(1)} %get-tuple-element.100.slot_ref, ...), custom_call_target="tpu_custom_call" | custom-call | tf_op jit(solution)/shard_map/row_piece/pallas_call | solution.py:194
  67.5 6.7 %convert_bitcast_fusion.1 = bf16[1,6144,1024]{2,1,0:T(8,128)(2,1)} fusion(bf16[160,1024]{1,0:T(8,128)(2,1)S(1)} %get-tuple-element.107.d_up_ref, bf16[120,6144]{1,0:T(8,128)(2,1)S(1)} %get-tuple-element.139, bf16[40,6144]{1,0:T(8,128)(2,1)S(1)} %convolution_convert_fusion), kind=kOutput, calls=%fused_computation.1 | convolution fusion | flops 2023489536 | bytes 14876672 | tf_op jit(solution)/shard_map/dot_general | solution.py:335
  74.2 6.6 %convert_bitcast_fusion.2 = bf16[1,6144,1024]{2,1,0:T(8,128)(2,1)} fusion(bf16[160,1024]{1,0:T(8,128)(2,1)S(1)} %get-tuple-element.106.d_gate_ref, bf16[120,6144]{1,0:T(8,128)(2,1)S(1)} %get-tuple-element.139, bf16[40,6144]{1,0:T(8,128)(2,1)S(1)} %convolution_convert_fusion), kind=kOutput, calls=%fused_computation.2 | convolution fusion | flops 2023489536 | bytes 14876672 | tf_op jit(solution)/shard_map/dot_general | solution.py:334
  80.8 4.5 %collective-permute-done.14 = bf16[160,1664]{1,0:T(8,128)(2,1)} collective-permute-done((bf16[160,1664]{1,0:T(8,128)(2,1)S(1)}, bf16[160,1664]{1,0:T(8,128)(2,1)}, u32[]{:S(2)}, u32[]{:S(2)}) %collective-permute-start.14) | collective-permute-done | bytes 532512 | tf_op jit(solution)/shard_map/ppermute | solution.py:21
  85.3 1.5 %fusion.22 = (bf16[160,1664]{1,0:T(8,128)(2,1)S(1)}, f32[160,1664]{1,0:T(8,128)S(1)}) fusion(bf16[160,1664]{1,0:T(8,128)(2,1)S(1)} %collective-permute-done.16, bf16[160,1664]{1,0:T(8,128)(2,1)} %collective-permute-done.15, f32[160,1664]{1,0:T(8,128)S(1)} %row_piece.7, bf16[160,1664]{1,0:T(8,128)(2,1)} %collective-permute-done.14), kind=kLoop, calls=%fused_computation.83 | loop fusion | flops 1863680 | bytes 4259840 | tf_op jit(solution)/shard_map/convert.3
  87.6 2.2 %collective-permute-start.18 = (bf16[40,1664]{1,0:T(8,128)(2,1)S(1)}, bf16[40,1664]{1,0:T(8,128)(2,1)S(1)}, u32[]{:S(2)}, u32[]{:S(2)}) collective-permute-start(bf16[40,1664]{1,0:T(8,128)(2,1)S(1)} %get-tuple-element.127), channel_id=1, source_target_pairs={{0,16},{8,24},{16,0},{24,8},{1,17},{9,25},{17,1},{25,9},{2,18},{10... | collective-permute-start | bytes 399368 | tf_op jit(solution)/shard_map/ppermute | solution.py:21
  89.8 1.4 %collective-permute-start.19 = (bf16[40,1664]{1,0:T(8,128)(2,1)S(1)}, bf16[40,1664]{1,0:T(8,128)(2,1)S(1)}, u32[]{:S(2)}, u32[]{:S(2)}) collective-permute-start(bf16[40,1664]{1,0:T(8,128)(2,1)S(1)} %get-tuple-element.126), channel_id=1, source_target_pairs={{0,24},{8,16},{16,8},{24,0},{1,25},{9,17},{17,9},{25,1},{2,26},{10... | collective-permute-start | bytes 399368 | tf_op jit(solution)/shard_map/ppermute | solution.py:21
  91.3 6.6 %convert_bitcast_fusion = bf16[1,1024,6144]{2,1,0:T(8,128)(2,1)} fusion(bf16[160,1024]{1,0:T(8,128)(2,1)S(1)} %get-tuple-element.108, bf16[120,6144]{1,0:T(8,128)(2,1)S(1)} %get-tuple-element.138, bf16[40,6144]{1,0:T(8,128)(2,1)S(1)} %fusion), kind=kOutput, calls=%fused_computation | convolution fusion | flops 2023489536 | bytes 14876672 | tf_op jit(solution)/shard_map/dot_general | solution.py:333
  97.9 1.3 %collective-permute-done.18 = bf16[40,1664]{1,0:T(8,128)(2,1)S(1)} collective-permute-done((bf16[40,1664]{1,0:T(8,128)(2,1)S(1)}, bf16[40,1664]{1,0:T(8,128)(2,1)S(1)}, u32[]{:S(2)}, u32[]{:S(2)}) %collective-permute-start.18) | collective-permute-done | bytes 133152 | tf_op jit(solution)/shard_map/ppermute | solution.py:21
  99.6 1.1 %collective-permute-done.20 = bf16[40,1664]{1,0:T(8,128)(2,1)S(1)} collective-permute-done((bf16[40,1664]{1,0:T(8,128)(2,1)S(1)}, bf16[40,1664]{1,0:T(8,128)(2,1)S(1)}, u32[]{:S(2)}, u32[]{:S(2)}) %collective-permute-start.20) | collective-permute-done | bytes 133152 | tf_op jit(solution)/shard_map/ppermute | solution.py:21
  101.2 1.2 %convolution_add_fusion = f32[128,1536]{1,0:T(8,128)} fusion(f32[128,1536]{1,0:T(8,128)S(1)} %fusion.9, bf16[128,40]{0,1:T(8,128)(2,1)S(1)} %get-tuple-element.116, bf16[40,1664]{1,0:T(8,128)(2,1)S(1)} %get-tuple-element.119), kind=kOutput, calls=%fused_computation.6 | convolution fusion | flops 15925248 | bytes 1705984 | tf_op jit(solution)/shard_map/dot_general | solution.py:323
  (105 shorter events, 18.2 us)
Async XLA Ops:
  0.6 10.4 %copy-start = (bf16[128,6144]{1,0:T(8,128)(2,1)S(1)}, bf16[128,6144]{1,0:T(8,128)(2,1)}, u32[]{:S(2)}) copy-start(bf16[128,6144]{1,0:T(8,128)(2,1)} %param.8) | copy-start | bytes 4718596
  2.6 14.0 %copy-start.2 = (bf16[128,6144]{1,0:T(8,128)(2,1)S(1)}, bf16[128,6144]{1,0:T(8,128)(2,1)}, u32[]{:S(2)}) copy-start(bf16[128,6144]{1,0:T(8,128)(2,1)} %param.7) | copy-start | bytes 4718596
  5.4 21.2 %collective-permute-start = (bf16[40,1536]{1,0:T(8,128)(2,1)}, bf16[40,1536]{1,0:T(8,128)(2,1)S(1)}, u32[]{:S(2)}, u32[]{:S(2)}) collective-permute-start(bf16[40,1536]{1,0:T(8,128)(2,1)} %convolution_convert_fusion.1), channel_id=1, source_target_pairs={{0,8},{8,0},{16,24},{24,16},{1,9},{9,1},{17,25},{25,17},{2,10},{10... | collective-permute-start | bytes 368648 | tf_op jit(solution)/shard_map/ppermute | solution.py:21
  8.4 18.3 %collective-permute-start.1 = (bf16[40,1536]{1,0:T(8,128)(2,1)}, bf16[40,1536]{1,0:T(8,128)(2,1)S(1)}, u32[]{:S(2)}, u32[]{:S(2)}) collective-permute-start(bf16[40,1536]{1,0:T(8,128)(2,1)} %convolution_convert_fusion.1), channel_id=1, source_target_pairs={{0,16},{8,24},{16,0},{24,8},{1,17},{9,25},{17,1},{25,9},{2,18},{10... | collective-permute-start | bytes 368648 | tf_op jit(solution)/shard_map/ppermute | solution.py:21
  11.0 15.7 %collective-permute-start.2 = (bf16[40,1536]{1,0:T(8,128)(2,1)}, bf16[40,1536]{1,0:T(8,128)(2,1)S(1)}, u32[]{:S(2)}, u32[]{:S(2)}) collective-permute-start(bf16[40,1536]{1,0:T(8,128)(2,1)} %convolution_convert_fusion.1), channel_id=1, source_target_pairs={{0,24},{8,16},{16,8},{24,0},{1,25},{9,17},{17,9},{25,1},{2,26},{10... | collective-permute-start | bytes 368648 | tf_op jit(solution)/shard_map/ppermute | solution.py:21
  11.9 19.5 %collective-permute-start.5 = (bf16[40,1536]{1,0:T(8,128)(2,1)}, bf16[40,1536]{1,0:T(8,128)(2,1)S(1)}, u32[]{:S(2)}, u32[]{:S(2)}) collective-permute-start(bf16[40,1536]{1,0:T(8,128)(2,1)} %fusion.1), channel_id=1, source_target_pairs={{0,8},{8,0},{16,24},{24,16},{1,9},{9,1},{17,25},{25,17},{2,10},{10... | collective-permute-start | bytes 368648 | tf_op jit(solution)/shard_map/ppermute | solution.py:21
  12.8 18.6 %collective-permute-start.6 = (bf16[40,1536]{1,0:T(8,128)(2,1)}, bf16[40,1536]{1,0:T(8,128)(2,1)S(1)}, u32[]{:S(2)}, u32[]{:S(2)}) collective-permute-start(bf16[40,1536]{1,0:T(8,128)(2,1)} %fusion.1), channel_id=1, source_target_pairs={{0,16},{8,24},{16,0},{24,8},{1,17},{9,25},{17,1},{25,9},{2,18},{10... | collective-permute-start | bytes 368648 | tf_op jit(solution)/shard_map/ppermute | solution.py:21
  26.7 7.0 %collective-permute-start.7 = (bf16[40,1536]{1,0:T(8,128)(2,1)}, bf16[40,1536]{1,0:T(8,128)(2,1)S(1)}, u32[]{:S(2)}, u32[]{:S(2)}) collective-permute-start(bf16[40,1536]{1,0:T(8,128)(2,1)} %fusion.1), channel_id=1, source_target_pairs={{0,24},{8,16},{16,8},{24,0},{1,25},{9,17},{17,9},{25,1},{2,26},{10... | collective-permute-start | bytes 368648 | tf_op jit(solution)/shard_map/ppermute | solution.py:21
  26.8 15.9 %collective-permute-start.3 = (bf16[120,1536]{1,0:T(8,128)(2,1)S(1)}, bf16[120,1536]{1,0:T(8,128)(2,1)S(1)}, u32[]{:S(2)}, u32[]{:S(2)}) collective-permute-start(bf16[120,1536]{1,0:T(8,128)(2,1)S(1)} %constant_dynamic-update-slice_fusion), channel_id=1, source_target_pairs={{0,1},{1,0},{2,3},{3,2},{4,5},{5,4},{6,7},{7,6},{8,9},{9,8},{10,11... | collective-permute-start | bytes 1105928 | tf_op jit(solution)/shard_map/ppermute | solution.py:21
  28.6 14.2 %collective-permute-start.4 = (bf16[120,1536]{1,0:T(8,128)(2,1)S(1)}, bf16[120,1536]{1,0:T(8,128)(2,1)S(1)}, u32[]{:S(2)}, u32[]{:S(2)}) collective-permute-start(bf16[120,1536]{1,0:T(8,128)(2,1)S(1)} %constant_dynamic-update-slice_fusion), channel_id=1, source_target_pairs={{0,2},{1,3},{2,0},{3,1},{4,6},{5,7},{6,4},{7,5},{8,10},{9,11},{10,... | collective-permute-start | bytes 1105928 | tf_op jit(solution)/shard_map/ppermute | solution.py:21
  33.8 12.7 %collective-permute-start.10 = (bf16[120,1536]{1,0:T(8,128)(2,1)S(1)}, bf16[120,1536]{1,0:T(8,128)(2,1)S(1)}, u32[]{:S(2)}, u32[]{:S(2)}) collective-permute-start(bf16[120,1536]{1,0:T(8,128)(2,1)S(1)} %constant_dynamic-update-slice_fusion.3), channel_id=1, source_target_pairs={{0,1},{1,0},{2,3},{3,2},{4,5},{5,4},{6,7},{7,6},{8,9},{9,8},{10,11... | collective-permute-start | bytes 1105928 | tf_op jit(solution)/shard_map/ppermute | solution.py:21
  35.3 11.6 %collective-permute-start.11 = (bf16[120,1536]{1,0:T(8,128)(2,1)S(1)}, bf16[120,1536]{1,0:T(8,128)(2,1)S(1)}, u32[]{:S(2)}, u32[]{:S(2)}) collective-permute-start(bf16[120,1536]{1,0:T(8,128)(2,1)S(1)} %constant_dynamic-update-slice_fusion.3), channel_id=1, source_target_pairs={{0,2},{1,3},{2,0},{3,1},{4,6},{5,7},{6,4},{7,5},{8,10},{9,11},{10,... | collective-permute-start | bytes 1105928 | tf_op jit(solution)/shard_map/ppermute | solution.py:21
  42.8 9.0 %collective-permute-start.8 = (bf16[64,1536]{1,0:T(8,128)(2,1)S(1)}, bf16[64,1536]{1,0:T(8,128)(2,1)S(1)}, u32[]{:S(2)}, u32[]{:S(2)}) collective-permute-start(bf16[64,1536]{1,0:T(8,128)(2,1)S(1)} %slice.57), channel_id=1, source_target_pairs={{0,2},{1,3},{2,0},{3,1},{4,6},{5,7},{6,4},{7,5},{8,10},{9,11},{10,... | collective-permute-start | bytes 589832 | tf_op jit(solution)/shard_map/ppermute | solution.py:21
  43.4 8.4 %collective-permute-start.9 = (bf16[56,1536]{1,0:T(8,128)(2,1)S(1)}, bf16[56,1536]{1,0:T(8,128)(2,1)S(1)}, u32[]{:S(2)}, u32[]{:S(2)}) collective-permute-start(bf16[56,1536]{1,0:T(8,128)(2,1)S(1)} %slice.58), channel_id=1, source_target_pairs={{0,1},{1,0},{2,3},{3,2},{4,5},{5,4},{6,7},{7,6},{8,9},{9,8},{10,11... | collective-permute-start | bytes 516104 | tf_op jit(solution)/shard_map/ppermute | solution.py:21
  47.0 6.3 %collective-permute-start.12 = (bf16[64,1536]{1,0:T(8,128)(2,1)S(1)}, bf16[64,1536]{1,0:T(8,128)(2,1)S(1)}, u32[]{:S(2)}, u32[]{:S(2)}) collective-permute-start(bf16[64,1536]{1,0:T(8,128)(2,1)S(1)} %slice.59), channel_id=1, source_target_pairs={{0,2},{1,3},{2,0},{3,1},{4,6},{5,7},{6,4},{7,5},{8,10},{9,11},{10,... | collective-permute-start | bytes 589832 | tf_op jit(solution)/shard_map/ppermute | solution.py:21
  48.6 5.5 %collective-permute-start.13 = (bf16[56,1536]{1,0:T(8,128)(2,1)S(1)}, bf16[56,1536]{1,0:T(8,128)(2,1)S(1)}, u32[]{:S(2)}, u32[]{:S(2)}) collective-permute-start(bf16[56,1536]{1,0:T(8,128)(2,1)S(1)} %slice.60), channel_id=1, source_target_pairs={{0,1},{1,0},{2,3},{3,2},{4,5},{5,4},{6,7},{7,6},{8,9},{9,8},{10,11... | collective-permute-start | bytes 516104 | tf_op jit(solution)/shard_map/ppermute | solution.py:21
  61.4 19.4 %collective-permute-start.16 = (bf16[160,1664]{1,0:T(8,128)(2,1)S(1)}, bf16[160,1664]{1,0:T(8,128)(2,1)S(1)}, u32[]{:S(2)}, u32[]{:S(2)}) collective-permute-start(bf16[160,1664]{1,0:T(8,128)(2,1)S(1)} %row_piece.6), channel_id=1, source_target_pairs={{0,1},{1,0},{2,3},{3,2},{4,5},{5,4},{6,7},{7,6},{8,9},{9,8},{10,11... | collective-permute-start | bytes 1597448 | tf_op jit(solution)/shard_map/ppermute | solution.py:21
  62.5 18.3 %collective-permute-start.15 = (bf16[160,1664]{1,0:T(8,128)(2,1)S(1)}, bf16[160,1664]{1,0:T(8,128)(2,1)}, u32[]{:S(2)}, u32[]{:S(2)}) collective-permute-start(bf16[160,1664]{1,0:T(8,128)(2,1)S(1)} %row_piece.5), channel_id=1, source_target_pairs={{0,2},{1,3},{2,0},{3,1},{4,6},{5,7},{6,4},{7,5},{8,10},{9,11},{10,... | collective-permute-start | bytes 1597448 | tf_op jit(solution)/shard_map/ppermute | solution.py:21
  63.0 22.3 %collective-permute-start.14 = (bf16[160,1664]{1,0:T(8,128)(2,1)S(1)}, bf16[160,1664]{1,0:T(8,128)(2,1)}, u32[]{:S(2)}, u32[]{:S(2)}) collective-permute-start(bf16[160,1664]{1,0:T(8,128)(2,1)S(1)} %row_piece.4), channel_id=1, source_target_pairs={{0,3},{1,2},{2,1},{3,0},{4,7},{5,6},{6,5},{7,4},{8,11},{9,10},{10,... | collective-permute-start | bytes 1597448 | tf_op jit(solution)/shard_map/ppermute | solution.py:21
  86.8 11.1 %collective-permute-start.17 = (bf16[40,1664]{1,0:T(8,128)(2,1)S(1)}, bf16[40,1664]{1,0:T(8,128)(2,1)S(1)}, u32[]{:S(2)}, u32[]{:S(2)}) collective-permute-start(bf16[40,1664]{1,0:T(8,128)(2,1)S(1)} %get-tuple-element.125), channel_id=1, source_target_pairs={{0,8},{8,0},{16,24},{24,16},{1,9},{9,1},{17,25},{25,17},{2,10},{10... | collective-permute-start | bytes 399368 | tf_op jit(solution)/shard_map/ppermute | solution.py:21
  87.6 11.6 %collective-permute-start.18 = (bf16[40,1664]{1,0:T(8,128)(2,1)S(1)}, bf16[40,1664]{1,0:T(8,128)(2,1)S(1)}, u32[]{:S(2)}, u32[]{:S(2)}) collective-permute-start(bf16[40,1664]{1,0:T(8,128)(2,1)S(1)} %get-tuple-element.127), channel_id=1, source_target_pairs={{0,16},{8,24},{16,0},{24,8},{1,17},{9,25},{17,1},{25,9},{2,18},{10... | collective-permute-start | bytes 399368 | tf_op jit(solution)/shard_map/ppermute | solution.py:21
  89.8 9.4 %collective-permute-start.19 = (bf16[40,1664]{1,0:T(8,128)(2,1)S(1)}, bf16[40,1664]{1,0:T(8,128)(2,1)S(1)}, u32[]{:S(2)}, u32[]{:S(2)}) collective-permute-start(bf16[40,1664]{1,0:T(8,128)(2,1)S(1)} %get-tuple-element.126), channel_id=1, source_target_pairs={{0,24},{8,16},{16,8},{24,0},{1,25},{9,17},{17,9},{25,1},{2,26},{10... | collective-permute-start | bytes 399368 | tf_op jit(solution)/shard_map/ppermute | solution.py:21
  99.2 3.7 %copy-start.1 = (bf16[128,6144]{1,0:T(8,128)(2,1)S(1)}, bf16[128,6144]{1,0:T(8,128)(2,1)}, u32[]{:S(2)}) copy-start(bf16[128,6144]{1,0:T(8,128)(2,1)} %param.8) | copy-start | bytes 4718596
  99.3 3.1 %copy-start.3 = (f32[128,2]{0,1:T(2,128)S(1)}, f32[128,2]{0,1:T(2,128)}, u32[]{:S(2)}) copy-start(f32[128,2]{0,1:T(2,128)} %param.10) | copy-start | bytes 3076
  99.3 1.4 %collective-permute-start.20 = (bf16[40,1664]{1,0:T(8,128)(2,1)S(1)}, bf16[40,1664]{1,0:T(8,128)(2,1)S(1)}, u32[]{:S(2)}, u32[]{:S(2)}) collective-permute-start(bf16[40,1664]{1,0:T(8,128)(2,1)S(1)} %get-tuple-element.119), channel_id=1, source_target_pairs={{0,4},{4,0},{1,5},{5,1},{2,6},{6,2},{3,7},{7,3},{8,12},{12,8},{9,1... | collective-permute-start | bytes 399368 | tf_op jit(solution)/shard_map/ppermute | solution.py:21

commit v4 on v3

--- a/solution.py
+++ b/solution.py
@@ -36,6 +36,40 @@
     return (
         (chosen[:, :, None] == 1) & (slot_index[:, :, None] == columns[None, None, :])
     ).astype(jnp.float32)
+
+
+def place_kernel(
+    expert_ref, ids_ref, probs_ref, own_ref, other_ref, half_ref, other_half_ref,
+    tokens_ref, gates_ref,
+):
+    piece = tokens_ref.shape[1]
+    own, other = own_ref[...], other_ref[...]
+    half, other_half = half_ref[...], other_half_ref[...]
+    tokens_ref[...] = jnp.dot(own, half[:, :piece], preferred_element_type=jnp.float32) + jnp.dot(
+        other, other_half[:, :piece], preferred_element_type=jnp.float32
+    )
+    ids = ids_ref[...]
+
+    def gates(select, sums, expert):
+        token = lax.dot_general(
+            sums[:, piece:], select, (((0,), (1,)), ((), ())), preferred_element_type=jnp.float32
+        )
+        return jnp.where(ids == expert, token[:1], 0.0)
+
+    mine = expert_ref[0]
+    gates_ref[...] = (gates(own, half, mine) + gates(other, other_half, 1 - mine)) / probs_ref[...]
+
+
+def sum_kernel(own_ref, *refs):
+    capacity = refs[-1].shape[0]
+    first = len(refs) - own_ref.shape[0] // capacity
+    parts, outs = refs[:first], refs[first:]
+    for k, out in enumerate(outs):
+        lines = slice(k * capacity, (k + 1) * capacity)
+        total = own_ref[lines, :]
+        for part in parts:
+            total = total + part[lines, :].astype(jnp.float32)
+        out[...] = total.astype(out.dtype)
 
 
 def fetch_kernel(*refs):
@@ -197,6 +231,11 @@
         out_specs=pl.BlockSpec(memory_space=pltpu.VMEM),
         out_shape=jax.ShapeDtypeStruct((rows, piece + LANES), dtype),
         compiler_params=pltpu.CompilerParams(vmem_limit_bytes=VMEM_LIMIT),
+        cost_estimate=pl.CostEstimate(
+            flops=4 * rows * hidden_local * piece,
+            transcendentals=0,
+            bytes_accessed=4 * hidden_local * (piece + rows),
+        ),
         name="row_piece",
     )(index.reshape(1), d_gate, d_up, slots, gate_mat, up_mat)
 
@@ -251,24 +290,34 @@
         return jnp.concatenate([mine, x], axis=0)
 
     row_message = row_slots(quarter(tokens))
-    row_blocks = spread(row_message)
     grad_message = after(grad_slots(quarter(out_grad)), row_message)
-    grad_blocks = spread(grad_message)
-    own_rows = row_slots(tokens)
-    own_grads = grad_slots(out_grad)
-    gate_mat, up_mat = after((w_gate[0], w_up[0]), (grad_message, own_rows, own_grads))
-    gate_mat, up_mat = fetch(gate_mat, up_mat)
-    row_blocks = after(row_blocks, gate_mat[:8, :LANES])
+    own_rows, own_grads = after((row_slots(tokens), grad_slots(out_grad)), grad_message)
+    gate_mat, up_mat, down_mat = w_gate[0], w_up[0], w_down[0]
+    if seq_count == 4:
+        row_two, row_one = swap(row_message, "seq", 2), swap(row_message, "seq", 1)
+        grad_two, grad_one = swap(grad_message, "seq", 2), swap(grad_message, "seq", 1)
+        row_two = after(row_two, (own_rows, own_grads))
+        row_three = swap(row_two, "seq", 1)
+        (gate_mat,) = fetch(after(gate_mat, row_two))
+        grad_two = after(grad_two, gate_mat[:8, :LANES])
+        grad_three = swap(grad_two, "seq", 1)
+        row_blocks = after([row_one, row_two, row_three], grad_two)
+        grad_blocks = [grad_one, grad_two, grad_three]
+    else:
+        row_blocks, grad_blocks = spread(row_message), spread(grad_message)
+        (gate_mat,) = fetch(after(gate_mat, (own_rows, own_grads)))
+        row_blocks = after(row_blocks, gate_mat[:8, :LANES])
     row_parts = [jnp.concatenate(row_blocks, axis=0)]
     row_across = across(row_parts[0])
-    down = fetch_columns(hid, after(w_down[0], row_parts[0]), hid_count)
-    pair = pair_step(
-        hid, with_own(own_rows, row_parts[0], 0), gate_mat, up_mat, ()
-    )
-    grad_blocks = after(grad_blocks, (pair, down[0][:8, :LANES]))
+    (up_mat,) = fetch(after(up_mat, row_parts[0]))
+    grad_blocks = after(grad_blocks, up_mat[:8, :LANES])
     grad_parts = [jnp.concatenate(grad_blocks, axis=0)]
     grad_across = across(grad_parts[0])
-    row_across = after(row_across, grad_parts[0])
+    down = fetch_columns(hid, after(down_mat, grad_parts[0]), hid_count)
+    pair = pair_step(
+        hid, with_own(own_rows, after(row_parts[0], grad_parts[0]), 0), gate_mat, up_mat, ()
+    )
+    row_across = after(row_across, (grad_parts[0], pair, down[0][:8, :LANES]))
     row_corner = corner(row_across[0], row_across[1])
     for j, x in enumerate(row_across, 1):
         pair = pair_step(hid ^ j, with_own(own_rows, x, j), gate_mat, up_mat, pair)
@@ -305,35 +354,42 @@
         source = after(source, part)
         if j:
             received.append(swap(part, "hid", j))
-    total = part
     hidden, d_gate, d_up = after((hidden, d_gate, d_up), part)
     rows_e = whole(own_rows, after(row_parts, part))
     grads_e = whole(own_grads, after(grad_parts, part))
-    for part in received:
-        total = total + part.astype(f32)
-    own_sum = total[:capacity]
-    for k in range(1, seq_count):
-        lines = slice(k * capacity, (k + 1) * capacity)
-        own_sum = own_sum + swap(total[lines].astype(bf16), "seq", k).astype(f32)
+    grad_gate = lax.dot_general(rows_e, d_gate, FIRST, preferred_element_type=f32).astype(bf16)
+    grad_up = lax.dot_general(rows_e, d_up, FIRST, preferred_element_type=f32).astype(bf16)
+    if len(received) == 3:
+        part = part + received[0].astype(f32)
+        received = after(received[1:], part)
+    received = after(received, (grad_gate, grad_up))
+    block = (capacity, piece + LANES)
+    own_sum, *messages = whole_call(
+        sum_kernel, "sum_step", [(block, f32)] + [(block, bf16)] * (seq_count - 1), None, part, *received
+    )
+    grad_down = lax.dot_general(hidden, grads_e, FIRST, preferred_element_type=f32).astype(bf16)
+    arrived = [swap(message, "seq", k) for k, message in enumerate(messages, 1)]
+    for part in after(arrived, grad_down):
+        own_sum = own_sum + part.astype(f32)
 
     half = own_sum.astype(bf16)
     other_half = swap(half, "exp", 1)
     pick_other = pick_of(expert_ids, 1 - expert, capacity)
     select_other = jnp.sum(pick_other, axis=1).astype(bf16)
-    d_tokens = jnp.dot(select_own, half[:, :piece], preferred_element_type=f32) + jnp.dot(
-        select_other, other_half[:, :piece], preferred_element_type=f32
-    )
-    slot_own = own_sum[:, piece]
-    slot_other = other_half[:, piece].astype(f32)
-    d_gates = (
-        jnp.sum(pick_own * slot_own[None, None, :], axis=2)
-        + jnp.sum(pick_other * slot_other[None, None, :], axis=2)
-    ) / gate_probs
-
-    grad_down = lax.dot_general(hidden, grads_e, FIRST, preferred_element_type=f32).astype(bf16)
-    grad_gate = lax.dot_general(rows_e, d_gate, FIRST, preferred_element_type=f32).astype(bf16)
-    grad_up = lax.dot_general(rows_e, d_up, FIRST, preferred_element_type=f32).astype(bf16)
-    return (grad_gate[None], grad_up[None], grad_down[None], d_tokens, d_gates)
+    d_tokens, d_gates = whole_call(
+        place_kernel,
+        "place_step",
+        [((tok_rows, piece), f32), ((2, tok_rows), f32)],
+        expert,
+        expert_ids.T,
+        gate_probs.T,
+        select_own,
+        select_other,
+        half,
+        other_half,
+    )
+
+    return (grad_gate[None], grad_up[None], grad_down[None], d_tokens, d_gates.T)
 
 
 def solution(mesh):

time: 103 us -> 97.8 us (0.950)
  waiting for transfers between devices: 10.8 us -> 6.17 us
  matrix products: 24.7 us -> 22.2 us
  Pallas kernels: 30.2 us -> 32.6 us
  other arithmetic: 5.2 us -> 3.87 us
    ppermute x21, waiting for transfers between devices: 10.8 us -> 6.17 us  [swap(): return lax.ppermute(x, axis, [(i, i ^ bits) for i in range(size)])]
    another operation x5 -> x4, other arithmetic: 2.18 us -> 0.68 us
    dot_general x2 -> x0, matrix products: 1.45 us -> none  [the longest x1 1.17 us: on_device(): jnp.dot(select_own, half[:, :piece], preferred_element_type=f32)]
    pallas_call x8 -> x10, Pallas kernels: 9.08 us -> 10.5 us  [whole_call(): pl.pallas_call(kernel, in_specs=[pl.BlockSpec(memory_space=pltpu.SMEM)] *...]
    add x0 -> x1, other arithmetic: none -> 1.16 us  [on_device(): part = part + received[0].astype(f32)]
    dot_general x4, matrix products: 3.38 us -> 2.29 us  [slots_of(): return lax.dot_general(select_own, x, FIRST, preferred_element_type=f32)]
    pallas_call x1 -> x2, Pallas kernels: 8.36 us -> 9.4 us  [fetch(): pl.pallas_call(fetch_kernel, in_specs=[pl.BlockSpec(memory_space=pltpu.HB...]
  transfers between devices with their start and end apart: 21 -> 21, of which waited for: 7 -> 4; matrix products, arithmetic and copies ran while one was open for 23% -> 25% of each run, Pallas kernels for 22% -> 29%
where the time goes in v4:
time: 97.8 us; the launch traced here: 97.5 us
  Pallas kernels  32.6 us (33%)
  starting transfers between devices  27.9 us (29%)
  matrix products  22.2 us (23%)
  waiting for transfers between devices  6.17 us (6%)
  other arithmetic  3.87 us (4%)
  local copies, waits for them, and re-layouts  3.54 us (4%)
  between operations  1.27 us (1%)
    ppermute x21, starting transfers between devices, swap(): return lax.ppermute(x, axis, [(i, i ^ bits) for i in range(size)])  27.9 us
    pallas_call x10, Pallas kernels, whole_call(): pl.pallas_call(kernel, in_specs=[pl.BlockSpec(memory_space=pltpu.SMEM)] *...  10.5 us
    pallas_call x2, Pallas kernels, fetch(): pl.pallas_call(fetch_kernel, in_specs=[pl.BlockSpec(memory_space=pltpu.HB...  9.4 us
    pallas_call x4, Pallas kernels, row_piece(): pl.pallas_call(piece_kernel, in_specs=[pl.BlockSpec(memory_space=pltpu.SM...  7.86 us
    dot_general x1, matrix products, on_device(): lax.dot_general(rows_e, d_up, FIRST, preferred_element_type=f32)  6.63 us
    dot_general x1, matrix products, on_device(): lax.dot_general(rows_e, d_gate, FIRST, preferred_element_type=f32)  6.63 us
    dot_general x1, matrix products, on_device(): lax.dot_general(hidden, grads_e, FIRST, preferred_element_type=f32)  6.62 us
    ppermute x21, waiting for transfers between devices, swap(): return lax.ppermute(x, axis, [(i, i ^ bits) for i in range(size)])  6.17 us
  transfers between devices with their start and end apart: 21, of which 4 were waited for; matrix products, arithmetic and copies ran while one was open for 25% of the time, Pallas kernels for 29%

profile of v4, /device:TPU:0, one launch (start us, length us, event | category | flops | bytes accessed | tf_op | source)
XLA Modules:
  0.0 97.5 jit_solution(12013434746645728838)
XLA Ops:
  3.6 1.3 %convolution_convert_fusion.4 = bf16[40,1536]{1,0:T(8,128)(2,1)S(1)} fusion(bf16[128,40]{1,0:T(8,128)(2,1)S(1)} %copy.28.own_ref, bf16[128,6144]{1,0:T(8,128)(2,1)} %param.7, s32[]{:T(128)S(6)} %select_n.8), kind=kOutput, calls=%fused_computation.8 | convolution fusion | flops 15790080 | bytes 526340 | tf_op jit(solution)/shard_map/dot_general | solution.py:258
  4.9 4.1 %collective-permute-start.1 = (bf16[40,1536]{1,0:T(8,128)(2,1)S(1)}, bf16[40,1536]{1,0:T(8,128)(2,1)S(1)}, u32[]{:S(2)}, u32[]{:S(2)}) collective-permute-start(bf16[40,1536]{1,0:T(8,128)(2,1)S(1)} %convolution_convert_fusion.4), channel_id=1, source_target_pairs={{0,16},{8,24},{16,0},{24,8},{1,17},{9,25},{17,1},{25,9},{2,18},{10... | collective-permute-start | bytes 368648 | tf_op jit(solution)/shard_map/ppermute | solution.py:21
  9.0 1.6 %collective-permute-start = (bf16[40,1536]{1,0:T(8,128)(2,1)S(1)}, bf16[40,1536]{1,0:T(8,128)(2,1)S(1)}, u32[]{:S(2)}, u32[]{:S(2)}) collective-permute-start(bf16[40,1536]{1,0:T(8,128)(2,1)S(1)} %convolution_convert_fusion.4), channel_id=1, source_target_pairs={{0,8},{8,0},{16,24},{24,16},{1,9},{9,1},{17,25},{25,17},{2,10},{10... | collective-permute-start | bytes 368648 | tf_op jit(solution)/shard_map/ppermute | solution.py:21
  13.4 3.2 %collective-permute-done.1 = bf16[40,1536]{1,0:T(8,128)(2,1)S(1)} collective-permute-done((bf16[40,1536]{1,0:T(8,128)(2,1)S(1)}, bf16[40,1536]{1,0:T(8,128)(2,1)S(1)}, u32[]{:S(2)}, u32[]{:S(2)}) %collective-permute-start.1) | collective-permute-done | bytes 122912 | tf_op jit(solution)/shard_map/ppermute | solution.py:21
  16.7 4.7 %fetch.2.gate_ref = bf16[6144,1024]{1,0:T(8,128)(2,1)S(1)} custom-call(bf16[6144,1024]{1,0:T(8,128)(2,1)} %bitcast.27), custom_call_target="tpu_custom_call" | custom-call | tf_op jit(solution)/shard_map/fetch/pallas_call | solution.py:93
  21.5 2.0 %collective-permute-start.7 = (bf16[40,1536]{1,0:T(8,128)(2,1)S(1)}, bf16[40,1536]{1,0:T(8,128)(2,1)S(1)}, u32[]{:S(2)}, u32[]{:S(2)}) collective-permute-start(bf16[40,1536]{1,0:T(8,128)(2,1)S(1)} %collective-permute-done.3), channel_id=1, source_target_pairs={{0,8},{8,0},{16,24},{24,16},{1,9},{9,1},{17,25},{25,17},{2,10},{10... | collective-permute-start | bytes 368648 | tf_op jit(solution)/shard_map/ppermute | solution.py:21
  23.5 1.7 %collective-permute-start.4 = (bf16[120,1536]{1,0:T(8,128)(2,1)S(1)}, bf16[120,1536]{1,0:T(8,128)(2,1)S(1)}, u32[]{:S(2)}, u32[]{:S(2)}) collective-permute-start(bf16[120,1536]{1,0:T(8,128)(2,1)S(1)} %constant_dynamic-update-slice_fusion), channel_id=1, source_target_pairs={{0,1},{1,0},{2,3},{3,2},{4,5},{5,4},{6,7},{7,6},{8,9},{9,8},{10,11... | collective-permute-start | bytes 1105928 | tf_op jit(solution)/shard_map/ppermute | solution.py:21
  25.2 1.5 %collective-permute-start.5 = (bf16[120,1536]{1,0:T(8,128)(2,1)S(1)}, bf16[120,1536]{1,0:T(8,128)(2,1)S(1)}, u32[]{:S(2)}, u32[]{:S(2)}) collective-permute-start(bf16[120,1536]{1,0:T(8,128)(2,1)S(1)} %constant_dynamic-update-slice_fusion), channel_id=1, source_target_pairs={{0,2},{1,3},{2,0},{3,1},{4,6},{5,7},{6,4},{7,5},{8,10},{9,11},{10,... | collective-permute-start | bytes 1105928 | tf_op jit(solution)/shard_map/ppermute | solution.py:21
  26.8 1.3 %collective-permute-start.10 = (bf16[120,1536]{1,0:T(8,128)(2,1)S(1)}, bf16[120,1536]{1,0:T(8,128)(2,1)S(1)}, u32[]{:S(2)}, u32[]{:S(2)}) collective-permute-start(bf16[120,1536]{1,0:T(8,128)(2,1)S(1)} %constant_dynamic-update-slice_fusion.3), channel_id=1, source_target_pairs={{0,1},{1,0},{2,3},{3,2},{4,5},{5,4},{6,7},{7,6},{8,9},{9,8},{10,11... | collective-permute-start | bytes 1105928 | tf_op jit(solution)/shard_map/ppermute | solution.py:21
  28.1 1.5 %collective-permute-start.11 = (bf16[120,1536]{1,0:T(8,128)(2,1)S(1)}, bf16[120,1536]{1,0:T(8,128)(2,1)S(1)}, u32[]{:S(2)}, u32[]{:S(2)}) collective-permute-start(bf16[120,1536]{1,0:T(8,128)(2,1)S(1)} %constant_dynamic-update-slice_fusion.3), channel_id=1, source_target_pairs={{0,2},{1,3},{2,0},{3,1},{4,6},{5,7},{6,4},{7,5},{8,10},{9,11},{10,... | collective-permute-start | bytes 1105928 | tf_op jit(solution)/shard_map/ppermute | solution.py:21
  29.6 4.7 %fetch.3.up_ref = bf16[6144,1024]{1,0:T(8,128)(2,1)S(1)} custom-call(bf16[6144,1024]{1,0:T(8,128)(2,1)} %bitcast.28), custom_call_target="tpu_custom_call" | custom-call | tf_op jit(solution)/shard_map/fetch/pallas_call | solution.py:93
  34.3 4.9 %fetch_columns.1 = (bf16[1024,1536]{1,0:T(8,128)(2,1)S(1)}, bf16[1024,1536]{1,0:T(8,128)(2,1)S(1)}, bf16[1024,1536]{1,0:T(8,128)(2,1)S(1)}, bf16[1024,1536]{1,0:T(8,128)(2,1)S(1)}) custom-call(s32[1]{0:T(128)} %bitcast.index_ref.piece_ref, bf16[1024,6144]{1,0:T(8,128)(2,1)} %bitcast.29), custom_call_target="tpu_custom_call" | custom-call | tf_op jit(solution)/shard_map/fetch_columns/pallas_call | solution.py:126
  43.0 1.2 %pair_step.5 = (f32[160,1024]{1,0:T(8,128)S(1)}, f32[160,1024]{1,0:T(8,128)S(1)}) custom-call(s32[1]{0:T(128)} %bitcast.4.index_ref.piece_ref, bf16[160,1536]{1,0:T(8,128)(2,1)S(1)} %pad_maximum_fusion.5.rows_ref, bf16[6144,1024]{1,0:T(8,128)(2,1)S(1)} %fetch.2.gate_ref, bf16[6144,1024]{1,0:T(8,128)(2,1)S(1)} %fetch.3.up_ref, ...), custom_call_target="tpu_custom_call" | custom-call | tf_op jit(solution)/shard_map/pair_step/pallas_call | solution.py:186
  44.3 1.2 %pair_step.6 = (f32[160,1024]{1,0:T(8,128)S(1)}, f32[160,1024]{1,0:T(8,128)S(1)}) custom-call(s32[1]{0:T(128)} %bitcast.3.index_ref.piece_ref, bf16[160,1536]{1,0:T(8,128)(2,1)S(1)} %pad_maximum_fusion.4.rows_ref, bf16[6144,1024]{1,0:T(8,128)(2,1)S(1)} %fetch.2.gate_ref, bf16[6144,1024]{1,0:T(8,128)(2,1)S(1)} %fetch.3.up_ref, ...), custom_call_target="tpu_custom_call" | custom-call | tf_op jit(solution)/shard_map/pair_step/pallas_call | solution.py:186
  45.6 1.3 %collective-permute-start.12 = (bf16[64,1536]{1,0:T(8,128)(2,1)S(1)}, bf16[64,1536]{1,0:T(8,128)(2,1)S(1)}, u32[]{:S(2)}, u32[]{:S(2)}) collective-permute-start(bf16[64,1536]{1,0:T(8,128)(2,1)S(1)} %slice.33), channel_id=1, source_target_pairs={{0,2},{1,3},{2,0},{3,1},{4,6},{5,7},{6,4},{7,5},{8,10},{9,11},{10,... | collective-permute-start | bytes 589832 | tf_op jit(solution)/shard_map/ppermute | solution.py:21
  46.9 1.6 %collective-permute-start.13 = (bf16[56,1536]{1,0:T(8,128)(2,1)S(1)}, bf16[56,1536]{1,0:T(8,128)(2,1)S(1)}, u32[]{:S(2)}, u32[]{:S(2)}) collective-permute-start(bf16[56,1536]{1,0:T(8,128)(2,1)S(1)} %slice.34), channel_id=1, source_target_pairs={{0,1},{1,0},{2,3},{3,2},{4,5},{5,4},{6,7},{7,6},{8,9},{9,8},{10,11... | collective-permute-start | bytes 516104 | tf_op jit(solution)/shard_map/ppermute | solution.py:21
  50.6 1.2 %pair_step.7 = (f32[160,1024]{1,0:T(8,128)S(1)}, f32[160,1024]{1,0:T(8,128)S(1)}) custom-call(s32[1]{0:T(128)} %bitcast.6.index_ref.piece_ref, bf16[160,1536]{1,0:T(8,128)(2,1)S(1)} %pad_maximum_fusion.9.rows_ref, bf16[6144,1024]{1,0:T(8,128)(2,1)S(1)} %fetch.2.gate_ref, bf16[6144,1024]{1,0:T(8,128)(2,1)S(1)} %fetch.3.up_ref, ...), custom_call_target="tpu_custom_call" | custom-call | tf_op jit(solution)/shard_map/pair_step/pallas_call | solution.py:186
  52.5 1.3 %back_step.7 = (bf16[160,1024]{1,0:T(8,128)(2,1)S(1)}, bf16[160,1024]{1,0:T(8,128)(2,1)S(1)}, bf16[160,1024]{1,0:T(8,128)(2,1)S(1)}, f32[160,128]{1,0:T(8,128)S(1)}) custom-call(bf16[160,1536]{1,0:T(8,128)(2,1)S(1)} %pad_maximum_fusion.10.grads_ref, bf16[1024,1536]{1,0:T(8,128)(2,1)S(1)} %get-tuple-element.105.down_ref, f32[1024,160]{1,0:T(8,128)S(1)} %back_step.6.refs_0_, ...), custom_call_target="tpu_custom_call" | custom-call | tf_op jit(solution)/shard_map/back_step/pallas_call | solution.py:186
  53.8 1.9 %row_piece.4 = bf16[160,1664]{1,0:T(8,128)(2,1)S(1)} custom-call(s32[1]{0:T(128)} %bitcast.6.index_ref.piece_ref, bf16[160,1024]{1,0:T(8,128)(2,1)S(1)} %get-tuple-element.123.d_gate_ref, bf16[160,1024]{1,0:T(8,128)(2,1)S(1)} %get-tuple-element.124.d_up_ref, f32[160,128]{1,0:T(8,128)S(1)} %get-tuple-element.117.slot_ref, ...), custom_call_target="tpu_custom_call" | custom-call | flops 1006632960 | bytes 6946816 | tf_op jit(solution)/shard_map/row_piece/pallas_call | solution.py:228
  55.7 1.5 %collective-permute-start.14 = (bf16[160,1664]{1,0:T(8,128)(2,1)S(1)}, bf16[160,1664]{1,0:T(8,128)(2,1)}, u32[]{:S(2)}, u32[]{:S(2)}) collective-permute-start(bf16[160,1664]{1,0:T(8,128)(2,1)S(1)} %row_piece.4), channel_id=1, source_target_pairs={{0,3},{1,2},{2,1},{3,0},{4,7},{5,6},{6,5},{7,4},{8,11},{9,10},{10,... | collective-permute-start | bytes 1597448 | tf_op jit(solution)/shard_map/ppermute | solution.py:21
  57.2 2.1 %row_piece.5 = bf16[160,1664]{1,0:T(8,128)(2,1)S(1)} custom-call(s32[1]{0:T(128)} %bitcast.3.index_ref.piece_ref, bf16[160,1024]{1,0:T(8,128)(2,1)S(1)} %get-tuple-element.123.d_gate_ref, bf16[160,1024]{1,0:T(8,128)(2,1)S(1)} %get-tuple-element.124.d_up_ref, f32[160,128]{1,0:T(8,128)S(1)} %get-tuple-element.117.slot_ref, ...), custom_call_target="tpu_custom_call" | custom-call | flops 1006632960 | bytes 6946816 | tf_op jit(solution)/shard_map/row_piece/pallas_call | solution.py:228
  59.3 1.9 %row_piece.6 = bf16[160,1664]{1,0:T(8,128)(2,1)S(1)} custom-call(s32[1]{0:T(128)} %bitcast.4.index_ref.piece_ref, bf16[160,1024]{1,0:T(8,128)(2,1)S(1)} %get-tuple-element.123.d_gate_ref, bf16[160,1024]{1,0:T(8,128)(2,1)S(1)} %get-tuple-element.124.d_up_ref, f32[160,128]{1,0:T(8,128)S(1)} %get-tuple-element.117.slot_ref, ...), custom_call_target="tpu_custom_call" | custom-call | flops 1006632960 | bytes 6946816 | tf_op jit(solution)/shard_map/row_piece/pallas_call | solution.py:228
  62.1 1.2 %collective-permute-start.15 = (bf16[160,1664]{1,0:T(8,128)(2,1)S(1)}, bf16[160,1664]{1,0:T(8,128)(2,1)S(1)}, u32[]{:S(2)}, u32[]{:S(2)}) collective-permute-start(bf16[160,1664]{1,0:T(8,128)(2,1)S(1)} %row_piece.5), channel_id=1, source_target_pairs={{0,2},{1,3},{2,0},{3,1},{4,6},{5,7},{6,4},{7,5},{8,10},{9,11},{10,... | collective-permute-start | bytes 1597448 | tf_op jit(solution)/shard_map/ppermute | solution.py:21
  63.3 2.0 %row_piece.7 = f32[160,1664]{1,0:T(8,128)S(1)} custom-call(s32[1]{0:T(128)} %bitcast.index_ref.piece_ref, bf16[160,1024]{1,0:T(8,128)(2,1)S(1)} %get-tuple-element.123.d_gate_ref, bf16[160,1024]{1,0:T(8,128)(2,1)S(1)} %get-tuple-element.124.d_up_ref, f32[160,128]{1,0:T(8,128)S(1)} %get-tuple-element.117.slot_ref, bf16[6144,1024]{1,0:T(8,128)(2,1)S(1)} %fetch.2.gate_ref, ...), custom_call_target="tpu_custom_call" | custom-call | flops 1006632960 | bytes 6946816 | tf_op jit(solution)/shard_map/row_piece/pallas_call | solution.py:228
  66.7 6.6 %convolution_convert_fusion.1 = bf16[6144,1024]{1,0:T(8,128)(2,1)} fusion(bf16[160,1024]{1,0:T(8,128)(2,1)S(1)} %get-tuple-element.124.d_up_ref, bf16[120,6144]{1,0:T(8,128)(2,1)S(1)} %constant_dynamic-update-slice_fusion.12, bf16[40,6144]{1,0:T(8,128)(2,1)S(1)} %copy-done.5), kind=kOutput, calls=%fused_computation.1 | convolution fusion | flops 2023489536 | bytes 14876672 | tf_op jit(solution)/shard_map/dot_general | solution.py:361
  73.3 6.6 %convolution_convert_fusion.2 = bf16[6144,1024]{1,0:T(8,128)(2,1)} fusion(bf16[160,1024]{1,0:T(8,128)(2,1)S(1)} %get-tuple-element.123.d_gate_ref, bf16[120,6144]{1,0:T(8,128)(2,1)S(1)} %constant_dynamic-update-slice_fusion.12, bf16[40,6144]{1,0:T(8,128)(2,1)S(1)} %copy-done.5), kind=kOutput, calls=%fused_computation.2 | convolution fusion | flops 2023489536 | bytes 14876672 | tf_op jit(solution)/shard_map/dot_general | solution.py:360
  81.4 2.1 %collective-permute-start.17 = (bf16[40,1664]{1,0:T(8,128)(2,1)S(1)}, bf16[40,1664]{1,0:T(8,128)(2,1)S(1)}, u32[]{:S(2)}, u32[]{:S(2)}) collective-permute-start(bf16[40,1664]{1,0:T(8,128)(2,1)S(1)} %get-tuple-element.135), channel_id=1, source_target_pairs={{0,8},{8,0},{16,24},{24,16},{1,9},{9,1},{17,25},{25,17},{2,10},{10... | collective-permute-start | bytes 399368 | tf_op jit(solution)/shard_map/ppermute | solution.py:21
  83.5 2.0 %collective-permute-start.18 = (bf16[40,1664]{1,0:T(8,128)(2,1)S(1)}, bf16[40,1664]{1,0:T(8,128)(2,1)S(1)}, u32[]{:S(2)}, u32[]{:S(2)}) collective-permute-start(bf16[40,1664]{1,0:T(8,128)(2,1)S(1)} %get-tuple-element.136), channel_id=1, source_target_pairs={{0,16},{8,24},{16,0},{24,8},{1,17},{9,25},{17,1},{25,9},{2,18},{10... | collective-permute-start | bytes 399368 | tf_op jit(solution)/shard_map/ppermute | solution.py:21
  85.6 1.4 %collective-permute-start.19 = (bf16[40,1664]{1,0:T(8,128)(2,1)S(1)}, bf16[40,1664]{1,0:T(8,128)(2,1)S(1)}, u32[]{:S(2)}, u32[]{:S(2)}) collective-permute-start(bf16[40,1664]{1,0:T(8,128)(2,1)S(1)} %get-tuple-element.137), channel_id=1, source_target_pairs={{0,24},{8,16},{16,8},{24,0},{1,25},{9,17},{17,9},{25,1},{2,26},{10... | collective-permute-start | bytes 399368 | tf_op jit(solution)/shard_map/ppermute | solution.py:21
  87.0 6.6 %convolution_convert_fusion = bf16[1024,6144]{1,0:T(8,128)(2,1)} fusion(bf16[160,1024]{1,0:T(8,128)(2,1)S(1)} %get-tuple-element.125, bf16[120,6144]{1,0:T(8,128)(2,1)S(1)} %constant_dynamic-update-slice_fusion.8, bf16[40,6144]{1,0:T(8,128)(2,1)S(1)} %copy-done.7), kind=kOutput, calls=%fused_computation | convolution fusion | flops 2023489536 | bytes 14876672 | tf_op jit(solution)/shard_map/dot_general | solution.py:370
  93.6 1.2 %collective-permute-done.18 = bf16[40,1664]{1,0:T(8,128)(2,1)S(1)} collective-permute-done((bf16[40,1664]{1,0:T(8,128)(2,1)S(1)}, bf16[40,1664]{1,0:T(8,128)(2,1)S(1)}, u32[]{:S(2)}, u32[]{:S(2)}) %collective-permute-start.18) | collective-permute-done | bytes 133152 | tf_op jit(solution)/shard_map/ppermute | solution.py:21
  96.3 1.2 %place_step.1 = (f32[128,1536]{1,0:T(8,128)}, f32[2,128]{1,0:T(2,128)}) custom-call(s32[1]{0:T(128)} %bitcast.10.expert_ref, s32[2,128]{1,0:T(2,128)S(1)} %bitcast.23, f32[2,128]{1,0:T(2,128)S(1)} %bitcast.24, bf16[128,40]{1,0:T(8,128)(2,1)S(1)} %copy.28.own_ref, bf16[128,40]{1,0:T(8,128)(2,1)S(1)} %copy.31.other_ref, ...), custom_call_target="tpu_custom_call" | custom-call | tf_op jit(solution)/shard_map/place_step/pallas_call | solution.py:186
  (121 shorter events, 17.6 us)
Async XLA Ops:
  0.6 10.0 %copy-start = (bf16[128,6144]{1,0:T(8,128)(2,1)S(1)}, bf16[128,6144]{1,0:T(8,128)(2,1)}, u32[]{:S(2)}) copy-start(bf16[128,6144]{1,0:T(8,128)(2,1)} %param.8) | copy-start | bytes 4718596
  3.6 8.2 %copy-start.8 = (bf16[128,6144]{1,0:T(8,128)(2,1)S(1)}, bf16[128,6144]{1,0:T(8,128)(2,1)}, u32[]{:S(2)}) copy-start(bf16[128,6144]{1,0:T(8,128)(2,1)} %param.7) | copy-start | bytes 4718596
  4.9 11.7 %collective-permute-start.1 = (bf16[40,1536]{1,0:T(8,128)(2,1)S(1)}, bf16[40,1536]{1,0:T(8,128)(2,1)S(1)}, u32[]{:S(2)}, u32[]{:S(2)}) collective-permute-start(bf16[40,1536]{1,0:T(8,128)(2,1)S(1)} %convolution_convert_fusion.4), channel_id=1, source_target_pairs={{0,16},{8,24},{16,0},{24,8},{1,17},{9,25},{17,1},{25,9},{2,18},{10... | collective-permute-start | bytes 368648 | tf_op jit(solution)/shard_map/ppermute | solution.py:21
  9.0 14.5 %collective-permute-start = (bf16[40,1536]{1,0:T(8,128)(2,1)S(1)}, bf16[40,1536]{1,0:T(8,128)(2,1)S(1)}, u32[]{:S(2)}, u32[]{:S(2)}) collective-permute-start(bf16[40,1536]{1,0:T(8,128)(2,1)S(1)} %convolution_convert_fusion.4), channel_id=1, source_target_pairs={{0,8},{8,0},{16,24},{24,16},{1,9},{9,1},{17,25},{25,17},{2,10},{10... | collective-permute-start | bytes 368648 | tf_op jit(solution)/shard_map/ppermute | solution.py:21
  10.8 10.6 %collective-permute-start.3 = (bf16[40,1536]{1,0:T(8,128)(2,1)S(1)}, bf16[40,1536]{1,0:T(8,128)(2,1)S(1)}, u32[]{:S(2)}, u32[]{:S(2)}) collective-permute-start(bf16[40,1536]{1,0:T(8,128)(2,1)S(1)} %fusion.1), channel_id=1, source_target_pairs={{0,16},{8,24},{16,0},{24,8},{1,17},{9,25},{17,1},{25,9},{2,18},{10... | collective-permute-start | bytes 368648 | tf_op jit(solution)/shard_map/ppermute | solution.py:21
  11.2 15.6 %collective-permute-start.6 = (bf16[40,1536]{1,0:T(8,128)(2,1)S(1)}, bf16[40,1536]{1,0:T(8,128)(2,1)S(1)}, u32[]{:S(2)}, u32[]{:S(2)}) collective-permute-start(bf16[40,1536]{1,0:T(8,128)(2,1)S(1)} %fusion.1), channel_id=1, source_target_pairs={{0,8},{8,0},{16,24},{24,16},{1,9},{9,1},{17,25},{25,17},{2,10},{10... | collective-permute-start | bytes 368648 | tf_op jit(solution)/shard_map/ppermute | solution.py:21
  11.8 4.9 %copy-start.6 = (bf16[40,6144]{1,0:T(8,128)(2,1)}, bf16[40,6144]{1,0:T(8,128)(2,1)S(1)}, u32[]{:S(2)}) copy-start(bf16[40,6144]{1,0:T(8,128)(2,1)S(1)} %fusion) | copy-start | bytes 1474564
  12.2 9.3 %copy-start.4 = (bf16[40,6144]{1,0:T(8,128)(2,1)}, bf16[40,6144]{1,0:T(8,128)(2,1)S(1)}, u32[]{:S(2)}) copy-start(bf16[40,6144]{1,0:T(8,128)(2,1)S(1)} %convolution_convert_fusion.3) | copy-start | bytes 1474564
  16.6 6.9 %collective-permute-start.2 = (bf16[40,1536]{1,0:T(8,128)(2,1)S(1)}, bf16[40,1536]{1,0:T(8,128)(2,1)S(1)}, u32[]{:S(2)}, u32[]{:S(2)}) collective-permute-start(bf16[40,1536]{1,0:T(8,128)(2,1)S(1)} %collective-permute-done.1), channel_id=1, source_target_pairs={{0,8},{8,0},{16,24},{24,16},{1,9},{9,1},{17,25},{25,17},{2,10},{10... | collective-permute-start | bytes 368648 | tf_op jit(solution)/shard_map/ppermute | solution.py:21
  21.5 5.3 %collective-permute-start.7 = (bf16[40,1536]{1,0:T(8,128)(2,1)S(1)}, bf16[40,1536]{1,0:T(8,128)(2,1)S(1)}, u32[]{:S(2)}, u32[]{:S(2)}) collective-permute-start(bf16[40,1536]{1,0:T(8,128)(2,1)S(1)} %collective-permute-done.3), channel_id=1, source_target_pairs={{0,8},{8,0},{16,24},{24,16},{1,9},{9,1},{17,25},{25,17},{2,10},{10... | collective-permute-start | bytes 368648 | tf_op jit(solution)/shard_map/ppermute | solution.py:21
  23.5 18.0 %collective-permute-start.4 = (bf16[120,1536]{1,0:T(8,128)(2,1)S(1)}, bf16[120,1536]{1,0:T(8,128)(2,1)S(1)}, u32[]{:S(2)}, u32[]{:S(2)}) collective-permute-start(bf16[120,1536]{1,0:T(8,128)(2,1)S(1)} %constant_dynamic-update-slice_fusion), channel_id=1, source_target_pairs={{0,1},{1,0},{2,3},{3,2},{4,5},{5,4},{6,7},{7,6},{8,9},{9,8},{10,11... | collective-permute-start | bytes 1105928 | tf_op jit(solution)/shard_map/ppermute | solution.py:21
  25.2 16.3 %collective-permute-start.5 = (bf16[120,1536]{1,0:T(8,128)(2,1)S(1)}, bf16[120,1536]{1,0:T(8,128)(2,1)S(1)}, u32[]{:S(2)}, u32[]{:S(2)}) collective-permute-start(bf16[120,1536]{1,0:T(8,128)(2,1)S(1)} %constant_dynamic-update-slice_fusion), channel_id=1, source_target_pairs={{0,2},{1,3},{2,0},{3,1},{4,6},{5,7},{6,4},{7,5},{8,10},{9,11},{10,... | collective-permute-start | bytes 1105928 | tf_op jit(solution)/shard_map/ppermute | solution.py:21
  26.8 18.7 %collective-permute-start.10 = (bf16[120,1536]{1,0:T(8,128)(2,1)S(1)}, bf16[120,1536]{1,0:T(8,128)(2,1)S(1)}, u32[]{:S(2)}, u32[]{:S(2)}) collective-permute-start(bf16[120,1536]{1,0:T(8,128)(2,1)S(1)} %constant_dynamic-update-slice_fusion.3), channel_id=1, source_target_pairs={{0,1},{1,0},{2,3},{3,2},{4,5},{5,4},{6,7},{7,6},{8,9},{9,8},{10,11... | collective-permute-start | bytes 1105928 | tf_op jit(solution)/shard_map/ppermute | solution.py:21
  28.1 17.4 %collective-permute-start.11 = (bf16[120,1536]{1,0:T(8,128)(2,1)S(1)}, bf16[120,1536]{1,0:T(8,128)(2,1)S(1)}, u32[]{:S(2)}, u32[]{:S(2)}) collective-permute-start(bf16[120,1536]{1,0:T(8,128)(2,1)S(1)} %constant_dynamic-update-slice_fusion.3), channel_id=1, source_target_pairs={{0,2},{1,3},{2,0},{3,1},{4,6},{5,7},{6,4},{7,5},{8,10},{9,11},{10,... | collective-permute-start | bytes 1105928 | tf_op jit(solution)/shard_map/ppermute | solution.py:21
  41.5 9.0 %collective-permute-start.8 = (bf16[64,1536]{1,0:T(8,128)(2,1)S(1)}, bf16[64,1536]{1,0:T(8,128)(2,1)S(1)}, u32[]{:S(2)}, u32[]{:S(2)}) collective-permute-start(bf16[64,1536]{1,0:T(8,128)(2,1)S(1)} %slice.31), channel_id=1, source_target_pairs={{0,2},{1,3},{2,0},{3,1},{4,6},{5,7},{6,4},{7,5},{8,10},{9,11},{10,... | collective-permute-start | bytes 589832 | tf_op jit(solution)/shard_map/ppermute | solution.py:21
  42.1 8.4 %collective-permute-start.9 = (bf16[56,1536]{1,0:T(8,128)(2,1)S(1)}, bf16[56,1536]{1,0:T(8,128)(2,1)S(1)}, u32[]{:S(2)}, u32[]{:S(2)}) collective-permute-start(bf16[56,1536]{1,0:T(8,128)(2,1)S(1)} %slice.32), channel_id=1, source_target_pairs={{0,1},{1,0},{2,3},{3,2},{4,5},{5,4},{6,7},{7,6},{8,9},{9,8},{10,11... | collective-permute-start | bytes 516104 | tf_op jit(solution)/shard_map/ppermute | solution.py:21
  45.5 3.9 %copy-start.11 = (bf16[120,1536]{1,0:T(8,128)(2,1)}, bf16[120,1536]{1,0:T(8,128)(2,1)S(1)}, u32[]{:S(2)}) copy-start(bf16[120,1536]{1,0:T(8,128)(2,1)S(1)} %collective-permute-done.11) | copy-start | bytes 1105924
  45.6 6.2 %collective-permute-start.12 = (bf16[64,1536]{1,0:T(8,128)(2,1)S(1)}, bf16[64,1536]{1,0:T(8,128)(2,1)S(1)}, u32[]{:S(2)}, u32[]{:S(2)}) collective-permute-start(bf16[64,1536]{1,0:T(8,128)(2,1)S(1)} %slice.33), channel_id=1, source_target_pairs={{0,2},{1,3},{2,0},{3,1},{4,6},{5,7},{6,4},{7,5},{8,10},{9,11},{10,... | collective-permute-start | bytes 589832 | tf_op jit(solution)/shard_map/ppermute | solution.py:21
  46.9 5.5 %collective-permute-start.13 = (bf16[56,1536]{1,0:T(8,128)(2,1)S(1)}, bf16[56,1536]{1,0:T(8,128)(2,1)S(1)}, u32[]{:S(2)}, u32[]{:S(2)}) collective-permute-start(bf16[56,1536]{1,0:T(8,128)(2,1)S(1)} %slice.34), channel_id=1, source_target_pairs={{0,1},{1,0},{2,3},{3,2},{4,5},{5,4},{6,7},{7,6},{8,9},{9,8},{10,11... | collective-permute-start | bytes 516104 | tf_op jit(solution)/shard_map/ppermute | solution.py:21
  55.7 24.4 %collective-permute-start.14 = (bf16[160,1664]{1,0:T(8,128)(2,1)S(1)}, bf16[160,1664]{1,0:T(8,128)(2,1)}, u32[]{:S(2)}, u32[]{:S(2)}) collective-permute-start(bf16[160,1664]{1,0:T(8,128)(2,1)S(1)} %row_piece.4), channel_id=1, source_target_pairs={{0,3},{1,2},{2,1},{3,0},{4,7},{5,6},{6,5},{7,4},{8,11},{9,10},{10,... | collective-permute-start | bytes 1597448 | tf_op jit(solution)/shard_map/ppermute | solution.py:21
  61.2 20.1 %collective-permute-start.16 = (bf16[160,1664]{1,0:T(8,128)(2,1)S(1)}, bf16[160,1664]{1,0:T(8,128)(2,1)S(1)}, u32[]{:S(2)}, u32[]{:S(2)}) collective-permute-start(bf16[160,1664]{1,0:T(8,128)(2,1)S(1)} %row_piece.6), channel_id=1, source_target_pairs={{0,1},{1,0},{2,3},{3,2},{4,5},{5,4},{6,7},{7,6},{8,9},{9,8},{10,11... | collective-permute-start | bytes 1597448 | tf_op jit(solution)/shard_map/ppermute | solution.py:21
  62.1 19.2 %collective-permute-start.15 = (bf16[160,1664]{1,0:T(8,128)(2,1)S(1)}, bf16[160,1664]{1,0:T(8,128)(2,1)S(1)}, u32[]{:S(2)}, u32[]{:S(2)}) collective-permute-start(bf16[160,1664]{1,0:T(8,128)(2,1)S(1)} %row_piece.5), channel_id=1, source_target_pairs={{0,2},{1,3},{2,0},{3,1},{4,6},{5,7},{6,4},{7,5},{8,10},{9,11},{10,... | collective-permute-start | bytes 1597448 | tf_op jit(solution)/shard_map/ppermute | solution.py:21
  73.3 6.6 %copy-start.12 = (bf16[120,1536]{1,0:T(8,128)(2,1)S(1)}, bf16[120,1536]{1,0:T(8,128)(2,1)}, u32[]{:S(2)}) copy-start(bf16[120,1536]{1,0:T(8,128)(2,1)} %copy-done.11) | copy-start | bytes 1105924
  73.3 6.7 %copy-start.10 = (bf16[120,1536]{1,0:T(8,128)(2,1)S(1)}, bf16[120,1536]{1,0:T(8,128)(2,1)}, u32[]{:S(2)}) copy-start(bf16[120,1536]{1,0:T(8,128)(2,1)} %copy-done.9) | copy-start | bytes 1105924
  81.2 5.7 %copy-start.7 = (bf16[40,6144]{1,0:T(8,128)(2,1)S(1)}, bf16[40,6144]{1,0:T(8,128)(2,1)}, u32[]{:S(2)}) copy-start(bf16[40,6144]{1,0:T(8,128)(2,1)} %copy-done.6) | copy-start | bytes 1474564
  81.4 12.1 %collective-permute-start.17 = (bf16[40,1664]{1,0:T(8,128)(2,1)S(1)}, bf16[40,1664]{1,0:T(8,128)(2,1)S(1)}, u32[]{:S(2)}, u32[]{:S(2)}) collective-permute-start(bf16[40,1664]{1,0:T(8,128)(2,1)S(1)} %get-tuple-element.135), channel_id=1, source_target_pairs={{0,8},{8,0},{16,24},{24,16},{1,9},{9,1},{17,25},{25,17},{2,10},{10... | collective-permute-start | bytes 399368 | tf_op jit(solution)/shard_map/ppermute | solution.py:21
  83.5 11.3 %collective-permute-start.18 = (bf16[40,1664]{1,0:T(8,128)(2,1)S(1)}, bf16[40,1664]{1,0:T(8,128)(2,1)S(1)}, u32[]{:S(2)}, u32[]{:S(2)}) collective-permute-start(bf16[40,1664]{1,0:T(8,128)(2,1)S(1)} %get-tuple-element.136), channel_id=1, source_target_pairs={{0,16},{8,24},{16,0},{24,8},{1,17},{9,25},{17,1},{25,9},{2,18},{10... | collective-permute-start | bytes 399368 | tf_op jit(solution)/shard_map/ppermute | solution.py:21
  85.6 10.7 %copy-start.2 = (s32[128,2]{0,1:T(2,128)S(1)}, s32[128,2]{0,1:T(2,128)}, u32[]{:S(2)}) copy-start(s32[128,2]{0,1:T(2,128)} %param.9) | copy-start | bytes 3076
  85.6 10.7 %copy-start.3 = (f32[128,2]{0,1:T(2,128)S(1)}, f32[128,2]{0,1:T(2,128)}, u32[]{:S(2)}) copy-start(f32[128,2]{0,1:T(2,128)} %param.10) | copy-start | bytes 3076
  85.6 9.2 %collective-permute-start.19 = (bf16[40,1664]{1,0:T(8,128)(2,1)S(1)}, bf16[40,1664]{1,0:T(8,128)(2,1)S(1)}, u32[]{:S(2)}, u32[]{:S(2)}) collective-permute-start(bf16[40,1664]{1,0:T(8,128)(2,1)S(1)} %get-tuple-element.137), channel_id=1, source_target_pairs={{0,24},{8,16},{16,8},{24,0},{1,25},{9,17},{17,9},{25,1},{2,26},{10... | collective-permute-start | bytes 399368 | tf_op jit(solution)/shard_map/ppermute | solution.py:21
  87.0 10.6 %copy-start.1 = (bf16[128,6144]{1,0:T(8,128)(2,1)S(1)}, bf16[128,6144]{1,0:T(8,128)(2,1)}, u32[]{:S(2)}) copy-start(bf16[128,6144]{1,0:T(8,128)(2,1)} %param.8) | copy-start | bytes 4718596
  94.9 1.4 %collective-permute-start.20 = (bf16[40,1664]{1,0:T(8,128)(2,1)S(1)}, bf16[40,1664]{1,0:T(8,128)(2,1)S(1)}, u32[]{:S(2)}, u32[]{:S(2)}) collective-permute-start(bf16[40,1664]{1,0:T(8,128)(2,1)S(1)} %add_convert_fusion.half_ref), channel_id=1, source_target_pairs={{0,4},{4,0},{1,5},{5,1},{2,6},{6,2},{3,7},{7,3},{8,12},{12,8},{9,1... | collective-permute-start | bytes 399368 | tf_op jit(solution)/shard_map/ppermute | solution.py:21
  (2 other events, 2.4 us)

commit v5 on v4

--- a/solution.py
+++ b/solution.py
@@ -28,14 +28,12 @@
     return size
 
 
-def pick_of(expert_ids, expert, capacity):
-    tok_rows = expert_ids.shape[0]
-    chosen = (expert_ids == expert).astype(jnp.int32)
-    slot_index = (jnp.cumsum(chosen.reshape(-1)) - 1).reshape(tok_rows, 2)
+def pick_of(chosen, capacity):
+    named = jnp.sum(chosen, axis=1)
+    place = jnp.arange(chosen.shape[0], dtype=jnp.int32)
+    slot = jnp.sum(jnp.where(place[None, :] < place[:, None], named[None, :], 0), axis=1)
     columns = jnp.arange(capacity, dtype=jnp.int32)
-    return (
-        (chosen[:, :, None] == 1) & (slot_index[:, :, None] == columns[None, None, :])
-    ).astype(jnp.float32)
+    return (named[:, None] > 0) & (slot[:, None] == columns[None, :])
 
 
 def place_kernel(
@@ -240,6 +238,55 @@
     )(index.reshape(1), d_gate, d_up, slots, gate_mat, up_mat)
 
 
+def outer_kernel(left_ref, *refs):
+    count = (len(refs) - 2) // 2
+    rights, outs, held, sems = refs[:count], refs[count : 2 * count], refs[-2], refs[-1]
+    slots, block, _ = held.shape
+    copies = []
+    for i in range(outs[0].shape[0] // block):
+        left = left_ref[:, i * block : (i + 1) * block].T
+        for right, out in zip(rights, outs):
+            turn = len(copies)
+            slot = turn % slots
+            if turn >= slots:
+                copies[turn - slots].wait()
+            held[slot] = jnp.dot(left, right[...], preferred_element_type=jnp.float32).astype(
+                held.dtype
+            )
+            copy = pltpu.make_async_copy(
+                held.at[slot], out.at[pl.ds(i * block, block)], sems.at[slot]
+            )
+            copy.start()
+            copies.append(copy)
+    for copy in copies[-min(slots, len(copies)) :]:
+        copy.wait()
+
+
+def outer(left, *rights):
+    height, width = left.shape[1], rights[0].shape[1]
+    count = len(rights)
+    block = block_of(height, max(LANES, 256 * 1024 // width // LANES * LANES))
+    vmem = pl.BlockSpec(memory_space=pltpu.VMEM)
+    slots = min(8, count * height // block)
+    return pl.pallas_call(
+        outer_kernel,
+        in_specs=[vmem] * (1 + count),
+        out_specs=[pl.BlockSpec(memory_space=pltpu.HBM)] * count,
+        out_shape=[jax.ShapeDtypeStruct((height, width), jnp.bfloat16)] * count,
+        scratch_shapes=[
+            pltpu.VMEM((slots, block, width), jnp.bfloat16),
+            pltpu.SemaphoreType.DMA((slots,)),
+        ],
+        compiler_params=pltpu.CompilerParams(vmem_limit_bytes=2 * VMEM_LIMIT),
+        cost_estimate=pl.CostEstimate(
+            flops=4 * count * left.shape[0] * height * width,
+            transcendentals=0,
+            bytes_accessed=2 * count * height * width,
+        ),
+        name="outer",
+    )(left, *rights)
+
+
 def on_device(tokens, out_grad, expert_ids, gate_probs, w_gate, w_up, w_down):
     expert = lax.axis_index("exp")
     hid = lax.axis_index("hid")
@@ -250,9 +297,11 @@
     piece = model_width // hid_count
     bf16, f32 = jnp.bfloat16, jnp.float32
 
-    pick_own = pick_of(expert_ids, expert, capacity)
-    select_own = jnp.sum(pick_own, axis=1).astype(bf16)
-    weight_own = jnp.sum(pick_own * gate_probs[:, :, None], axis=(0, 1))
+    chosen = (expert_ids == expert).astype(jnp.int32)
+    pick_own = pick_of(chosen, capacity)
+    select_own = pick_own.astype(bf16)
+    probs = jnp.sum(chosen * gate_probs, axis=1)
+    weight_own = jnp.sum(jnp.where(pick_own, probs[:, None], 0.0), axis=0)
 
     def slots_of(x):
         return lax.dot_general(select_own, x, FIRST, preferred_element_type=f32)
@@ -357,8 +406,7 @@
     hidden, d_gate, d_up = after((hidden, d_gate, d_up), part)
     rows_e = whole(own_rows, after(row_parts, part))
     grads_e = whole(own_grads, after(grad_parts, part))
-    grad_gate = lax.dot_general(rows_e, d_gate, FIRST, preferred_element_type=f32).astype(bf16)
-    grad_up = lax.dot_general(rows_e, d_up, FIRST, preferred_element_type=f32).astype(bf16)
+    grad_gate, grad_up = outer(rows_e, d_gate, d_up)
     if len(received) == 3:
         part = part + received[0].astype(f32)
         received = after(received[1:], part)
@@ -367,15 +415,14 @@
     own_sum, *messages = whole_call(
         sum_kernel, "sum_step", [(block, f32)] + [(block, bf16)] * (seq_count - 1), None, part, *received
     )
-    grad_down = lax.dot_general(hidden, grads_e, FIRST, preferred_element_type=f32).astype(bf16)
+    (grad_down,) = outer(hidden, grads_e)
     arrived = [swap(message, "seq", k) for k, message in enumerate(messages, 1)]
     for part in after(arrived, grad_down):
         own_sum = own_sum + part.astype(f32)
 
     half = own_sum.astype(bf16)
     other_half = swap(half, "exp", 1)
-    pick_other = pick_of(expert_ids, 1 - expert, capacity)
-    select_other = jnp.sum(pick_other, axis=1).astype(bf16)
+    select_other = pick_of((expert_ids == 1 - expert).astype(jnp.int32), capacity).astype(bf16)
     d_tokens, d_gates = whole_call(
         place_kernel,
         "place_step",

time: 97.8 us -> 95.7 us (0.979)
  matrix products: 22.2 us -> 2.63 us
  Pallas kernels: 32.6 us -> 51.5 us
  local copies, waits for them, and re-layouts: 3.54 us -> 0.84 us
  waiting for transfers between devices: 6.17 us -> 8.04 us
    dot_general x3 -> x0, matrix products: 19.9 us -> none  [the longest x1 6.63 us: on_device(): lax.dot_general(rows_e, d_up, FIRST, preferred_element_type=f32)]
    pallas_call x0 -> x2, Pallas kernels: none -> 18.9 us  [outer(): pl.pallas_call(outer_kernel, in_specs=[vmem] * (1 + count), out_specs=[pl...]
    ppermute x21, waiting for transfers between devices: 6.17 us -> 8.04 us  [swap(): return lax.ppermute(x, axis, [(i, i ^ bits) for i in range(size)])]
    another operation x14 -> x2, local copies, waits for them, and re-layouts: 1.46 us -> 0.29 us
    reduce_sum x2 -> x5, other arithmetic: 0.83 us -> 1.86 us  [the longest x1 0.81 us: pick_of(): named = jnp.sum(chosen, axis=1)]
  transfers between devices with their start and end apart: 21 -> 21, of which waited for: 4 -> 6; matrix products, arithmetic and copies ran while one was open for 25% -> 4% of each run, Pallas kernels for 29% -> 49%
where the time goes in v5:
time: 95.7 us; the launch traced here: 95.5 us
  Pallas kernels  51.5 us (54%)
  starting transfers between devices  28.1 us (29%)
  waiting for transfers between devices  8.04 us (8%)
  other arithmetic  3.12 us (3%)
  matrix products  2.63 us (3%)
  between operations  1.21 us (1%)
    ppermute x21, starting transfers between devices, swap(): return lax.ppermute(x, axis, [(i, i ^ bits) for i in range(size)])  28.1 us
    pallas_call x2, Pallas kernels, outer(): pl.pallas_call(outer_kernel, in_specs=[vmem] * (1 + count), out_specs=[pl...  18.9 us
    pallas_call x10, Pallas kernels, whole_call(): pl.pallas_call(kernel, in_specs=[pl.BlockSpec(memory_space=pltpu.SMEM)] *...  10.5 us
    pallas_call x2, Pallas kernels, fetch(): pl.pallas_call(fetch_kernel, in_specs=[pl.BlockSpec(memory_space=pltpu.HB...  9.41 us
    ppermute x21, waiting for transfers between devices, swap(): return lax.ppermute(x, axis, [(i, i ^ bits) for i in range(size)])  8.04 us
    pallas_call x4, Pallas kernels, row_piece(): pl.pallas_call(piece_kernel, in_specs=[pl.BlockSpec(memory_space=pltpu.SM...  7.84 us
    pallas_call x1, Pallas kernels, fetch_columns(): pl.pallas_call(columns_kernel, in_specs=[pl.BlockSpec(memory_space=pltpu....  4.88 us
    dot_general x4, matrix products, slots_of(): return lax.dot_general(select_own, x, FIRST, preferred_element_type=f32)  2.63 us
  transfers between devices with their start and end apart: 21, of which 6 were waited for; matrix products, arithmetic and copies ran while one was open for 4% of the time, Pallas kernels for 49%

profile of v5, /device:TPU:0, one launch (start us, length us, event | category | flops | bytes accessed | tf_op | source)
XLA Modules:
  0.0 95.5 jit_solution(15071646597629301624)
XLA Ops:
  1.6 1.4 %convolution_convert_fusion.1 = bf16[40,1536]{1,0:T(8,128)(2,1)S(1)} fusion(bf16[128,6144]{1,0:T(8,128)(2,1)} %param.7, s32[]{:T(128)S(6)} %select_n.21, s32[128]{0:T(128)S(1)} %select_reduce_fusion.2, pred[128]{0:T(512)(128)(4,1)S(1)} %broadcast_compare_fusion.1), kind=kOutput, calls=%fused_computation.5 | convolution fusion | flops 15800320 | bytes 516740 | tf_op jit(solution)/shard_map/dot_general | solution.py:307
  3.0 4.1 %collective-permute-start.1 = (bf16[40,1536]{1,0:T(8,128)(2,1)S(1)}, bf16[40,1536]{1,0:T(8,128)(2,1)S(1)}, u32[]{:S(2)}, u32[]{:S(2)}) collective-permute-start(bf16[40,1536]{1,0:T(8,128)(2,1)S(1)} %convolution_convert_fusion.1), channel_id=1, source_target_pairs={{0,16},{8,24},{16,0},{24,8},{1,17},{9,25},{17,1},{25,9},{2,18},{10... | collective-permute-start | bytes 368648 | tf_op jit(solution)/shard_map/ppermute | solution.py:21
  7.1 1.6 %collective-permute-start = (bf16[40,1536]{1,0:T(8,128)(2,1)S(1)}, bf16[40,1536]{1,0:T(8,128)(2,1)S(1)}, u32[]{:S(2)}, u32[]{:S(2)}) collective-permute-start(bf16[40,1536]{1,0:T(8,128)(2,1)S(1)} %convolution_convert_fusion.1), channel_id=1, source_target_pairs={{0,8},{8,0},{16,24},{24,16},{1,9},{9,1},{17,25},{25,17},{2,10},{10... | collective-permute-start | bytes 368648 | tf_op jit(solution)/shard_map/ppermute | solution.py:21
  11.5 2.2 %collective-permute-done.1 = bf16[40,1536]{1,0:T(8,128)(2,1)S(1)} collective-permute-done((bf16[40,1536]{1,0:T(8,128)(2,1)S(1)}, bf16[40,1536]{1,0:T(8,128)(2,1)S(1)}, u32[]{:S(2)}, u32[]{:S(2)}) %collective-permute-start.1) | collective-permute-done | bytes 122912 | tf_op jit(solution)/shard_map/ppermute | solution.py:21
  14.9 4.7 %fetch.2.gate_ref = bf16[6144,1024]{1,0:T(8,128)(2,1)S(1)} custom-call(bf16[6144,1024]{1,0:T(8,128)(2,1)} %bitcast.18), custom_call_target="tpu_custom_call" | custom-call | tf_op jit(solution)/shard_map/fetch/pallas_call | solution.py:91
  21.4 1.6 %collective-permute-start.4 = (bf16[120,1536]{1,0:T(8,128)(2,1)S(1)}, bf16[120,1536]{1,0:T(8,128)(2,1)S(1)}, u32[]{:S(2)}, u32[]{:S(2)}) collective-permute-start(bf16[120,1536]{1,0:T(8,128)(2,1)S(1)} %constant_dynamic-update-slice_fusion), channel_id=1, source_target_pairs={{0,1},{1,0},{2,3},{3,2},{4,5},{5,4},{6,7},{7,6},{8,9},{9,8},{10,11... | collective-permute-start | bytes 1105928 | tf_op jit(solution)/shard_map/ppermute | solution.py:21
  23.0 1.5 %collective-permute-start.5 = (bf16[120,1536]{1,0:T(8,128)(2,1)S(1)}, bf16[120,1536]{1,0:T(8,128)(2,1)S(1)}, u32[]{:S(2)}, u32[]{:S(2)}) collective-permute-start(bf16[120,1536]{1,0:T(8,128)(2,1)S(1)} %constant_dynamic-update-slice_fusion), channel_id=1, source_target_pairs={{0,2},{1,3},{2,0},{3,1},{4,6},{5,7},{6,4},{7,5},{8,10},{9,11},{10,... | collective-permute-start | bytes 1105928 | tf_op jit(solution)/shard_map/ppermute | solution.py:21
  24.6 1.6 %collective-permute-start.10 = (bf16[120,1536]{1,0:T(8,128)(2,1)S(1)}, bf16[120,1536]{1,0:T(8,128)(2,1)S(1)}, u32[]{:S(2)}, u32[]{:S(2)}) collective-permute-start(bf16[120,1536]{1,0:T(8,128)(2,1)S(1)} %constant_dynamic-update-slice_fusion.3), channel_id=1, source_target_pairs={{0,1},{1,0},{2,3},{3,2},{4,5},{5,4},{6,7},{7,6},{8,9},{9,8},{10,11... | collective-permute-start | bytes 1105928 | tf_op jit(solution)/shard_map/ppermute | solution.py:21
  26.2 1.5 %collective-permute-start.11 = (bf16[120,1536]{1,0:T(8,128)(2,1)S(1)}, bf16[120,1536]{1,0:T(8,128)(2,1)S(1)}, u32[]{:S(2)}, u32[]{:S(2)}) collective-permute-start(bf16[120,1536]{1,0:T(8,128)(2,1)S(1)} %constant_dynamic-update-slice_fusion.3), channel_id=1, source_target_pairs={{0,2},{1,3},{2,0},{3,1},{4,6},{5,7},{6,4},{7,5},{8,10},{9,11},{10,... | collective-permute-start | bytes 1105928 | tf_op jit(solution)/shard_map/ppermute | solution.py:21
  27.7 4.7 %fetch.3.up_ref = bf16[6144,1024]{1,0:T(8,128)(2,1)S(1)} custom-call(bf16[6144,1024]{1,0:T(8,128)(2,1)} %bitcast.19), custom_call_target="tpu_custom_call" | custom-call | tf_op jit(solution)/shard_map/fetch/pallas_call | solution.py:91
  32.4 4.9 %fetch_columns.1 = (bf16[1024,1536]{1,0:T(8,128)(2,1)S(1)}, bf16[1024,1536]{1,0:T(8,128)(2,1)S(1)}, bf16[1024,1536]{1,0:T(8,128)(2,1)S(1)}, bf16[1024,1536]{1,0:T(8,128)(2,1)S(1)}) custom-call(s32[1]{0:T(128)} %bitcast.index_ref.piece_ref, bf16[1024,6144]{1,0:T(8,128)(2,1)} %bitcast.20), custom_call_target="tpu_custom_call" | custom-call | tf_op jit(solution)/shard_map/fetch_columns/pallas_call | solution.py:124
  38.4 1.2 %pair_step.4 = (f32[160,1024]{1,0:T(8,128)S(1)}, f32[160,1024]{1,0:T(8,128)S(1)}) custom-call(s32[1]{0:T(128)} %bitcast.index_ref.piece_ref, bf16[160,1536]{1,0:T(8,128)(2,1)S(1)} %pad_maximum_fusion.2.rows_ref, bf16[6144,1024]{1,0:T(8,128)(2,1)S(1)} %fetch.2.gate_ref, bf16[6144,1024]{1,0:T(8,128)(2,1)S(1)} %fetch.3.up_ref), custom_call_target="tpu_custom_call" | custom-call | tf_op jit(solution)/shard_map/pair_step/pallas_call | solution.py:184
  40.9 1.2 %pair_step.5 = (f32[160,1024]{1,0:T(8,128)S(1)}, f32[160,1024]{1,0:T(8,128)S(1)}) custom-call(s32[1]{0:T(128)} %bitcast.4.index_ref.piece_ref, bf16[160,1536]{1,0:T(8,128)(2,1)S(1)} %pad_maximum_fusion.4.rows_ref, bf16[6144,1024]{1,0:T(8,128)(2,1)S(1)} %fetch.2.gate_ref, bf16[6144,1024]{1,0:T(8,128)(2,1)S(1)} %fetch.3.up_ref, ...), custom_call_target="tpu_custom_call" | custom-call | tf_op jit(solution)/shard_map/pair_step/pallas_call | solution.py:184
  42.1 1.2 %pair_step.6 = (f32[160,1024]{1,0:T(8,128)S(1)}, f32[160,1024]{1,0:T(8,128)S(1)}) custom-call(s32[1]{0:T(128)} %bitcast.3.index_ref.piece_ref, bf16[160,1536]{1,0:T(8,128)(2,1)S(1)} %pad_maximum_fusion.3.rows_ref, bf16[6144,1024]{1,0:T(8,128)(2,1)S(1)} %fetch.2.gate_ref, bf16[6144,1024]{1,0:T(8,128)(2,1)S(1)} %fetch.3.up_ref, ...), custom_call_target="tpu_custom_call" | custom-call | tf_op jit(solution)/shard_map/pair_step/pallas_call | solution.py:184
  43.4 1.6 %collective-permute-start.12 = (bf16[64,1536]{1,0:T(8,128)(2,1)S(1)}, bf16[64,1536]{1,0:T(8,128)(2,1)S(1)}, u32[]{:S(2)}, u32[]{:S(2)}) collective-permute-start(bf16[64,1536]{1,0:T(8,128)(2,1)S(1)} %slice.17), channel_id=1, source_target_pairs={{0,2},{1,3},{2,0},{3,1},{4,6},{5,7},{6,4},{7,5},{8,10},{9,11},{10,... | collective-permute-start | bytes 589832 | tf_op jit(solution)/shard_map/ppermute | solution.py:21
  45.0 1.6 %collective-permute-start.13 = (bf16[56,1536]{1,0:T(8,128)(2,1)S(1)}, bf16[56,1536]{1,0:T(8,128)(2,1)S(1)}, u32[]{:S(2)}, u32[]{:S(2)}) collective-permute-start(bf16[56,1536]{1,0:T(8,128)(2,1)S(1)} %slice.18), channel_id=1, source_target_pairs={{0,1},{1,0},{2,3},{3,2},{4,5},{5,4},{6,7},{7,6},{8,9},{9,8},{10,11... | collective-permute-start | bytes 516104 | tf_op jit(solution)/shard_map/ppermute | solution.py:21
  48.7 1.2 %pair_step.7 = (f32[160,1024]{1,0:T(8,128)S(1)}, f32[160,1024]{1,0:T(8,128)S(1)}) custom-call(s32[1]{0:T(128)} %bitcast.6.index_ref.piece_ref, bf16[160,1536]{1,0:T(8,128)(2,1)S(1)} %pad_maximum_fusion.8.rows_ref, bf16[6144,1024]{1,0:T(8,128)(2,1)S(1)} %fetch.2.gate_ref, bf16[6144,1024]{1,0:T(8,128)(2,1)S(1)} %fetch.3.up_ref, ...), custom_call_target="tpu_custom_call" | custom-call | tf_op jit(solution)/shard_map/pair_step/pallas_call | solution.py:184
  50.5 1.3 %back_step.7 = (bf16[160,1024]{1,0:T(8,128)(2,1)S(1)}, bf16[160,1024]{1,0:T(8,128)(2,1)S(1)}, bf16[160,1024]{1,0:T(8,128)(2,1)S(1)}, f32[160,128]{1,0:T(8,128)S(1)}) custom-call(bf16[160,1536]{1,0:T(8,128)(2,1)S(1)} %pad_maximum_fusion.9.grads_ref, bf16[1024,1536]{1,0:T(8,128)(2,1)S(1)} %get-tuple-element.107.down_ref, f32[1024,160]{1,0:T(8,128)S(1)} %back_step.6.refs_0_, ...), custom_call_target="tpu_custom_call" | custom-call | tf_op jit(solution)/shard_map/back_step/pallas_call | solution.py:184
  51.9 1.9 %row_piece.4 = bf16[160,1664]{1,0:T(8,128)(2,1)S(1)} custom-call(s32[1]{0:T(128)} %bitcast.6.index_ref.piece_ref, bf16[160,1024]{1,0:T(8,128)(2,1)S(1)} %get-tuple-element.125.d_gate_ref.refs_0_, bf16[160,1024]{1,0:T(8,128)(2,1)S(1)} %get-tuple-element.126.d_up_ref.refs_1_, f32[160,128]{1,0:T(8,128)S(1)} %get-tuple-element.119.slot_ref, ...), custom_call_target="tpu_custom_call" | custom-call | flops 1006632960 | bytes 6946816 | tf_op jit(solution)/shard_map/row_piece/pallas_call | solution.py:226
  53.8 1.5 %collective-permute-start.14 = (bf16[160,1664]{1,0:T(8,128)(2,1)S(1)}, bf16[160,1664]{1,0:T(8,128)(2,1)S(1)}, u32[]{:S(2)}, u32[]{:S(2)}) collective-permute-start(bf16[160,1664]{1,0:T(8,128)(2,1)S(1)} %row_piece.4), channel_id=1, source_target_pairs={{0,3},{1,2},{2,1},{3,0},{4,7},{5,6},{6,5},{7,4},{8,11},{9,10},{10,... | collective-permute-start | bytes 1597448 | tf_op jit(solution)/shard_map/ppermute | solution.py:21
  55.3 2.1 %row_piece.5 = bf16[160,1664]{1,0:T(8,128)(2,1)S(1)} custom-call(s32[1]{0:T(128)} %bitcast.3.index_ref.piece_ref, bf16[160,1024]{1,0:T(8,128)(2,1)S(1)} %get-tuple-element.125.d_gate_ref.refs_0_, bf16[160,1024]{1,0:T(8,128)(2,1)S(1)} %get-tuple-element.126.d_up_ref.refs_1_, f32[160,128]{1,0:T(8,128)S(1)} %get-tuple-element.119.slot_ref, ...), custom_call_target="tpu_custom_call" | custom-call | flops 1006632960 | bytes 6946816 | tf_op jit(solution)/shard_map/row_piece/pallas_call | solution.py:226
  57.4 1.9 %row_piece.6 = bf16[160,1664]{1,0:T(8,128)(2,1)S(1)} custom-call(s32[1]{0:T(128)} %bitcast.4.index_ref.piece_ref, bf16[160,1024]{1,0:T(8,128)(2,1)S(1)} %get-tuple-element.125.d_gate_ref.refs_0_, bf16[160,1024]{1,0:T(8,128)(2,1)S(1)} %get-tuple-element.126.d_up_ref.refs_1_, f32[160,128]{1,0:T(8,128)S(1)} %get-tuple-element.119.slot_ref, ...), custom_call_target="tpu_custom_call" | custom-call | flops 1006632960 | bytes 6946816 | tf_op jit(solution)/shard_map/row_piece/pallas_call | solution.py:226
  59.8 1.5 %collective-permute-start.15 = (bf16[160,1664]{1,0:T(8,128)(2,1)S(1)}, bf16[160,1664]{1,0:T(8,128)(2,1)S(1)}, u32[]{:S(2)}, u32[]{:S(2)}) collective-permute-start(bf16[160,1664]{1,0:T(8,128)(2,1)S(1)} %row_piece.5), channel_id=1, source_target_pairs={{0,2},{1,3},{2,0},{3,1},{4,6},{5,7},{6,4},{7,5},{8,10},{9,11},{10,... | collective-permute-start | bytes 1597448 | tf_op jit(solution)/shard_map/ppermute | solution.py:21
  61.4 2.0 %row_piece.7 = f32[160,1664]{1,0:T(8,128)S(1)} custom-call(s32[1]{0:T(128)} %bitcast.index_ref.piece_ref, bf16[160,1024]{1,0:T(8,128)(2,1)S(1)} %get-tuple-element.125.d_gate_ref.refs_0_, bf16[160,1024]{1,0:T(8,128)(2,1)S(1)} %get-tuple-element.126.d_up_ref.refs_1_, f32[160,128]{1,0:T(8,128)S(1)} %get-tuple-element.119.slot_ref, ...), custom_call_target="tpu_custom_call" | custom-call | flops 1006632960 | bytes 6946816 | tf_op jit(solution)/shard_map/row_piece/pallas_call | solution.py:226
  64.2 13.6 %outer.2 = (bf16[6144,1024]{1,0:T(8,128)(2,1)}, bf16[6144,1024]{1,0:T(8,128)(2,1)}) custom-call(bf16[160,6144]{1,0:T(8,128)(2,1)S(1)} %pad_maximum_fusion.left_ref, bf16[160,1024]{1,0:T(8,128)(2,1)S(1)} %get-tuple-element.125.d_gate_ref.refs_0_, bf16[160,1024]{1,0:T(8,128)(2,1)S(1)} %get-tuple-element.126.d_up_ref.refs_1_), custom_call_target="tpu_custom_call" | custom-call | flops 8053063680 | bytes 25165824 | tf_op jit(solution)/shard_map/outer/pallas_call | solution.py:271
  78.6 1.2 %collective-permute-start.17 = (bf16[40,1664]{1,0:T(8,128)(2,1)S(1)}, bf16[40,1664]{1,0:T(8,128)(2,1)S(1)}, u32[]{:S(2)}, u32[]{:S(2)}) collective-permute-start(bf16[40,1664]{1,0:T(8,128)(2,1)S(1)} %get-tuple-element.139), channel_id=1, source_target_pairs={{0,8},{8,0},{16,24},{24,16},{1,9},{9,1},{17,25},{25,17},{2,10},{10... | collective-permute-start | bytes 399368 | tf_op jit(solution)/shard_map/ppermute | solution.py:21
  79.8 3.0 %collective-permute-start.18 = (bf16[40,1664]{1,0:T(8,128)(2,1)S(1)}, bf16[40,1664]{1,0:T(8,128)(2,1)S(1)}, u32[]{:S(2)}, u32[]{:S(2)}) collective-permute-start(bf16[40,1664]{1,0:T(8,128)(2,1)S(1)} %get-tuple-element.140), channel_id=1, source_target_pairs={{0,16},{8,24},{16,0},{24,8},{1,17},{9,25},{17,1},{25,9},{2,18},{10... | collective-permute-start | bytes 399368 | tf_op jit(solution)/shard_map/ppermute | solution.py:21
  82.8 1.4 %collective-permute-start.19 = (bf16[40,1664]{1,0:T(8,128)(2,1)S(1)}, bf16[40,1664]{1,0:T(8,128)(2,1)S(1)}, u32[]{:S(2)}, u32[]{:S(2)}) collective-permute-start(bf16[40,1664]{1,0:T(8,128)(2,1)S(1)} %get-tuple-element.141), channel_id=1, source_target_pairs={{0,24},{8,16},{16,8},{24,0},{1,25},{9,17},{17,9},{25,1},{2,26},{10... | collective-permute-start | bytes 399368 | tf_op jit(solution)/shard_map/ppermute | solution.py:21
  84.1 5.3 %outer.3 = bf16[1024,6144]{1,0:T(8,128)(2,1)} custom-call(bf16[160,1024]{1,0:T(8,128)(2,1)S(1)} %get-tuple-element.129.left_ref, bf16[160,6144]{1,0:T(8,128)(2,1)S(1)} %pad_maximum_fusion.1.refs_0_), custom_call_target="tpu_custom_call" | custom-call | flops 4026531840 | bytes 12582912 | tf_op jit(solution)/shard_map/outer/pallas_call | solution.py:271
  89.4 3.3 %collective-permute-done.18 = bf16[40,1664]{1,0:T(8,128)(2,1)S(1)} collective-permute-done((bf16[40,1664]{1,0:T(8,128)(2,1)S(1)}, bf16[40,1664]{1,0:T(8,128)(2,1)S(1)}, u32[]{:S(2)}, u32[]{:S(2)}) %collective-permute-start.18) | collective-permute-done | bytes 133152 | tf_op jit(solution)/shard_map/ppermute | solution.py:21
  93.0 1.2 %collective-permute-done.20.other_half_ref = bf16[40,1664]{1,0:T(8,128)(2,1)S(1)} collective-permute-done((bf16[40,1664]{1,0:T(8,128)(2,1)S(1)}, bf16[40,1664]{1,0:T(8,128)(2,1)S(1)}, u32[]{:S(2)}, u32[]{:S(2)}) %collective-permute-start.20) | collective-permute-done | bytes 133152 | tf_op jit(solution)/shard_map/ppermute | solution.py:21
  94.2 1.2 %place_step.1 = (f32[128,1536]{1,0:T(8,128)}, f32[2,128]{1,0:T(2,128)}) custom-call(s32[1]{0:T(128)} %bitcast.10.expert_ref, s32[2,128]{1,0:T(2,128)S(1)} %bitcast.16, f32[2,128]{1,0:T(2,128)S(1)} %bitcast.17, bf16[128,40]{1,0:T(8,128)(2,1)S(1)} %get-tuple-element.159.own_ref, bf16[128,40]{1,0:T(8,128)(2,1)S(1)} %get-tuple-element.160.other_ref, ...), custom_call_target="tpu_custom_call" | custom-call | tf_op jit(solution)/shard_map/place_step/pallas_call | solution.py:184
  (87 shorter events, 14.2 us)
Async XLA Ops:
  0.6 8.9 %copy-start = (bf16[128,6144]{1,0:T(8,128)(2,1)S(1)}, bf16[128,6144]{1,0:T(8,128)(2,1)}, u32[]{:S(2)}) copy-start(bf16[128,6144]{1,0:T(8,128)(2,1)} %param.8) | copy-start | bytes 4718596
  1.6 9.3 %copy-start.4 = (bf16[128,6144]{1,0:T(8,128)(2,1)S(1)}, bf16[128,6144]{1,0:T(8,128)(2,1)}, u32[]{:S(2)}) copy-start(bf16[128,6144]{1,0:T(8,128)(2,1)} %param.7) | copy-start | bytes 4718596
  3.0 10.7 %collective-permute-start.1 = (bf16[40,1536]{1,0:T(8,128)(2,1)S(1)}, bf16[40,1536]{1,0:T(8,128)(2,1)S(1)}, u32[]{:S(2)}, u32[]{:S(2)}) collective-permute-start(bf16[40,1536]{1,0:T(8,128)(2,1)S(1)} %convolution_convert_fusion.1), channel_id=1, source_target_pairs={{0,16},{8,24},{16,0},{24,8},{1,17},{9,25},{17,1},{25,9},{2,18},{10... | collective-permute-start | bytes 368648 | tf_op jit(solution)/shard_map/ppermute | solution.py:21
  7.1 13.5 %collective-permute-start = (bf16[40,1536]{1,0:T(8,128)(2,1)S(1)}, bf16[40,1536]{1,0:T(8,128)(2,1)S(1)}, u32[]{:S(2)}, u32[]{:S(2)}) collective-permute-start(bf16[40,1536]{1,0:T(8,128)(2,1)S(1)} %convolution_convert_fusion.1), channel_id=1, source_target_pairs={{0,8},{8,0},{16,24},{24,16},{1,9},{9,1},{17,25},{25,17},{2,10},{10... | collective-permute-start | bytes 368648 | tf_op jit(solution)/shard_map/ppermute | solution.py:21
  9.9 9.8 %collective-permute-start.3 = (bf16[40,1536]{1,0:T(8,128)(2,1)S(1)}, bf16[40,1536]{1,0:T(8,128)(2,1)S(1)}, u32[]{:S(2)}, u32[]{:S(2)}) collective-permute-start(bf16[40,1536]{1,0:T(8,128)(2,1)S(1)} %fusion.1), channel_id=1, source_target_pairs={{0,16},{8,24},{16,0},{24,8},{1,17},{9,25},{17,1},{25,9},{2,18},{10... | collective-permute-start | bytes 368648 | tf_op jit(solution)/shard_map/ppermute | solution.py:21
  10.3 14.2 %collective-permute-start.6 = (bf16[40,1536]{1,0:T(8,128)(2,1)S(1)}, bf16[40,1536]{1,0:T(8,128)(2,1)S(1)}, u32[]{:S(2)}, u32[]{:S(2)}) collective-permute-start(bf16[40,1536]{1,0:T(8,128)(2,1)S(1)} %fusion.1), channel_id=1, source_target_pairs={{0,8},{8,0},{16,24},{24,16},{1,9},{9,1},{17,25},{25,17},{2,10},{10... | collective-permute-start | bytes 368648 | tf_op jit(solution)/shard_map/ppermute | solution.py:21
  13.7 7.6 %collective-permute-start.2 = (bf16[40,1536]{1,0:T(8,128)(2,1)S(1)}, bf16[40,1536]{1,0:T(8,128)(2,1)S(1)}, u32[]{:S(2)}, u32[]{:S(2)}) collective-permute-start(bf16[40,1536]{1,0:T(8,128)(2,1)S(1)} %collective-permute-done.1), channel_id=1, source_target_pairs={{0,8},{8,0},{16,24},{24,16},{1,9},{9,1},{17,25},{25,17},{2,10},{10... | collective-permute-start | bytes 368648 | tf_op jit(solution)/shard_map/ppermute | solution.py:21
  19.6 4.9 %collective-permute-start.7 = (bf16[40,1536]{1,0:T(8,128)(2,1)S(1)}, bf16[40,1536]{1,0:T(8,128)(2,1)S(1)}, u32[]{:S(2)}, u32[]{:S(2)}) collective-permute-start(bf16[40,1536]{1,0:T(8,128)(2,1)S(1)} %collective-permute-done.3), channel_id=1, source_target_pairs={{0,8},{8,0},{16,24},{24,16},{1,9},{9,1},{17,25},{25,17},{2,10},{10... | collective-permute-start | bytes 368648 | tf_op jit(solution)/shard_map/ppermute | solution.py:21
  21.4 18.2 %collective-permute-start.4 = (bf16[120,1536]{1,0:T(8,128)(2,1)S(1)}, bf16[120,1536]{1,0:T(8,128)(2,1)S(1)}, u32[]{:S(2)}, u32[]{:S(2)}) collective-permute-start(bf16[120,1536]{1,0:T(8,128)(2,1)S(1)} %constant_dynamic-update-slice_fusion), channel_id=1, source_target_pairs={{0,1},{1,0},{2,3},{3,2},{4,5},{5,4},{6,7},{7,6},{8,9},{9,8},{10,11... | collective-permute-start | bytes 1105928 | tf_op jit(solution)/shard_map/ppermute | solution.py:21
  23.0 16.6 %collective-permute-start.5 = (bf16[120,1536]{1,0:T(8,128)(2,1)S(1)}, bf16[120,1536]{1,0:T(8,128)(2,1)S(1)}, u32[]{:S(2)}, u32[]{:S(2)}) collective-permute-start(bf16[120,1536]{1,0:T(8,128)(2,1)S(1)} %constant_dynamic-update-slice_fusion), channel_id=1, source_target_pairs={{0,2},{1,3},{2,0},{3,1},{4,6},{5,7},{6,4},{7,5},{8,10},{9,11},{10,... | collective-permute-start | bytes 1105928 | tf_op jit(solution)/shard_map/ppermute | solution.py:21
  24.6 18.7 %collective-permute-start.10 = (bf16[120,1536]{1,0:T(8,128)(2,1)S(1)}, bf16[120,1536]{1,0:T(8,128)(2,1)S(1)}, u32[]{:S(2)}, u32[]{:S(2)}) collective-permute-start(bf16[120,1536]{1,0:T(8,128)(2,1)S(1)} %constant_dynamic-update-slice_fusion.3), channel_id=1, source_target_pairs={{0,1},{1,0},{2,3},{3,2},{4,5},{5,4},{6,7},{7,6},{8,9},{9,8},{10,11... | collective-permute-start | bytes 1105928 | tf_op jit(solution)/shard_map/ppermute | solution.py:21
  26.2 17.1 %collective-permute-start.11 = (bf16[120,1536]{1,0:T(8,128)(2,1)S(1)}, bf16[120,1536]{1,0:T(8,128)(2,1)S(1)}, u32[]{:S(2)}, u32[]{:S(2)}) collective-permute-start(bf16[120,1536]{1,0:T(8,128)(2,1)S(1)} %constant_dynamic-update-slice_fusion.3), channel_id=1, source_target_pairs={{0,2},{1,3},{2,0},{3,1},{4,6},{5,7},{6,4},{7,5},{8,10},{9,11},{10,... | collective-permute-start | bytes 1105928 | tf_op jit(solution)/shard_map/ppermute | solution.py:21
  39.6 9.0 %collective-permute-start.8 = (bf16[64,1536]{1,0:T(8,128)(2,1)S(1)}, bf16[64,1536]{1,0:T(8,128)(2,1)S(1)}, u32[]{:S(2)}, u32[]{:S(2)}) collective-permute-start(bf16[64,1536]{1,0:T(8,128)(2,1)S(1)} %slice.15), channel_id=1, source_target_pairs={{0,2},{1,3},{2,0},{3,1},{4,6},{5,7},{6,4},{7,5},{8,10},{9,11},{10,... | collective-permute-start | bytes 589832 | tf_op jit(solution)/shard_map/ppermute | solution.py:21
  40.2 8.4 %collective-permute-start.9 = (bf16[56,1536]{1,0:T(8,128)(2,1)S(1)}, bf16[56,1536]{1,0:T(8,128)(2,1)S(1)}, u32[]{:S(2)}, u32[]{:S(2)}) collective-permute-start(bf16[56,1536]{1,0:T(8,128)(2,1)S(1)} %slice.16), channel_id=1, source_target_pairs={{0,1},{1,0},{2,3},{3,2},{4,5},{5,4},{6,7},{7,6},{8,9},{9,8},{10,11... | collective-permute-start | bytes 516104 | tf_op jit(solution)/shard_map/ppermute | solution.py:21
  43.4 6.5 %collective-permute-start.12 = (bf16[64,1536]{1,0:T(8,128)(2,1)S(1)}, bf16[64,1536]{1,0:T(8,128)(2,1)S(1)}, u32[]{:S(2)}, u32[]{:S(2)}) collective-permute-start(bf16[64,1536]{1,0:T(8,128)(2,1)S(1)} %slice.17), channel_id=1, source_target_pairs={{0,2},{1,3},{2,0},{3,1},{4,6},{5,7},{6,4},{7,5},{8,10},{9,11},{10,... | collective-permute-start | bytes 589832 | tf_op jit(solution)/shard_map/ppermute | solution.py:21
  45.0 5.5 %collective-permute-start.13 = (bf16[56,1536]{1,0:T(8,128)(2,1)S(1)}, bf16[56,1536]{1,0:T(8,128)(2,1)S(1)}, u32[]{:S(2)}, u32[]{:S(2)}) collective-permute-start(bf16[56,1536]{1,0:T(8,128)(2,1)S(1)} %slice.18), channel_id=1, source_target_pairs={{0,1},{1,0},{2,3},{3,2},{4,5},{5,4},{6,7},{7,6},{8,9},{9,8},{10,11... | collective-permute-start | bytes 516104 | tf_op jit(solution)/shard_map/ppermute | solution.py:21
  53.8 24.3 %collective-permute-start.14 = (bf16[160,1664]{1,0:T(8,128)(2,1)S(1)}, bf16[160,1664]{1,0:T(8,128)(2,1)S(1)}, u32[]{:S(2)}, u32[]{:S(2)}) collective-permute-start(bf16[160,1664]{1,0:T(8,128)(2,1)S(1)} %row_piece.4), channel_id=1, source_target_pairs={{0,3},{1,2},{2,1},{3,0},{4,7},{5,6},{6,5},{7,4},{8,11},{9,10},{10,... | collective-permute-start | bytes 1597448 | tf_op jit(solution)/shard_map/ppermute | solution.py:21
  59.3 19.1 %collective-permute-start.16 = (bf16[160,1664]{1,0:T(8,128)(2,1)S(1)}, bf16[160,1664]{1,0:T(8,128)(2,1)S(1)}, u32[]{:S(2)}, u32[]{:S(2)}) collective-permute-start(bf16[160,1664]{1,0:T(8,128)(2,1)S(1)} %row_piece.6), channel_id=1, source_target_pairs={{0,1},{1,0},{2,3},{3,2},{4,5},{5,4},{6,7},{7,6},{8,9},{9,8},{10,11... | collective-permute-start | bytes 1597448 | tf_op jit(solution)/shard_map/ppermute | solution.py:21
  59.8 18.5 %collective-permute-start.15 = (bf16[160,1664]{1,0:T(8,128)(2,1)S(1)}, bf16[160,1664]{1,0:T(8,128)(2,1)S(1)}, u32[]{:S(2)}, u32[]{:S(2)}) collective-permute-start(bf16[160,1664]{1,0:T(8,128)(2,1)S(1)} %row_piece.5), channel_id=1, source_target_pairs={{0,2},{1,3},{2,0},{3,1},{4,6},{5,7},{6,4},{7,5},{8,10},{9,11},{10,... | collective-permute-start | bytes 1597448 | tf_op jit(solution)/shard_map/ppermute | solution.py:21
  78.6 10.9 %collective-permute-start.17 = (bf16[40,1664]{1,0:T(8,128)(2,1)S(1)}, bf16[40,1664]{1,0:T(8,128)(2,1)S(1)}, u32[]{:S(2)}, u32[]{:S(2)}) collective-permute-start(bf16[40,1664]{1,0:T(8,128)(2,1)S(1)} %get-tuple-element.139), channel_id=1, source_target_pairs={{0,8},{8,0},{16,24},{24,16},{1,9},{9,1},{17,25},{25,17},{2,10},{10... | collective-permute-start | bytes 399368 | tf_op jit(solution)/shard_map/ppermute | solution.py:21
  79.8 13.0 %collective-permute-start.18 = (bf16[40,1664]{1,0:T(8,128)(2,1)S(1)}, bf16[40,1664]{1,0:T(8,128)(2,1)S(1)}, u32[]{:S(2)}, u32[]{:S(2)}) collective-permute-start(bf16[40,1664]{1,0:T(8,128)(2,1)S(1)} %get-tuple-element.140), channel_id=1, source_target_pairs={{0,16},{8,24},{16,0},{24,8},{1,17},{9,25},{17,1},{25,9},{2,18},{10... | collective-permute-start | bytes 399368 | tf_op jit(solution)/shard_map/ppermute | solution.py:21
  82.7 11.5 %copy-start.2 = (s32[128,2]{0,1:T(2,128)S(1)}, s32[128,2]{0,1:T(2,128)}, u32[]{:S(2)}) copy-start(s32[128,2]{0,1:T(2,128)} %param.9) | copy-start | bytes 3076
  82.8 11.5 %copy-start.3 = (f32[128,2]{0,1:T(2,128)S(1)}, f32[128,2]{0,1:T(2,128)}, u32[]{:S(2)}) copy-start(f32[128,2]{0,1:T(2,128)} %param.10) | copy-start | bytes 3076
  82.8 10.0 %collective-permute-start.19 = (bf16[40,1664]{1,0:T(8,128)(2,1)S(1)}, bf16[40,1664]{1,0:T(8,128)(2,1)S(1)}, u32[]{:S(2)}, u32[]{:S(2)}) collective-permute-start(bf16[40,1664]{1,0:T(8,128)(2,1)S(1)} %get-tuple-element.141), channel_id=1, source_target_pairs={{0,24},{8,16},{16,8},{24,0},{1,25},{9,17},{17,9},{25,1},{2,26},{10... | collective-permute-start | bytes 399368 | tf_op jit(solution)/shard_map/ppermute | solution.py:21
  84.1 11.3 %copy-start.1 = (bf16[128,6144]{1,0:T(8,128)(2,1)S(1)}, bf16[128,6144]{1,0:T(8,128)(2,1)}, u32[]{:S(2)}) copy-start(bf16[128,6144]{1,0:T(8,128)(2,1)} %param.8) | copy-start | bytes 4718596
  92.8 1.4 %collective-permute-start.20 = (bf16[40,1664]{1,0:T(8,128)(2,1)S(1)}, bf16[40,1664]{1,0:T(8,128)(2,1)S(1)}, u32[]{:S(2)}, u32[]{:S(2)}) collective-permute-start(bf16[40,1664]{1,0:T(8,128)(2,1)S(1)} %add_convert_fusion.half_ref), channel_id=1, source_target_pairs={{0,4},{4,0},{1,5},{5,1},{2,6},{6,2},{3,7},{7,3},{8,12},{12,8},{9,1... | collective-permute-start | bytes 399368 | tf_op jit(solution)/shard_map/ppermute | solution.py:21

commit v6 on v5

--- a/solution.py
+++ b/solution.py
@@ -406,18 +406,19 @@
     hidden, d_gate, d_up = after((hidden, d_gate, d_up), part)
     rows_e = whole(own_rows, after(row_parts, part))
     grads_e = whole(own_grads, after(grad_parts, part))
-    grad_gate, grad_up = outer(rows_e, d_gate, d_up)
+    (grad_gate,) = outer(rows_e, d_gate)
+    (grad_down,) = outer(hidden, grads_e)
     if len(received) == 3:
         part = part + received[0].astype(f32)
         received = after(received[1:], part)
-    received = after(received, (grad_gate, grad_up))
+    received = after(received, (grad_gate, grad_down))
     block = (capacity, piece + LANES)
     own_sum, *messages = whole_call(
         sum_kernel, "sum_step", [(block, f32)] + [(block, bf16)] * (seq_count - 1), None, part, *received
     )
-    (grad_down,) = outer(hidden, grads_e)
+    (grad_up,) = outer(rows_e, d_up)
     arrived = [swap(message, "seq", k) for k, message in enumerate(messages, 1)]
-    for part in after(arrived, grad_down):
+    for part in after(arrived, grad_up):
         own_sum = own_sum + part.astype(f32)
 
     half = own_sum.astype(bf16)

time: 95.7 us -> 94.6 us (0.989)
  waiting for transfers between devices: 8.04 us -> 6.38 us
    ppermute x21, waiting for transfers between devices: 8.04 us -> 6.38 us  [swap(): return lax.ppermute(x, axis, [(i, i ^ bits) for i in range(size)])]
    pallas_call x2 -> x3, Pallas kernels: 18.9 us -> 19 us  [outer(): pl.pallas_call(outer_kernel, in_specs=[vmem] * (1 + count), out_specs=[pl...]
  transfers between devices with their start and end apart: 21 -> 21, of which waited for: 6 -> 7; matrix products, arithmetic and copies ran while one was open for 4% -> 5% of each run, Pallas kernels for 49% -> 50%
where the time goes in v6:
time: 94.6 us; the launch traced here: 94.4 us
  Pallas kernels  51.6 us (55%)
  starting transfers between devices  27.9 us (29%)
  waiting for transfers between devices  6.38 us (7%)
  other arithmetic  3.86 us (4%)
  matrix products  2.63 us (3%)
  between operations  1.2 us (1%)
    ppermute x21, starting transfers between devices, swap(): return lax.ppermute(x, axis, [(i, i ^ bits) for i in range(size)])  27.9 us
    pallas_call x3, Pallas kernels, outer(): pl.pallas_call(outer_kernel, in_specs=[vmem] * (1 + count), out_specs=[pl...  19 us
    pallas_call x10, Pallas kernels, whole_call(): pl.pallas_call(kernel, in_specs=[pl.BlockSpec(memory_space=pltpu.SMEM)] *...  10.5 us
    pallas_call x2, Pallas kernels, fetch(): pl.pallas_call(fetch_kernel, in_specs=[pl.BlockSpec(memory_space=pltpu.HB...  9.41 us
    pallas_call x4, Pallas kernels, row_piece(): pl.pallas_call(piece_kernel, in_specs=[pl.BlockSpec(memory_space=pltpu.SM...  7.85 us
    ppermute x21, waiting for transfers between devices, swap(): return lax.ppermute(x, axis, [(i, i ^ bits) for i in range(size)])  6.38 us
    pallas_call x1, Pallas kernels, fetch_columns(): pl.pallas_call(columns_kernel, in_specs=[pl.BlockSpec(memory_space=pltpu....  4.88 us
    dot_general x4, matrix products, slots_of(): return lax.dot_general(select_own, x, FIRST, preferred_element_type=f32)  2.63 us
  transfers between devices with their start and end apart: 21, of which 7 were waited for; matrix products, arithmetic and copies ran while one was open for 5% of the time, Pallas kernels for 50%

profile of v6, /device:TPU:0, one launch (start us, length us, event | category | flops | bytes accessed | tf_op | source)
XLA Modules:
  0.0 94.4 jit_solution(14821188014659183789)
XLA Ops:
  1.6 1.4 %convolution_convert_fusion.1 = bf16[40,1536]{1,0:T(8,128)(2,1)S(1)} fusion(bf16[128,6144]{1,0:T(8,128)(2,1)} %param.7, s32[]{:T(128)S(6)} %select_n.21, s32[128]{0:T(128)S(1)} %select_reduce_fusion.2, pred[128]{0:T(512)(128)(4,1)S(1)} %broadcast_compare_fusion.1), kind=kOutput, calls=%fused_computation.5 | convolution fusion | flops 15800320 | bytes 516740 | tf_op jit(solution)/shard_map/dot_general | solution.py:307
  3.0 4.1 %collective-permute-start.1 = (bf16[40,1536]{1,0:T(8,128)(2,1)S(1)}, bf16[40,1536]{1,0:T(8,128)(2,1)S(1)}, u32[]{:S(2)}, u32[]{:S(2)}) collective-permute-start(bf16[40,1536]{1,0:T(8,128)(2,1)S(1)} %convolution_convert_fusion.1), channel_id=1, source_target_pairs={{0,16},{8,24},{16,0},{24,8},{1,17},{9,25},{17,1},{25,9},{2,18},{10... | collective-permute-start | bytes 368648 | tf_op jit(solution)/shard_map/ppermute | solution.py:21
  7.1 1.6 %collective-permute-start = (bf16[40,1536]{1,0:T(8,128)(2,1)S(1)}, bf16[40,1536]{1,0:T(8,128)(2,1)S(1)}, u32[]{:S(2)}, u32[]{:S(2)}) collective-permute-start(bf16[40,1536]{1,0:T(8,128)(2,1)S(1)} %convolution_convert_fusion.1), channel_id=1, source_target_pairs={{0,8},{8,0},{16,24},{24,16},{1,9},{9,1},{17,25},{25,17},{2,10},{10... | collective-permute-start | bytes 368648 | tf_op jit(solution)/shard_map/ppermute | solution.py:21
  11.5 2.2 %collective-permute-done.1 = bf16[40,1536]{1,0:T(8,128)(2,1)S(1)} collective-permute-done((bf16[40,1536]{1,0:T(8,128)(2,1)S(1)}, bf16[40,1536]{1,0:T(8,128)(2,1)S(1)}, u32[]{:S(2)}, u32[]{:S(2)}) %collective-permute-start.1) | collective-permute-done | bytes 122912 | tf_op jit(solution)/shard_map/ppermute | solution.py:21
  14.9 4.7 %fetch.2.gate_ref = bf16[6144,1024]{1,0:T(8,128)(2,1)S(1)} custom-call(bf16[6144,1024]{1,0:T(8,128)(2,1)} %bitcast.18), custom_call_target="tpu_custom_call" | custom-call | tf_op jit(solution)/shard_map/fetch/pallas_call | solution.py:91
  21.4 1.6 %collective-permute-start.4 = (bf16[120,1536]{1,0:T(8,128)(2,1)S(1)}, bf16[120,1536]{1,0:T(8,128)(2,1)S(1)}, u32[]{:S(2)}, u32[]{:S(2)}) collective-permute-start(bf16[120,1536]{1,0:T(8,128)(2,1)S(1)} %constant_dynamic-update-slice_fusion), channel_id=1, source_target_pairs={{0,1},{1,0},{2,3},{3,2},{4,5},{5,4},{6,7},{7,6},{8,9},{9,8},{10,11... | collective-permute-start | bytes 1105928 | tf_op jit(solution)/shard_map/ppermute | solution.py:21
  23.0 1.5 %collective-permute-start.5 = (bf16[120,1536]{1,0:T(8,128)(2,1)S(1)}, bf16[120,1536]{1,0:T(8,128)(2,1)S(1)}, u32[]{:S(2)}, u32[]{:S(2)}) collective-permute-start(bf16[120,1536]{1,0:T(8,128)(2,1)S(1)} %constant_dynamic-update-slice_fusion), channel_id=1, source_target_pairs={{0,2},{1,3},{2,0},{3,1},{4,6},{5,7},{6,4},{7,5},{8,10},{9,11},{10,... | collective-permute-start | bytes 1105928 | tf_op jit(solution)/shard_map/ppermute | solution.py:21
  24.6 1.6 %collective-permute-start.10 = (bf16[120,1536]{1,0:T(8,128)(2,1)S(1)}, bf16[120,1536]{1,0:T(8,128)(2,1)S(1)}, u32[]{:S(2)}, u32[]{:S(2)}) collective-permute-start(bf16[120,1536]{1,0:T(8,128)(2,1)S(1)} %constant_dynamic-update-slice_fusion.3), channel_id=1, source_target_pairs={{0,1},{1,0},{2,3},{3,2},{4,5},{5,4},{6,7},{7,6},{8,9},{9,8},{10,11... | collective-permute-start | bytes 1105928 | tf_op jit(solution)/shard_map/ppermute | solution.py:21
  26.2 1.5 %collective-permute-start.11 = (bf16[120,1536]{1,0:T(8,128)(2,1)S(1)}, bf16[120,1536]{1,0:T(8,128)(2,1)S(1)}, u32[]{:S(2)}, u32[]{:S(2)}) collective-permute-start(bf16[120,1536]{1,0:T(8,128)(2,1)S(1)} %constant_dynamic-update-slice_fusion.3), channel_id=1, source_target_pairs={{0,2},{1,3},{2,0},{3,1},{4,6},{5,7},{6,4},{7,5},{8,10},{9,11},{10,... | collective-permute-start | bytes 1105928 | tf_op jit(solution)/shard_map/ppermute | solution.py:21
  27.7 4.7 %fetch.3.up_ref = bf16[6144,1024]{1,0:T(8,128)(2,1)S(1)} custom-call(bf16[6144,1024]{1,0:T(8,128)(2,1)} %bitcast.19), custom_call_target="tpu_custom_call" | custom-call | tf_op jit(solution)/shard_map/fetch/pallas_call | solution.py:91
  32.4 4.9 %fetch_columns.1 = (bf16[1024,1536]{1,0:T(8,128)(2,1)S(1)}, bf16[1024,1536]{1,0:T(8,128)(2,1)S(1)}, bf16[1024,1536]{1,0:T(8,128)(2,1)S(1)}, bf16[1024,1536]{1,0:T(8,128)(2,1)S(1)}) custom-call(s32[1]{0:T(128)} %bitcast.index_ref.piece_ref, bf16[1024,6144]{1,0:T(8,128)(2,1)} %bitcast.20), custom_call_target="tpu_custom_call" | custom-call | tf_op jit(solution)/shard_map/fetch_columns/pallas_call | solution.py:124
  38.4 1.2 %pair_step.4 = (f32[160,1024]{1,0:T(8,128)S(1)}, f32[160,1024]{1,0:T(8,128)S(1)}) custom-call(s32[1]{0:T(128)} %bitcast.index_ref.piece_ref, bf16[160,1536]{1,0:T(8,128)(2,1)S(1)} %pad_maximum_fusion.2.rows_ref, bf16[6144,1024]{1,0:T(8,128)(2,1)S(1)} %fetch.2.gate_ref, bf16[6144,1024]{1,0:T(8,128)(2,1)S(1)} %fetch.3.up_ref), custom_call_target="tpu_custom_call" | custom-call | tf_op jit(solution)/shard_map/pair_step/pallas_call | solution.py:184
  39.7 1.2 %pair_step.5 = (f32[160,1024]{1,0:T(8,128)S(1)}, f32[160,1024]{1,0:T(8,128)S(1)}) custom-call(s32[1]{0:T(128)} %bitcast.4.index_ref.piece_ref, bf16[160,1536]{1,0:T(8,128)(2,1)S(1)} %pad_maximum_fusion.4.rows_ref, bf16[6144,1024]{1,0:T(8,128)(2,1)S(1)} %fetch.2.gate_ref, bf16[6144,1024]{1,0:T(8,128)(2,1)S(1)} %fetch.3.up_ref, ...), custom_call_target="tpu_custom_call" | custom-call | tf_op jit(solution)/shard_map/pair_step/pallas_call | solution.py:184
  41.0 1.2 %pair_step.6 = (f32[160,1024]{1,0:T(8,128)S(1)}, f32[160,1024]{1,0:T(8,128)S(1)}) custom-call(s32[1]{0:T(128)} %bitcast.3.index_ref.piece_ref, bf16[160,1536]{1,0:T(8,128)(2,1)S(1)} %pad_maximum_fusion.3.rows_ref, bf16[6144,1024]{1,0:T(8,128)(2,1)S(1)} %fetch.2.gate_ref, bf16[6144,1024]{1,0:T(8,128)(2,1)S(1)} %fetch.3.up_ref, ...), custom_call_target="tpu_custom_call" | custom-call | tf_op jit(solution)/shard_map/pair_step/pallas_call | solution.py:184
  43.4 1.6 %collective-permute-start.12 = (bf16[64,1536]{1,0:T(8,128)(2,1)S(1)}, bf16[64,1536]{1,0:T(8,128)(2,1)S(1)}, u32[]{:S(2)}, u32[]{:S(2)}) collective-permute-start(bf16[64,1536]{1,0:T(8,128)(2,1)S(1)} %slice.17), channel_id=1, source_target_pairs={{0,2},{1,3},{2,0},{3,1},{4,6},{5,7},{6,4},{7,5},{8,10},{9,11},{10,... | collective-permute-start | bytes 589832 | tf_op jit(solution)/shard_map/ppermute | solution.py:21
  45.0 1.6 %collective-permute-start.13 = (bf16[56,1536]{1,0:T(8,128)(2,1)S(1)}, bf16[56,1536]{1,0:T(8,128)(2,1)S(1)}, u32[]{:S(2)}, u32[]{:S(2)}) collective-permute-start(bf16[56,1536]{1,0:T(8,128)(2,1)S(1)} %slice.18), channel_id=1, source_target_pairs={{0,1},{1,0},{2,3},{3,2},{4,5},{5,4},{6,7},{7,6},{8,9},{9,8},{10,11... | collective-permute-start | bytes 516104 | tf_op jit(solution)/shard_map/ppermute | solution.py:21
  48.8 1.2 %pair_step.7 = (f32[160,1024]{1,0:T(8,128)S(1)}, f32[160,1024]{1,0:T(8,128)S(1)}) custom-call(s32[1]{0:T(128)} %bitcast.6.index_ref.piece_ref, bf16[160,1536]{1,0:T(8,128)(2,1)S(1)} %pad_maximum_fusion.8.rows_ref, bf16[6144,1024]{1,0:T(8,128)(2,1)S(1)} %fetch.2.gate_ref, bf16[6144,1024]{1,0:T(8,128)(2,1)S(1)} %fetch.3.up_ref, ...), custom_call_target="tpu_custom_call" | custom-call | tf_op jit(solution)/shard_map/pair_step/pallas_call | solution.py:184
  50.9 1.3 %back_step.7 = (bf16[160,1024]{1,0:T(8,128)(2,1)S(1)}, bf16[160,1024]{1,0:T(8,128)(2,1)S(1)}, bf16[160,1024]{1,0:T(8,128)(2,1)S(1)}, f32[160,128]{1,0:T(8,128)S(1)}) custom-call(bf16[160,1536]{1,0:T(8,128)(2,1)S(1)} %pad_maximum_fusion.9.grads_ref, bf16[1024,1536]{1,0:T(8,128)(2,1)S(1)} %get-tuple-element.105.down_ref, f32[1024,160]{1,0:T(8,128)S(1)} %back_step.6.refs_0_, ...), custom_call_target="tpu_custom_call" | custom-call | tf_op jit(solution)/shard_map/back_step/pallas_call | solution.py:184
  52.2 1.9 %row_piece.4 = bf16[160,1664]{1,0:T(8,128)(2,1)S(1)} custom-call(s32[1]{0:T(128)} %bitcast.6.index_ref.piece_ref, bf16[160,1024]{1,0:T(8,128)(2,1)S(1)} %get-tuple-element.123.d_gate_ref.refs_0_, bf16[160,1024]{1,0:T(8,128)(2,1)S(1)} %get-tuple-element.124.d_up_ref.refs_0_, f32[160,128]{1,0:T(8,128)S(1)} %get-tuple-element.117.slot_ref, ...), custom_call_target="tpu_custom_call" | custom-call | flops 1006632960 | bytes 6946816 | tf_op jit(solution)/shard_map/row_piece/pallas_call | solution.py:226
  54.1 1.2 %collective-permute-start.14 = (bf16[160,1664]{1,0:T(8,128)(2,1)S(1)}, bf16[160,1664]{1,0:T(8,128)(2,1)}, u32[]{:S(2)}, u32[]{:S(2)}) collective-permute-start(bf16[160,1664]{1,0:T(8,128)(2,1)S(1)} %row_piece.4), channel_id=1, source_target_pairs={{0,3},{1,2},{2,1},{3,0},{4,7},{5,6},{6,5},{7,4},{8,11},{9,10},{10,... | collective-permute-start | bytes 1597448 | tf_op jit(solution)/shard_map/ppermute | solution.py:21
  55.3 2.1 %row_piece.5 = bf16[160,1664]{1,0:T(8,128)(2,1)S(1)} custom-call(s32[1]{0:T(128)} %bitcast.3.index_ref.piece_ref, bf16[160,1024]{1,0:T(8,128)(2,1)S(1)} %get-tuple-element.123.d_gate_ref.refs_0_, bf16[160,1024]{1,0:T(8,128)(2,1)S(1)} %get-tuple-element.124.d_up_ref.refs_0_, f32[160,128]{1,0:T(8,128)S(1)} %get-tuple-element.117.slot_ref, ...), custom_call_target="tpu_custom_call" | custom-call | flops 1006632960 | bytes 6946816 | tf_op jit(solution)/shard_map/row_piece/pallas_call | solution.py:226
  57.4 1.9 %row_piece.6 = bf16[160,1664]{1,0:T(8,128)(2,1)S(1)} custom-call(s32[1]{0:T(128)} %bitcast.4.index_ref.piece_ref, bf16[160,1024]{1,0:T(8,128)(2,1)S(1)} %get-tuple-element.123.d_gate_ref.refs_0_, bf16[160,1024]{1,0:T(8,128)(2,1)S(1)} %get-tuple-element.124.d_up_ref.refs_0_, f32[160,128]{1,0:T(8,128)S(1)} %get-tuple-element.117.slot_ref, ...), custom_call_target="tpu_custom_call" | custom-call | flops 1006632960 | bytes 6946816 | tf_op jit(solution)/shard_map/row_piece/pallas_call | solution.py:226
  60.4 1.4 %collective-permute-start.15 = (bf16[160,1664]{1,0:T(8,128)(2,1)S(1)}, bf16[160,1664]{1,0:T(8,128)(2,1)S(1)}, u32[]{:S(2)}, u32[]{:S(2)}) collective-permute-start(bf16[160,1664]{1,0:T(8,128)(2,1)S(1)} %row_piece.5), channel_id=1, source_target_pairs={{0,2},{1,3},{2,0},{3,1},{4,6},{5,7},{6,4},{7,5},{8,10},{9,11},{10,... | collective-permute-start | bytes 1597448 | tf_op jit(solution)/shard_map/ppermute | solution.py:21
  61.7 2.0 %row_piece.7 = f32[160,1664]{1,0:T(8,128)S(1)} custom-call(s32[1]{0:T(128)} %bitcast.index_ref.piece_ref, bf16[160,1024]{1,0:T(8,128)(2,1)S(1)} %get-tuple-element.123.d_gate_ref.refs_0_, bf16[160,1024]{1,0:T(8,128)(2,1)S(1)} %get-tuple-element.124.d_up_ref.refs_0_, f32[160,128]{1,0:T(8,128)S(1)} %get-tuple-element.117.slot_ref, ...), custom_call_target="tpu_custom_call" | custom-call | flops 1006632960 | bytes 6946816 | tf_op jit(solution)/shard_map/row_piece/pallas_call | solution.py:226
  64.7 5.3 %outer.5 = bf16[1024,6144]{1,0:T(8,128)(2,1)} custom-call(bf16[160,1024]{1,0:T(8,128)(2,1)S(1)} %get-tuple-element.125.left_ref, bf16[160,6144]{1,0:T(8,128)(2,1)S(1)} %get-tuple-element.154.refs_0_), custom_call_target="tpu_custom_call" | custom-call | flops 4026531840 | bytes 12582912 | tf_op jit(solution)/shard_map/outer/pallas_call | solution.py:271
  69.9 6.7 %outer.3 = bf16[6144,1024]{1,0:T(8,128)(2,1)} custom-call(bf16[160,6144]{1,0:T(8,128)(2,1)S(1)} %get-tuple-element.153.left_ref, bf16[160,1024]{1,0:T(8,128)(2,1)S(1)} %get-tuple-element.123.d_gate_ref.refs_0_), custom_call_target="tpu_custom_call" | custom-call | flops 4026531840 | bytes 12582912 | tf_op jit(solution)/shard_map/outer/pallas_call | solution.py:271
  78.1 1.2 %collective-permute-start.17 = (bf16[40,1664]{1,0:T(8,128)(2,1)S(1)}, bf16[40,1664]{1,0:T(8,128)(2,1)S(1)}, u32[]{:S(2)}, u32[]{:S(2)}) collective-permute-start(bf16[40,1664]{1,0:T(8,128)(2,1)S(1)} %get-tuple-element.135), channel_id=1, source_target_pairs={{0,8},{8,0},{16,24},{24,16},{1,9},{9,1},{17,25},{25,17},{2,10},{10... | collective-permute-start | bytes 399368 | tf_op jit(solution)/shard_map/ppermute | solution.py:21
  79.3 3.0 %collective-permute-start.18 = (bf16[40,1664]{1,0:T(8,128)(2,1)S(1)}, bf16[40,1664]{1,0:T(8,128)(2,1)S(1)}, u32[]{:S(2)}, u32[]{:S(2)}) collective-permute-start(bf16[40,1664]{1,0:T(8,128)(2,1)S(1)} %get-tuple-element.136), channel_id=1, source_target_pairs={{0,16},{8,24},{16,0},{24,8},{1,17},{9,25},{17,1},{25,9},{2,18},{10... | collective-permute-start | bytes 399368 | tf_op jit(solution)/shard_map/ppermute | solution.py:21
  83.5 7.0 %outer.4 = bf16[6144,1024]{1,0:T(8,128)(2,1)} custom-call(bf16[160,6144]{1,0:T(8,128)(2,1)S(1)} %get-tuple-element.153.left_ref, bf16[160,1024]{1,0:T(8,128)(2,1)S(1)} %get-tuple-element.124.d_up_ref.refs_0_), custom_call_target="tpu_custom_call" | custom-call | flops 4026531840 | bytes 12582912 | tf_op jit(solution)/shard_map/outer/pallas_call | solution.py:271
  90.5 1.2 %collective-permute-done.18 = bf16[40,1664]{1,0:T(8,128)(2,1)S(1)} collective-permute-done((bf16[40,1664]{1,0:T(8,128)(2,1)S(1)}, bf16[40,1664]{1,0:T(8,128)(2,1)S(1)}, u32[]{:S(2)}, u32[]{:S(2)}) %collective-permute-start.18) | collective-permute-done | bytes 133152 | tf_op jit(solution)/shard_map/ppermute | solution.py:21
  92.0 1.2 %collective-permute-done.20.other_half_ref = bf16[40,1664]{1,0:T(8,128)(2,1)S(1)} collective-permute-done((bf16[40,1664]{1,0:T(8,128)(2,1)S(1)}, bf16[40,1664]{1,0:T(8,128)(2,1)S(1)}, u32[]{:S(2)}, u32[]{:S(2)}) %collective-permute-start.20) | collective-permute-done | bytes 133152 | tf_op jit(solution)/shard_map/ppermute | solution.py:21
  93.2 1.2 %place_step.1 = (f32[128,1536]{1,0:T(8,128)}, f32[2,128]{1,0:T(2,128)}) custom-call(s32[1]{0:T(128)} %bitcast.10.expert_ref, s32[2,128]{1,0:T(2,128)S(1)} %bitcast.16, f32[2,128]{1,0:T(2,128)S(1)} %bitcast.17, bf16[128,40]{1,0:T(8,128)(2,1)S(1)} %get-tuple-element.155.own_ref, bf16[128,40]{1,0:T(8,128)(2,1)S(1)} %get-tuple-element.156.other_ref, ...), custom_call_target="tpu_custom_call" | custom-call | tf_op jit(solution)/shard_map/place_step/pallas_call | solution.py:184
  (88 shorter events, 17.0 us)
Async XLA Ops:
  0.6 8.9 %copy-start = (bf16[128,6144]{1,0:T(8,128)(2,1)S(1)}, bf16[128,6144]{1,0:T(8,128)(2,1)}, u32[]{:S(2)}) copy-start(bf16[128,6144]{1,0:T(8,128)(2,1)} %param.8) | copy-start | bytes 4718596
  1.6 9.3 %copy-start.4 = (bf16[128,6144]{1,0:T(8,128)(2,1)S(1)}, bf16[128,6144]{1,0:T(8,128)(2,1)}, u32[]{:S(2)}) copy-start(bf16[128,6144]{1,0:T(8,128)(2,1)} %param.7) | copy-start | bytes 4718596
  3.0 10.7 %collective-permute-start.1 = (bf16[40,1536]{1,0:T(8,128)(2,1)S(1)}, bf16[40,1536]{1,0:T(8,128)(2,1)S(1)}, u32[]{:S(2)}, u32[]{:S(2)}) collective-permute-start(bf16[40,1536]{1,0:T(8,128)(2,1)S(1)} %convolution_convert_fusion.1), channel_id=1, source_target_pairs={{0,16},{8,24},{16,0},{24,8},{1,17},{9,25},{17,1},{25,9},{2,18},{10... | collective-permute-start | bytes 368648 | tf_op jit(solution)/shard_map/ppermute | solution.py:21
  7.1 13.5 %collective-permute-start = (bf16[40,1536]{1,0:T(8,128)(2,1)S(1)}, bf16[40,1536]{1,0:T(8,128)(2,1)S(1)}, u32[]{:S(2)}, u32[]{:S(2)}) collective-permute-start(bf16[40,1536]{1,0:T(8,128)(2,1)S(1)} %convolution_convert_fusion.1), channel_id=1, source_target_pairs={{0,8},{8,0},{16,24},{24,16},{1,9},{9,1},{17,25},{25,17},{2,10},{10... | collective-permute-start | bytes 368648 | tf_op jit(solution)/shard_map/ppermute | solution.py:21
  9.9 9.8 %collective-permute-start.3 = (bf16[40,1536]{1,0:T(8,128)(2,1)S(1)}, bf16[40,1536]{1,0:T(8,128)(2,1)S(1)}, u32[]{:S(2)}, u32[]{:S(2)}) collective-permute-start(bf16[40,1536]{1,0:T(8,128)(2,1)S(1)} %fusion.1), channel_id=1, source_target_pairs={{0,16},{8,24},{16,0},{24,8},{1,17},{9,25},{17,1},{25,9},{2,18},{10... | collective-permute-start | bytes 368648 | tf_op jit(solution)/shard_map/ppermute | solution.py:21
  10.3 14.2 %collective-permute-start.6 = (bf16[40,1536]{1,0:T(8,128)(2,1)S(1)}, bf16[40,1536]{1,0:T(8,128)(2,1)S(1)}, u32[]{:S(2)}, u32[]{:S(2)}) collective-permute-start(bf16[40,1536]{1,0:T(8,128)(2,1)S(1)} %fusion.1), channel_id=1, source_target_pairs={{0,8},{8,0},{16,24},{24,16},{1,9},{9,1},{17,25},{25,17},{2,10},{10... | collective-permute-start | bytes 368648 | tf_op jit(solution)/shard_map/ppermute | solution.py:21
  13.7 7.6 %collective-permute-start.2 = (bf16[40,1536]{1,0:T(8,128)(2,1)S(1)}, bf16[40,1536]{1,0:T(8,128)(2,1)S(1)}, u32[]{:S(2)}, u32[]{:S(2)}) collective-permute-start(bf16[40,1536]{1,0:T(8,128)(2,1)S(1)} %collective-permute-done.1), channel_id=1, source_target_pairs={{0,8},{8,0},{16,24},{24,16},{1,9},{9,1},{17,25},{25,17},{2,10},{10... | collective-permute-start | bytes 368648 | tf_op jit(solution)/shard_map/ppermute | solution.py:21
  19.6 4.9 %collective-permute-start.7 = (bf16[40,1536]{1,0:T(8,128)(2,1)S(1)}, bf16[40,1536]{1,0:T(8,128)(2,1)S(1)}, u32[]{:S(2)}, u32[]{:S(2)}) collective-permute-start(bf16[40,1536]{1,0:T(8,128)(2,1)S(1)} %collective-permute-done.3), channel_id=1, source_target_pairs={{0,8},{8,0},{16,24},{24,16},{1,9},{9,1},{17,25},{25,17},{2,10},{10... | collective-permute-start | bytes 368648 | tf_op jit(solution)/shard_map/ppermute | solution.py:21
  21.4 18.2 %collective-permute-start.4 = (bf16[120,1536]{1,0:T(8,128)(2,1)S(1)}, bf16[120,1536]{1,0:T(8,128)(2,1)S(1)}, u32[]{:S(2)}, u32[]{:S(2)}) collective-permute-start(bf16[120,1536]{1,0:T(8,128)(2,1)S(1)} %constant_dynamic-update-slice_fusion), channel_id=1, source_target_pairs={{0,1},{1,0},{2,3},{3,2},{4,5},{5,4},{6,7},{7,6},{8,9},{9,8},{10,11... | collective-permute-start | bytes 1105928 | tf_op jit(solution)/shard_map/ppermute | solution.py:21
  23.0 16.6 %collective-permute-start.5 = (bf16[120,1536]{1,0:T(8,128)(2,1)S(1)}, bf16[120,1536]{1,0:T(8,128)(2,1)S(1)}, u32[]{:S(2)}, u32[]{:S(2)}) collective-permute-start(bf16[120,1536]{1,0:T(8,128)(2,1)S(1)} %constant_dynamic-update-slice_fusion), channel_id=1, source_target_pairs={{0,2},{1,3},{2,0},{3,1},{4,6},{5,7},{6,4},{7,5},{8,10},{9,11},{10,... | collective-permute-start | bytes 1105928 | tf_op jit(solution)/shard_map/ppermute | solution.py:21
  24.6 17.5 %collective-permute-start.10 = (bf16[120,1536]{1,0:T(8,128)(2,1)S(1)}, bf16[120,1536]{1,0:T(8,128)(2,1)S(1)}, u32[]{:S(2)}, u32[]{:S(2)}) collective-permute-start(bf16[120,1536]{1,0:T(8,128)(2,1)S(1)} %constant_dynamic-update-slice_fusion.3), channel_id=1, source_target_pairs={{0,1},{1,0},{2,3},{3,2},{4,5},{5,4},{6,7},{7,6},{8,9},{9,8},{10,11... | collective-permute-start | bytes 1105928 | tf_op jit(solution)/shard_map/ppermute | solution.py:21
  26.2 16.0 %collective-permute-start.11 = (bf16[120,1536]{1,0:T(8,128)(2,1)S(1)}, bf16[120,1536]{1,0:T(8,128)(2,1)S(1)}, u32[]{:S(2)}, u32[]{:S(2)}) collective-permute-start(bf16[120,1536]{1,0:T(8,128)(2,1)S(1)} %constant_dynamic-update-slice_fusion.3), channel_id=1, source_target_pairs={{0,2},{1,3},{2,0},{3,1},{4,6},{5,7},{6,4},{7,5},{8,10},{9,11},{10,... | collective-permute-start | bytes 1105928 | tf_op jit(solution)/shard_map/ppermute | solution.py:21
  42.2 6.6 %collective-permute-start.8 = (bf16[64,1536]{1,0:T(8,128)(2,1)S(1)}, bf16[64,1536]{1,0:T(8,128)(2,1)S(1)}, u32[]{:S(2)}, u32[]{:S(2)}) collective-permute-start(bf16[64,1536]{1,0:T(8,128)(2,1)S(1)} %slice.15), channel_id=1, source_target_pairs={{0,2},{1,3},{2,0},{3,1},{4,6},{5,7},{6,4},{7,5},{8,10},{9,11},{10,... | collective-permute-start | bytes 589832 | tf_op jit(solution)/shard_map/ppermute | solution.py:21
  42.8 5.8 %collective-permute-start.9 = (bf16[56,1536]{1,0:T(8,128)(2,1)S(1)}, bf16[56,1536]{1,0:T(8,128)(2,1)S(1)}, u32[]{:S(2)}, u32[]{:S(2)}) collective-permute-start(bf16[56,1536]{1,0:T(8,128)(2,1)S(1)} %slice.16), channel_id=1, source_target_pairs={{0,1},{1,0},{2,3},{3,2},{4,5},{5,4},{6,7},{7,6},{8,9},{9,8},{10,11... | collective-permute-start | bytes 516104 | tf_op jit(solution)/shard_map/ppermute | solution.py:21
  43.4 7.5 %collective-permute-start.12 = (bf16[64,1536]{1,0:T(8,128)(2,1)S(1)}, bf16[64,1536]{1,0:T(8,128)(2,1)S(1)}, u32[]{:S(2)}, u32[]{:S(2)}) collective-permute-start(bf16[64,1536]{1,0:T(8,128)(2,1)S(1)} %slice.17), channel_id=1, source_target_pairs={{0,2},{1,3},{2,0},{3,1},{4,6},{5,7},{6,4},{7,5},{8,10},{9,11},{10,... | collective-permute-start | bytes 589832 | tf_op jit(solution)/shard_map/ppermute | solution.py:21
  45.0 5.9 %collective-permute-start.13 = (bf16[56,1536]{1,0:T(8,128)(2,1)S(1)}, bf16[56,1536]{1,0:T(8,128)(2,1)S(1)}, u32[]{:S(2)}, u32[]{:S(2)}) collective-permute-start(bf16[56,1536]{1,0:T(8,128)(2,1)S(1)} %slice.18), channel_id=1, source_target_pairs={{0,1},{1,0},{2,3},{3,2},{4,5},{5,4},{6,7},{7,6},{8,9},{9,8},{10,11... | collective-permute-start | bytes 516104 | tf_op jit(solution)/shard_map/ppermute | solution.py:21
  54.1 22.5 %collective-permute-start.14 = (bf16[160,1664]{1,0:T(8,128)(2,1)S(1)}, bf16[160,1664]{1,0:T(8,128)(2,1)}, u32[]{:S(2)}, u32[]{:S(2)}) collective-permute-start(bf16[160,1664]{1,0:T(8,128)(2,1)S(1)} %row_piece.4), channel_id=1, source_target_pairs={{0,3},{1,2},{2,1},{3,0},{4,7},{5,6},{6,5},{7,4},{8,11},{9,10},{10,... | collective-permute-start | bytes 1597448 | tf_op jit(solution)/shard_map/ppermute | solution.py:21
  59.3 18.6 %collective-permute-start.16 = (bf16[160,1664]{1,0:T(8,128)(2,1)S(1)}, bf16[160,1664]{1,0:T(8,128)(2,1)S(1)}, u32[]{:S(2)}, u32[]{:S(2)}) collective-permute-start(bf16[160,1664]{1,0:T(8,128)(2,1)S(1)} %row_piece.6), channel_id=1, source_target_pairs={{0,1},{1,0},{2,3},{3,2},{4,5},{5,4},{6,7},{7,6},{8,9},{9,8},{10,11... | collective-permute-start | bytes 1597448 | tf_op jit(solution)/shard_map/ppermute | solution.py:21
  60.4 17.5 %collective-permute-start.15 = (bf16[160,1664]{1,0:T(8,128)(2,1)S(1)}, bf16[160,1664]{1,0:T(8,128)(2,1)S(1)}, u32[]{:S(2)}, u32[]{:S(2)}) collective-permute-start(bf16[160,1664]{1,0:T(8,128)(2,1)S(1)} %row_piece.5), channel_id=1, source_target_pairs={{0,2},{1,3},{2,0},{3,1},{4,6},{5,7},{6,4},{7,5},{8,10},{9,11},{10,... | collective-permute-start | bytes 1597448 | tf_op jit(solution)/shard_map/ppermute | solution.py:21
  78.1 12.4 %collective-permute-start.17 = (bf16[40,1664]{1,0:T(8,128)(2,1)S(1)}, bf16[40,1664]{1,0:T(8,128)(2,1)S(1)}, u32[]{:S(2)}, u32[]{:S(2)}) collective-permute-start(bf16[40,1664]{1,0:T(8,128)(2,1)S(1)} %get-tuple-element.135), channel_id=1, source_target_pairs={{0,8},{8,0},{16,24},{24,16},{1,9},{9,1},{17,25},{25,17},{2,10},{10... | collective-permute-start | bytes 399368 | tf_op jit(solution)/shard_map/ppermute | solution.py:21
  79.3 12.4 %collective-permute-start.18 = (bf16[40,1664]{1,0:T(8,128)(2,1)S(1)}, bf16[40,1664]{1,0:T(8,128)(2,1)S(1)}, u32[]{:S(2)}, u32[]{:S(2)}) collective-permute-start(bf16[40,1664]{1,0:T(8,128)(2,1)S(1)} %get-tuple-element.136), channel_id=1, source_target_pairs={{0,16},{8,24},{16,0},{24,8},{1,17},{9,25},{17,1},{25,9},{2,18},{10... | collective-permute-start | bytes 399368 | tf_op jit(solution)/shard_map/ppermute | solution.py:21
  82.3 10.8 %copy-start.2 = (s32[128,2]{0,1:T(2,128)S(1)}, s32[128,2]{0,1:T(2,128)}, u32[]{:S(2)}) copy-start(s32[128,2]{0,1:T(2,128)} %param.9) | copy-start | bytes 3076
  82.3 10.8 %copy-start.3 = (f32[128,2]{0,1:T(2,128)S(1)}, f32[128,2]{0,1:T(2,128)}, u32[]{:S(2)}) copy-start(f32[128,2]{0,1:T(2,128)} %param.10) | copy-start | bytes 3076
  82.3 9.3 %collective-permute-start.19 = (bf16[40,1664]{1,0:T(8,128)(2,1)S(1)}, bf16[40,1664]{1,0:T(8,128)(2,1)S(1)}, u32[]{:S(2)}, u32[]{:S(2)}) collective-permute-start(bf16[40,1664]{1,0:T(8,128)(2,1)S(1)} %get-tuple-element.137), channel_id=1, source_target_pairs={{0,24},{8,16},{16,8},{24,0},{1,25},{9,17},{17,9},{25,1},{2,26},{10... | collective-permute-start | bytes 399368 | tf_op jit(solution)/shard_map/ppermute | solution.py:21
  83.5 10.9 %copy-start.1 = (bf16[128,6144]{1,0:T(8,128)(2,1)S(1)}, bf16[128,6144]{1,0:T(8,128)(2,1)}, u32[]{:S(2)}) copy-start(bf16[128,6144]{1,0:T(8,128)(2,1)} %param.8) | copy-start | bytes 4718596
  91.7 1.4 %collective-permute-start.20 = (bf16[40,1664]{1,0:T(8,128)(2,1)S(1)}, bf16[40,1664]{1,0:T(8,128)(2,1)S(1)}, u32[]{:S(2)}, u32[]{:S(2)}) collective-permute-start(bf16[40,1664]{1,0:T(8,128)(2,1)S(1)} %add_convert_fusion.half_ref), channel_id=1, source_target_pairs={{0,4},{4,0},{1,5},{5,1},{2,6},{6,2},{3,7},{7,3},{8,12},{12,8},{9,1... | collective-permute-start | bytes 399368 | tf_op jit(solution)/shard_map/ppermute | solution.py:21

commit v7 on v6

--- a/solution.py
+++ b/solution.py
@@ -265,9 +265,9 @@
 def outer(left, *rights):
     height, width = left.shape[1], rights[0].shape[1]
     count = len(rights)
-    block = block_of(height, max(LANES, 256 * 1024 // width // LANES * LANES))
+    block = block_of(height, max(LANES, 512 * 1024 // width // LANES * LANES))
     vmem = pl.BlockSpec(memory_space=pltpu.VMEM)
-    slots = min(8, count * height // block)
+    slots = min(6, count * height // block)
     return pl.pallas_call(
         outer_kernel,
         in_specs=[vmem] * (1 + count),

time: 94.6 us -> 94.6 us (level)
  waiting for transfers between devices: 6.38 us -> 9.14 us
  Pallas kernels: 51.6 us -> 49 us
    ppermute x21, waiting for transfers between devices: 6.38 us -> 9.14 us  [swap(): return lax.ppermute(x, axis, [(i, i ^ bits) for i in range(size)])]
    pallas_call x3, Pallas kernels: 19 us -> 16.4 us  [outer(): pl.pallas_call(outer_kernel, in_specs=[vmem] * (1 + count), out_specs=[pl...]
  transfers between devices with their start and end apart: 21 -> 21, of which waited for: 7 -> 8; matrix products, arithmetic and copies ran while one was open for 5% -> 5% of each run, Pallas kernels for 50% -> 47%
where the time goes in v7:
time: 94.6 us; the launch traced here: 94.4 us
  Pallas kernels  49 us (52%)
  starting transfers between devices  27.7 us (29%)
  waiting for transfers between devices  9.14 us (10%)
  other arithmetic  3.86 us (4%)
  matrix products  2.63 us (3%)
  between operations  1.19 us (1%)
    ppermute x21, starting transfers between devices, swap(): return lax.ppermute(x, axis, [(i, i ^ bits) for i in range(size)])  27.7 us
    pallas_call x3, Pallas kernels, outer(): pl.pallas_call(outer_kernel, in_specs=[vmem] * (1 + count), out_specs=[pl...  16.4 us
    pallas_call x10, Pallas kernels, whole_call(): pl.pallas_call(kernel, in_specs=[pl.BlockSpec(memory_space=pltpu.SMEM)] *...  10.5 us
    pallas_call x2, Pallas kernels, fetch(): pl.pallas_call(fetch_kernel, in_specs=[pl.BlockSpec(memory_space=pltpu.HB...  9.41 us
    ppermute x21, waiting for transfers between devices, swap(): return lax.ppermute(x, axis, [(i, i ^ bits) for i in range(size)])  9.14 us
    pallas_call x4, Pallas kernels, row_piece(): pl.pallas_call(piece_kernel, in_specs=[pl.BlockSpec(memory_space=pltpu.SM...  7.85 us
    pallas_call x1, Pallas kernels, fetch_columns(): pl.pallas_call(columns_kernel, in_specs=[pl.BlockSpec(memory_space=pltpu....  4.88 us
    dot_general x4, matrix products, slots_of(): return lax.dot_general(select_own, x, FIRST, preferred_element_type=f32)  2.63 us
  transfers between devices with their start and end apart: 21, of which 8 were waited for; matrix products, arithmetic and copies ran while one was open for 5% of the time, Pallas kernels for 47%

profile of v7, /device:TPU:0, one launch (start us, length us, event | category | flops | bytes accessed | tf_op | source)
XLA Modules:
  0.0 94.4 jit_solution(6011397727843230099)
XLA Ops:
  1.6 1.4 %convolution_convert_fusion.1 = bf16[40,1536]{1,0:T(8,128)(2,1)S(1)} fusion(bf16[128,6144]{1,0:T(8,128)(2,1)} %param.7, s32[]{:T(128)S(6)} %select_n.21, s32[128]{0:T(128)S(1)} %select_reduce_fusion.2, pred[128]{0:T(512)(128)(4,1)S(1)} %broadcast_compare_fusion.1), kind=kOutput, calls=%fused_computation.5 | convolution fusion | flops 15800320 | bytes 516740 | tf_op jit(solution)/shard_map/dot_general | solution.py:307
  3.0 4.1 %collective-permute-start.1 = (bf16[40,1536]{1,0:T(8,128)(2,1)S(1)}, bf16[40,1536]{1,0:T(8,128)(2,1)S(1)}, u32[]{:S(2)}, u32[]{:S(2)}) collective-permute-start(bf16[40,1536]{1,0:T(8,128)(2,1)S(1)} %convolution_convert_fusion.1), channel_id=1, source_target_pairs={{0,16},{8,24},{16,0},{24,8},{1,17},{9,25},{17,1},{25,9},{2,18},{10... | collective-permute-start | bytes 368648 | tf_op jit(solution)/shard_map/ppermute | solution.py:21
  7.1 1.6 %collective-permute-start = (bf16[40,1536]{1,0:T(8,128)(2,1)S(1)}, bf16[40,1536]{1,0:T(8,128)(2,1)S(1)}, u32[]{:S(2)}, u32[]{:S(2)}) collective-permute-start(bf16[40,1536]{1,0:T(8,128)(2,1)S(1)} %convolution_convert_fusion.1), channel_id=1, source_target_pairs={{0,8},{8,0},{16,24},{24,16},{1,9},{9,1},{17,25},{25,17},{2,10},{10... | collective-permute-start | bytes 368648 | tf_op jit(solution)/shard_map/ppermute | solution.py:21
  11.5 2.2 %collective-permute-done.1 = bf16[40,1536]{1,0:T(8,128)(2,1)S(1)} collective-permute-done((bf16[40,1536]{1,0:T(8,128)(2,1)S(1)}, bf16[40,1536]{1,0:T(8,128)(2,1)S(1)}, u32[]{:S(2)}, u32[]{:S(2)}) %collective-permute-start.1) | collective-permute-done | bytes 122912 | tf_op jit(solution)/shard_map/ppermute | solution.py:21
  14.9 4.7 %fetch.2.gate_ref = bf16[6144,1024]{1,0:T(8,128)(2,1)S(1)} custom-call(bf16[6144,1024]{1,0:T(8,128)(2,1)} %bitcast.18), custom_call_target="tpu_custom_call" | custom-call | tf_op jit(solution)/shard_map/fetch/pallas_call | solution.py:91
  21.4 1.6 %collective-permute-start.4 = (bf16[120,1536]{1,0:T(8,128)(2,1)S(1)}, bf16[120,1536]{1,0:T(8,128)(2,1)S(1)}, u32[]{:S(2)}, u32[]{:S(2)}) collective-permute-start(bf16[120,1536]{1,0:T(8,128)(2,1)S(1)} %constant_dynamic-update-slice_fusion), channel_id=1, source_target_pairs={{0,1},{1,0},{2,3},{3,2},{4,5},{5,4},{6,7},{7,6},{8,9},{9,8},{10,11... | collective-permute-start | bytes 1105928 | tf_op jit(solution)/shard_map/ppermute | solution.py:21
  23.0 1.5 %collective-permute-start.5 = (bf16[120,1536]{1,0:T(8,128)(2,1)S(1)}, bf16[120,1536]{1,0:T(8,128)(2,1)S(1)}, u32[]{:S(2)}, u32[]{:S(2)}) collective-permute-start(bf16[120,1536]{1,0:T(8,128)(2,1)S(1)} %constant_dynamic-update-slice_fusion), channel_id=1, source_target_pairs={{0,2},{1,3},{2,0},{3,1},{4,6},{5,7},{6,4},{7,5},{8,10},{9,11},{10,... | collective-permute-start | bytes 1105928 | tf_op jit(solution)/shard_map/ppermute | solution.py:21
  24.6 1.6 %collective-permute-start.10 = (bf16[120,1536]{1,0:T(8,128)(2,1)S(1)}, bf16[120,1536]{1,0:T(8,128)(2,1)S(1)}, u32[]{:S(2)}, u32[]{:S(2)}) collective-permute-start(bf16[120,1536]{1,0:T(8,128)(2,1)S(1)} %constant_dynamic-update-slice_fusion.3), channel_id=1, source_target_pairs={{0,1},{1,0},{2,3},{3,2},{4,5},{5,4},{6,7},{7,6},{8,9},{9,8},{10,11... | collective-permute-start | bytes 1105928 | tf_op jit(solution)/shard_map/ppermute | solution.py:21
  26.2 1.5 %collective-permute-start.11 = (bf16[120,1536]{1,0:T(8,128)(2,1)S(1)}, bf16[120,1536]{1,0:T(8,128)(2,1)S(1)}, u32[]{:S(2)}, u32[]{:S(2)}) collective-permute-start(bf16[120,1536]{1,0:T(8,128)(2,1)S(1)} %constant_dynamic-update-slice_fusion.3), channel_id=1, source_target_pairs={{0,2},{1,3},{2,0},{3,1},{4,6},{5,7},{6,4},{7,5},{8,10},{9,11},{10,... | collective-permute-start | bytes 1105928 | tf_op jit(solution)/shard_map/ppermute | solution.py:21
  27.7 4.7 %fetch.3.up_ref = bf16[6144,1024]{1,0:T(8,128)(2,1)S(1)} custom-call(bf16[6144,1024]{1,0:T(8,128)(2,1)} %bitcast.19), custom_call_target="tpu_custom_call" | custom-call | tf_op jit(solution)/shard_map/fetch/pallas_call | solution.py:91
  32.4 4.9 %fetch_columns.1 = (bf16[1024,1536]{1,0:T(8,128)(2,1)S(1)}, bf16[1024,1536]{1,0:T(8,128)(2,1)S(1)}, bf16[1024,1536]{1,0:T(8,128)(2,1)S(1)}, bf16[1024,1536]{1,0:T(8,128)(2,1)S(1)}) custom-call(s32[1]{0:T(128)} %bitcast.index_ref.piece_ref, bf16[1024,6144]{1,0:T(8,128)(2,1)} %bitcast.20), custom_call_target="tpu_custom_call" | custom-call | tf_op jit(solution)/shard_map/fetch_columns/pallas_call | solution.py:124
  38.4 1.2 %pair_step.4 = (f32[160,1024]{1,0:T(8,128)S(1)}, f32[160,1024]{1,0:T(8,128)S(1)}) custom-call(s32[1]{0:T(128)} %bitcast.index_ref.piece_ref, bf16[160,1536]{1,0:T(8,128)(2,1)S(1)} %pad_maximum_fusion.2.rows_ref, bf16[6144,1024]{1,0:T(8,128)(2,1)S(1)} %fetch.2.gate_ref, bf16[6144,1024]{1,0:T(8,128)(2,1)S(1)} %fetch.3.up_ref), custom_call_target="tpu_custom_call" | custom-call | tf_op jit(solution)/shard_map/pair_step/pallas_call | solution.py:184
  39.7 1.2 %pair_step.5 = (f32[160,1024]{1,0:T(8,128)S(1)}, f32[160,1024]{1,0:T(8,128)S(1)}) custom-call(s32[1]{0:T(128)} %bitcast.4.index_ref.piece_ref, bf16[160,1536]{1,0:T(8,128)(2,1)S(1)} %pad_maximum_fusion.4.rows_ref, bf16[6144,1024]{1,0:T(8,128)(2,1)S(1)} %fetch.2.gate_ref, bf16[6144,1024]{1,0:T(8,128)(2,1)S(1)} %fetch.3.up_ref, ...), custom_call_target="tpu_custom_call" | custom-call | tf_op jit(solution)/shard_map/pair_step/pallas_call | solution.py:184
  41.0 1.2 %pair_step.6 = (f32[160,1024]{1,0:T(8,128)S(1)}, f32[160,1024]{1,0:T(8,128)S(1)}) custom-call(s32[1]{0:T(128)} %bitcast.3.index_ref.piece_ref, bf16[160,1536]{1,0:T(8,128)(2,1)S(1)} %pad_maximum_fusion.3.rows_ref, bf16[6144,1024]{1,0:T(8,128)(2,1)S(1)} %fetch.2.gate_ref, bf16[6144,1024]{1,0:T(8,128)(2,1)S(1)} %fetch.3.up_ref, ...), custom_call_target="tpu_custom_call" | custom-call | tf_op jit(solution)/shard_map/pair_step/pallas_call | solution.py:184
  43.4 1.6 %collective-permute-start.12 = (bf16[64,1536]{1,0:T(8,128)(2,1)S(1)}, bf16[64,1536]{1,0:T(8,128)(2,1)S(1)}, u32[]{:S(2)}, u32[]{:S(2)}) collective-permute-start(bf16[64,1536]{1,0:T(8,128)(2,1)S(1)} %slice.17), channel_id=1, source_target_pairs={{0,2},{1,3},{2,0},{3,1},{4,6},{5,7},{6,4},{7,5},{8,10},{9,11},{10,... | collective-permute-start | bytes 589832 | tf_op jit(solution)/shard_map/ppermute | solution.py:21
  45.0 1.6 %collective-permute-start.13 = (bf16[56,1536]{1,0:T(8,128)(2,1)S(1)}, bf16[56,1536]{1,0:T(8,128)(2,1)S(1)}, u32[]{:S(2)}, u32[]{:S(2)}) collective-permute-start(bf16[56,1536]{1,0:T(8,128)(2,1)S(1)} %slice.18), channel_id=1, source_target_pairs={{0,1},{1,0},{2,3},{3,2},{4,5},{5,4},{6,7},{7,6},{8,9},{9,8},{10,11... | collective-permute-start | bytes 516104 | tf_op jit(solution)/shard_map/ppermute | solution.py:21
  48.8 1.2 %pair_step.7 = (f32[160,1024]{1,0:T(8,128)S(1)}, f32[160,1024]{1,0:T(8,128)S(1)}) custom-call(s32[1]{0:T(128)} %bitcast.6.index_ref.piece_ref, bf16[160,1536]{1,0:T(8,128)(2,1)S(1)} %pad_maximum_fusion.8.rows_ref, bf16[6144,1024]{1,0:T(8,128)(2,1)S(1)} %fetch.2.gate_ref, bf16[6144,1024]{1,0:T(8,128)(2,1)S(1)} %fetch.3.up_ref, ...), custom_call_target="tpu_custom_call" | custom-call | tf_op jit(solution)/shard_map/pair_step/pallas_call | solution.py:184
  50.9 1.3 %back_step.7 = (bf16[160,1024]{1,0:T(8,128)(2,1)S(1)}, bf16[160,1024]{1,0:T(8,128)(2,1)S(1)}, bf16[160,1024]{1,0:T(8,128)(2,1)S(1)}, f32[160,128]{1,0:T(8,128)S(1)}) custom-call(bf16[160,1536]{1,0:T(8,128)(2,1)S(1)} %pad_maximum_fusion.9.grads_ref, bf16[1024,1536]{1,0:T(8,128)(2,1)S(1)} %get-tuple-element.105.down_ref, f32[1024,160]{1,0:T(8,128)S(1)} %back_step.6.refs_0_, ...), custom_call_target="tpu_custom_call" | custom-call | tf_op jit(solution)/shard_map/back_step/pallas_call | solution.py:184
  52.2 1.9 %row_piece.4 = bf16[160,1664]{1,0:T(8,128)(2,1)S(1)} custom-call(s32[1]{0:T(128)} %bitcast.6.index_ref.piece_ref, bf16[160,1024]{1,0:T(8,128)(2,1)S(1)} %get-tuple-element.123.d_gate_ref.refs_0_, bf16[160,1024]{1,0:T(8,128)(2,1)S(1)} %get-tuple-element.124.d_up_ref.refs_0_, f32[160,128]{1,0:T(8,128)S(1)} %get-tuple-element.117.slot_ref, ...), custom_call_target="tpu_custom_call" | custom-call | flops 1006632960 | bytes 6946816 | tf_op jit(solution)/shard_map/row_piece/pallas_call | solution.py:226
  54.1 1.2 %collective-permute-start.14 = (bf16[160,1664]{1,0:T(8,128)(2,1)S(1)}, bf16[160,1664]{1,0:T(8,128)(2,1)}, u32[]{:S(2)}, u32[]{:S(2)}) collective-permute-start(bf16[160,1664]{1,0:T(8,128)(2,1)S(1)} %row_piece.4), channel_id=1, source_target_pairs={{0,3},{1,2},{2,1},{3,0},{4,7},{5,6},{6,5},{7,4},{8,11},{9,10},{10,... | collective-permute-start | bytes 1597448 | tf_op jit(solution)/shard_map/ppermute | solution.py:21
  55.3 2.1 %row_piece.5 = bf16[160,1664]{1,0:T(8,128)(2,1)S(1)} custom-call(s32[1]{0:T(128)} %bitcast.3.index_ref.piece_ref, bf16[160,1024]{1,0:T(8,128)(2,1)S(1)} %get-tuple-element.123.d_gate_ref.refs_0_, bf16[160,1024]{1,0:T(8,128)(2,1)S(1)} %get-tuple-element.124.d_up_ref.refs_0_, f32[160,128]{1,0:T(8,128)S(1)} %get-tuple-element.117.slot_ref, ...), custom_call_target="tpu_custom_call" | custom-call | flops 1006632960 | bytes 6946816 | tf_op jit(solution)/shard_map/row_piece/pallas_call | solution.py:226
  57.4 1.9 %row_piece.6 = bf16[160,1664]{1,0:T(8,128)(2,1)S(1)} custom-call(s32[1]{0:T(128)} %bitcast.4.index_ref.piece_ref, bf16[160,1024]{1,0:T(8,128)(2,1)S(1)} %get-tuple-element.123.d_gate_ref.refs_0_, bf16[160,1024]{1,0:T(8,128)(2,1)S(1)} %get-tuple-element.124.d_up_ref.refs_0_, f32[160,128]{1,0:T(8,128)S(1)} %get-tuple-element.117.slot_ref, ...), custom_call_target="tpu_custom_call" | custom-call | flops 1006632960 | bytes 6946816 | tf_op jit(solution)/shard_map/row_piece/pallas_call | solution.py:226
  60.4 1.4 %collective-permute-start.15 = (bf16[160,1664]{1,0:T(8,128)(2,1)S(1)}, bf16[160,1664]{1,0:T(8,128)(2,1)S(1)}, u32[]{:S(2)}, u32[]{:S(2)}) collective-permute-start(bf16[160,1664]{1,0:T(8,128)(2,1)S(1)} %row_piece.5), channel_id=1, source_target_pairs={{0,2},{1,3},{2,0},{3,1},{4,6},{5,7},{6,4},{7,5},{8,10},{9,11},{10,... | collective-permute-start | bytes 1597448 | tf_op jit(solution)/shard_map/ppermute | solution.py:21
  61.7 2.0 %row_piece.7 = f32[160,1664]{1,0:T(8,128)S(1)} custom-call(s32[1]{0:T(128)} %bitcast.index_ref.piece_ref, bf16[160,1024]{1,0:T(8,128)(2,1)S(1)} %get-tuple-element.123.d_gate_ref.refs_0_, bf16[160,1024]{1,0:T(8,128)(2,1)S(1)} %get-tuple-element.124.d_up_ref.refs_0_, f32[160,128]{1,0:T(8,128)S(1)} %get-tuple-element.117.slot_ref, ...), custom_call_target="tpu_custom_call" | custom-call | flops 1006632960 | bytes 6946816 | tf_op jit(solution)/shard_map/row_piece/pallas_call | solution.py:226
  64.7 5.2 %outer.5 = bf16[1024,6144]{1,0:T(8,128)(2,1)} custom-call(bf16[160,1024]{1,0:T(8,128)(2,1)S(1)} %get-tuple-element.125.left_ref, bf16[160,6144]{1,0:T(8,128)(2,1)S(1)} %get-tuple-element.154.refs_0_), custom_call_target="tpu_custom_call" | custom-call | flops 4026531840 | bytes 12582912 | tf_op jit(solution)/shard_map/outer/pallas_call | solution.py:271
  69.9 5.5 %outer.3 = bf16[6144,1024]{1,0:T(8,128)(2,1)} custom-call(bf16[160,6144]{1,0:T(8,128)(2,1)S(1)} %get-tuple-element.153.left_ref, bf16[160,1024]{1,0:T(8,128)(2,1)S(1)} %get-tuple-element.123.d_gate_ref.refs_0_), custom_call_target="tpu_custom_call" | custom-call | flops 4026531840 | bytes 12582912 | tf_op jit(solution)/shard_map/outer/pallas_call | solution.py:271
  77.4 1.2 %collective-permute-start.17 = (bf16[40,1664]{1,0:T(8,128)(2,1)S(1)}, bf16[40,1664]{1,0:T(8,128)(2,1)S(1)}, u32[]{:S(2)}, u32[]{:S(2)}) collective-permute-start(bf16[40,1664]{1,0:T(8,128)(2,1)S(1)} %get-tuple-element.135), channel_id=1, source_target_pairs={{0,8},{8,0},{16,24},{24,16},{1,9},{9,1},{17,25},{25,17},{2,10},{10... | collective-permute-start | bytes 399368 | tf_op jit(solution)/shard_map/ppermute | solution.py:21
  78.6 3.1 %collective-permute-start.18 = (bf16[40,1664]{1,0:T(8,128)(2,1)S(1)}, bf16[40,1664]{1,0:T(8,128)(2,1)S(1)}, u32[]{:S(2)}, u32[]{:S(2)}) collective-permute-start(bf16[40,1664]{1,0:T(8,128)(2,1)S(1)} %get-tuple-element.136), channel_id=1, source_target_pairs={{0,16},{8,24},{16,0},{24,8},{1,17},{9,25},{17,1},{25,9},{2,18},{10... | collective-permute-start | bytes 399368 | tf_op jit(solution)/shard_map/ppermute | solution.py:21
  82.6 5.7 %outer.4 = bf16[6144,1024]{1,0:T(8,128)(2,1)} custom-call(bf16[160,6144]{1,0:T(8,128)(2,1)S(1)} %get-tuple-element.153.left_ref, bf16[160,1024]{1,0:T(8,128)(2,1)S(1)} %get-tuple-element.124.d_up_ref.refs_0_), custom_call_target="tpu_custom_call" | custom-call | flops 4026531840 | bytes 12582912 | tf_op jit(solution)/shard_map/outer/pallas_call | solution.py:271
  88.3 3.3 %collective-permute-done.18 = bf16[40,1664]{1,0:T(8,128)(2,1)S(1)} collective-permute-done((bf16[40,1664]{1,0:T(8,128)(2,1)S(1)}, bf16[40,1664]{1,0:T(8,128)(2,1)S(1)}, u32[]{:S(2)}, u32[]{:S(2)}) %collective-permute-start.18) | collective-permute-done | bytes 133152 | tf_op jit(solution)/shard_map/ppermute | solution.py:21
  92.0 1.2 %collective-permute-done.20.other_half_ref = bf16[40,1664]{1,0:T(8,128)(2,1)S(1)} collective-permute-done((bf16[40,1664]{1,0:T(8,128)(2,1)S(1)}, bf16[40,1664]{1,0:T(8,128)(2,1)S(1)}, u32[]{:S(2)}, u32[]{:S(2)}) %collective-permute-start.20) | collective-permute-done | bytes 133152 | tf_op jit(solution)/shard_map/ppermute | solution.py:21
  93.2 1.2 %place_step.1 = (f32[128,1536]{1,0:T(8,128)}, f32[2,128]{1,0:T(2,128)}) custom-call(s32[1]{0:T(128)} %bitcast.10.expert_ref, s32[2,128]{1,0:T(2,128)S(1)} %bitcast.16, f32[2,128]{1,0:T(2,128)S(1)} %bitcast.17, bf16[128,40]{1,0:T(8,128)(2,1)S(1)} %get-tuple-element.155.own_ref, bf16[128,40]{1,0:T(8,128)(2,1)S(1)} %get-tuple-element.156.other_ref, ...), custom_call_target="tpu_custom_call" | custom-call | tf_op jit(solution)/shard_map/place_step/pallas_call | solution.py:184
  (88 shorter events, 17.4 us)
Async XLA Ops:
  0.6 8.9 %copy-start = (bf16[128,6144]{1,0:T(8,128)(2,1)S(1)}, bf16[128,6144]{1,0:T(8,128)(2,1)}, u32[]{:S(2)}) copy-start(bf16[128,6144]{1,0:T(8,128)(2,1)} %param.8) | copy-start | bytes 4718596
  1.6 9.3 %copy-start.4 = (bf16[128,6144]{1,0:T(8,128)(2,1)S(1)}, bf16[128,6144]{1,0:T(8,128)(2,1)}, u32[]{:S(2)}) copy-start(bf16[128,6144]{1,0:T(8,128)(2,1)} %param.7) | copy-start | bytes 4718596
  3.0 10.7 %collective-permute-start.1 = (bf16[40,1536]{1,0:T(8,128)(2,1)S(1)}, bf16[40,1536]{1,0:T(8,128)(2,1)S(1)}, u32[]{:S(2)}, u32[]{:S(2)}) collective-permute-start(bf16[40,1536]{1,0:T(8,128)(2,1)S(1)} %convolution_convert_fusion.1), channel_id=1, source_target_pairs={{0,16},{8,24},{16,0},{24,8},{1,17},{9,25},{17,1},{25,9},{2,18},{10... | collective-permute-start | bytes 368648 | tf_op jit(solution)/shard_map/ppermute | solution.py:21
  7.1 13.5 %collective-permute-start = (bf16[40,1536]{1,0:T(8,128)(2,1)S(1)}, bf16[40,1536]{1,0:T(8,128)(2,1)S(1)}, u32[]{:S(2)}, u32[]{:S(2)}) collective-permute-start(bf16[40,1536]{1,0:T(8,128)(2,1)S(1)} %convolution_convert_fusion.1), channel_id=1, source_target_pairs={{0,8},{8,0},{16,24},{24,16},{1,9},{9,1},{17,25},{25,17},{2,10},{10... | collective-permute-start | bytes 368648 | tf_op jit(solution)/shard_map/ppermute | solution.py:21
  9.9 9.8 %collective-permute-start.3 = (bf16[40,1536]{1,0:T(8,128)(2,1)S(1)}, bf16[40,1536]{1,0:T(8,128)(2,1)S(1)}, u32[]{:S(2)}, u32[]{:S(2)}) collective-permute-start(bf16[40,1536]{1,0:T(8,128)(2,1)S(1)} %fusion.1), channel_id=1, source_target_pairs={{0,16},{8,24},{16,0},{24,8},{1,17},{9,25},{17,1},{25,9},{2,18},{10... | collective-permute-start | bytes 368648 | tf_op jit(solution)/shard_map/ppermute | solution.py:21
  10.3 14.2 %collective-permute-start.6 = (bf16[40,1536]{1,0:T(8,128)(2,1)S(1)}, bf16[40,1536]{1,0:T(8,128)(2,1)S(1)}, u32[]{:S(2)}, u32[]{:S(2)}) collective-permute-start(bf16[40,1536]{1,0:T(8,128)(2,1)S(1)} %fusion.1), channel_id=1, source_target_pairs={{0,8},{8,0},{16,24},{24,16},{1,9},{9,1},{17,25},{25,17},{2,10},{10... | collective-permute-start | bytes 368648 | tf_op jit(solution)/shard_map/ppermute | solution.py:21
  13.7 7.6 %collective-permute-start.2 = (bf16[40,1536]{1,0:T(8,128)(2,1)S(1)}, bf16[40,1536]{1,0:T(8,128)(2,1)S(1)}, u32[]{:S(2)}, u32[]{:S(2)}) collective-permute-start(bf16[40,1536]{1,0:T(8,128)(2,1)S(1)} %collective-permute-done.1), channel_id=1, source_target_pairs={{0,8},{8,0},{16,24},{24,16},{1,9},{9,1},{17,25},{25,17},{2,10},{10... | collective-permute-start | bytes 368648 | tf_op jit(solution)/shard_map/ppermute | solution.py:21
  19.6 4.9 %collective-permute-start.7 = (bf16[40,1536]{1,0:T(8,128)(2,1)S(1)}, bf16[40,1536]{1,0:T(8,128)(2,1)S(1)}, u32[]{:S(2)}, u32[]{:S(2)}) collective-permute-start(bf16[40,1536]{1,0:T(8,128)(2,1)S(1)} %collective-permute-done.3), channel_id=1, source_target_pairs={{0,8},{8,0},{16,24},{24,16},{1,9},{9,1},{17,25},{25,17},{2,10},{10... | collective-permute-start | bytes 368648 | tf_op jit(solution)/shard_map/ppermute | solution.py:21
  21.4 18.2 %collective-permute-start.4 = (bf16[120,1536]{1,0:T(8,128)(2,1)S(1)}, bf16[120,1536]{1,0:T(8,128)(2,1)S(1)}, u32[]{:S(2)}, u32[]{:S(2)}) collective-permute-start(bf16[120,1536]{1,0:T(8,128)(2,1)S(1)} %constant_dynamic-update-slice_fusion), channel_id=1, source_target_pairs={{0,1},{1,0},{2,3},{3,2},{4,5},{5,4},{6,7},{7,6},{8,9},{9,8},{10,11... | collective-permute-start | bytes 1105928 | tf_op jit(solution)/shard_map/ppermute | solution.py:21
  23.0 16.6 %collective-permute-start.5 = (bf16[120,1536]{1,0:T(8,128)(2,1)S(1)}, bf16[120,1536]{1,0:T(8,128)(2,1)S(1)}, u32[]{:S(2)}, u32[]{:S(2)}) collective-permute-start(bf16[120,1536]{1,0:T(8,128)(2,1)S(1)} %constant_dynamic-update-slice_fusion), channel_id=1, source_target_pairs={{0,2},{1,3},{2,0},{3,1},{4,6},{5,7},{6,4},{7,5},{8,10},{9,11},{10,... | collective-permute-start | bytes 1105928 | tf_op jit(solution)/shard_map/ppermute | solution.py:21
  24.6 17.5 %collective-permute-start.10 = (bf16[120,1536]{1,0:T(8,128)(2,1)S(1)}, bf16[120,1536]{1,0:T(8,128)(2,1)S(1)}, u32[]{:S(2)}, u32[]{:S(2)}) collective-permute-start(bf16[120,1536]{1,0:T(8,128)(2,1)S(1)} %constant_dynamic-update-slice_fusion.3), channel_id=1, source_target_pairs={{0,1},{1,0},{2,3},{3,2},{4,5},{5,4},{6,7},{7,6},{8,9},{9,8},{10,11... | collective-permute-start | bytes 1105928 | tf_op jit(solution)/shard_map/ppermute | solution.py:21
  26.2 16.0 %collective-permute-start.11 = (bf16[120,1536]{1,0:T(8,128)(2,1)S(1)}, bf16[120,1536]{1,0:T(8,128)(2,1)S(1)}, u32[]{:S(2)}, u32[]{:S(2)}) collective-permute-start(bf16[120,1536]{1,0:T(8,128)(2,1)S(1)} %constant_dynamic-update-slice_fusion.3), channel_id=1, source_target_pairs={{0,2},{1,3},{2,0},{3,1},{4,6},{5,7},{6,4},{7,5},{8,10},{9,11},{10,... | collective-permute-start | bytes 1105928 | tf_op jit(solution)/shard_map/ppermute | solution.py:21
  42.2 6.6 %collective-permute-start.8 = (bf16[64,1536]{1,0:T(8,128)(2,1)S(1)}, bf16[64,1536]{1,0:T(8,128)(2,1)S(1)}, u32[]{:S(2)}, u32[]{:S(2)}) collective-permute-start(bf16[64,1536]{1,0:T(8,128)(2,1)S(1)} %slice.15), channel_id=1, source_target_pairs={{0,2},{1,3},{2,0},{3,1},{4,6},{5,7},{6,4},{7,5},{8,10},{9,11},{10,... | collective-permute-start | bytes 589832 | tf_op jit(solution)/shard_map/ppermute | solution.py:21
  42.8 5.8 %collective-permute-start.9 = (bf16[56,1536]{1,0:T(8,128)(2,1)S(1)}, bf16[56,1536]{1,0:T(8,128)(2,1)S(1)}, u32[]{:S(2)}, u32[]{:S(2)}) collective-permute-start(bf16[56,1536]{1,0:T(8,128)(2,1)S(1)} %slice.16), channel_id=1, source_target_pairs={{0,1},{1,0},{2,3},{3,2},{4,5},{5,4},{6,7},{7,6},{8,9},{9,8},{10,11... | collective-permute-start | bytes 516104 | tf_op jit(solution)/shard_map/ppermute | solution.py:21
  43.4 7.5 %collective-permute-start.12 = (bf16[64,1536]{1,0:T(8,128)(2,1)S(1)}, bf16[64,1536]{1,0:T(8,128)(2,1)S(1)}, u32[]{:S(2)}, u32[]{:S(2)}) collective-permute-start(bf16[64,1536]{1,0:T(8,128)(2,1)S(1)} %slice.17), channel_id=1, source_target_pairs={{0,2},{1,3},{2,0},{3,1},{4,6},{5,7},{6,4},{7,5},{8,10},{9,11},{10,... | collective-permute-start | bytes 589832 | tf_op jit(solution)/shard_map/ppermute | solution.py:21
  45.0 5.9 %collective-permute-start.13 = (bf16[56,1536]{1,0:T(8,128)(2,1)S(1)}, bf16[56,1536]{1,0:T(8,128)(2,1)S(1)}, u32[]{:S(2)}, u32[]{:S(2)}) collective-permute-start(bf16[56,1536]{1,0:T(8,128)(2,1)S(1)} %slice.18), channel_id=1, source_target_pairs={{0,1},{1,0},{2,3},{3,2},{4,5},{5,4},{6,7},{7,6},{8,9},{9,8},{10,11... | collective-permute-start | bytes 516104 | tf_op jit(solution)/shard_map/ppermute | solution.py:21
  54.1 21.2 %collective-permute-start.14 = (bf16[160,1664]{1,0:T(8,128)(2,1)S(1)}, bf16[160,1664]{1,0:T(8,128)(2,1)}, u32[]{:S(2)}, u32[]{:S(2)}) collective-permute-start(bf16[160,1664]{1,0:T(8,128)(2,1)S(1)} %row_piece.4), channel_id=1, source_target_pairs={{0,3},{1,2},{2,1},{3,0},{4,7},{5,6},{6,5},{7,4},{8,11},{9,10},{10,... | collective-permute-start | bytes 1597448 | tf_op jit(solution)/shard_map/ppermute | solution.py:21
  59.3 17.3 %collective-permute-start.16 = (bf16[160,1664]{1,0:T(8,128)(2,1)S(1)}, bf16[160,1664]{1,0:T(8,128)(2,1)S(1)}, u32[]{:S(2)}, u32[]{:S(2)}) collective-permute-start(bf16[160,1664]{1,0:T(8,128)(2,1)S(1)} %row_piece.6), channel_id=1, source_target_pairs={{0,1},{1,0},{2,3},{3,2},{4,5},{5,4},{6,7},{7,6},{8,9},{9,8},{10,11... | collective-permute-start | bytes 1597448 | tf_op jit(solution)/shard_map/ppermute | solution.py:21
  60.4 16.8 %collective-permute-start.15 = (bf16[160,1664]{1,0:T(8,128)(2,1)S(1)}, bf16[160,1664]{1,0:T(8,128)(2,1)S(1)}, u32[]{:S(2)}, u32[]{:S(2)}) collective-permute-start(bf16[160,1664]{1,0:T(8,128)(2,1)S(1)} %row_piece.5), channel_id=1, source_target_pairs={{0,2},{1,3},{2,0},{3,1},{4,6},{5,7},{6,4},{7,5},{8,10},{9,11},{10,... | collective-permute-start | bytes 1597448 | tf_op jit(solution)/shard_map/ppermute | solution.py:21
  77.4 11.0 %collective-permute-start.17 = (bf16[40,1664]{1,0:T(8,128)(2,1)S(1)}, bf16[40,1664]{1,0:T(8,128)(2,1)S(1)}, u32[]{:S(2)}, u32[]{:S(2)}) collective-permute-start(bf16[40,1664]{1,0:T(8,128)(2,1)S(1)} %get-tuple-element.135), channel_id=1, source_target_pairs={{0,8},{8,0},{16,24},{24,16},{1,9},{9,1},{17,25},{25,17},{2,10},{10... | collective-permute-start | bytes 399368 | tf_op jit(solution)/shard_map/ppermute | solution.py:21
  78.6 13.1 %collective-permute-start.18 = (bf16[40,1664]{1,0:T(8,128)(2,1)S(1)}, bf16[40,1664]{1,0:T(8,128)(2,1)S(1)}, u32[]{:S(2)}, u32[]{:S(2)}) collective-permute-start(bf16[40,1664]{1,0:T(8,128)(2,1)S(1)} %get-tuple-element.136), channel_id=1, source_target_pairs={{0,16},{8,24},{16,0},{24,8},{1,17},{9,25},{17,1},{25,9},{2,18},{10... | collective-permute-start | bytes 399368 | tf_op jit(solution)/shard_map/ppermute | solution.py:21
  81.7 11.5 %copy-start.2 = (s32[128,2]{0,1:T(2,128)S(1)}, s32[128,2]{0,1:T(2,128)}, u32[]{:S(2)}) copy-start(s32[128,2]{0,1:T(2,128)} %param.9) | copy-start | bytes 3076
  81.7 11.5 %copy-start.3 = (f32[128,2]{0,1:T(2,128)S(1)}, f32[128,2]{0,1:T(2,128)}, u32[]{:S(2)}) copy-start(f32[128,2]{0,1:T(2,128)} %param.10) | copy-start | bytes 3076
  81.7 10.0 %collective-permute-start.19 = (bf16[40,1664]{1,0:T(8,128)(2,1)S(1)}, bf16[40,1664]{1,0:T(8,128)(2,1)S(1)}, u32[]{:S(2)}, u32[]{:S(2)}) collective-permute-start(bf16[40,1664]{1,0:T(8,128)(2,1)S(1)} %get-tuple-element.137), channel_id=1, source_target_pairs={{0,24},{8,16},{16,8},{24,0},{1,25},{9,17},{17,9},{25,1},{2,26},{10... | collective-permute-start | bytes 399368 | tf_op jit(solution)/shard_map/ppermute | solution.py:21
  82.6 11.8 %copy-start.1 = (bf16[128,6144]{1,0:T(8,128)(2,1)S(1)}, bf16[128,6144]{1,0:T(8,128)(2,1)}, u32[]{:S(2)}) copy-start(bf16[128,6144]{1,0:T(8,128)(2,1)} %param.8) | copy-start | bytes 4718596
  91.7 1.4 %collective-permute-start.20 = (bf16[40,1664]{1,0:T(8,128)(2,1)S(1)}, bf16[40,1664]{1,0:T(8,128)(2,1)S(1)}, u32[]{:S(2)}, u32[]{:S(2)}) collective-permute-start(bf16[40,1664]{1,0:T(8,128)(2,1)S(1)} %add_convert_fusion.half_ref), channel_id=1, source_target_pairs={{0,4},{4,0},{1,5},{5,1},{2,6},{6,2},{3,7},{7,3},{8,12},{12,8},{9,1... | collective-permute-start | bytes 399368 | tf_op jit(solution)/shard_map/ppermute | solution.py:21
